TPU v7x, 32 devices: a whole 2x2x4 slice. The times are simulated.
32 devices in a mesh: mode: 16 (over z, x, core), rank: 2 (over y).
Axes of the slice: x: 2, y: 2, z: 4, core: 2. Of those that a mesh axis runs over, the one named last changes fastest.
Arguments:
- core_right: float32 [1024, 256, 1024], P('rank', 'mode'), may hold values from -0.1875 to 0.1875
- sketch_right: float32 [256, 256, 256], P('rank', 'mode'), may hold values from -0.0234375 to 0.0234375
- core_left: float32 [1024, 256, 1024], P('rank', 'mode'), may hold values from -0.1875 to 0.1875
- sketch_left: float32 [256, 256, 256], P('rank', 'mode'), may hold values from -0.0234375 to 0.0234375
- carry_in: float32 [1024, 256], P('rank'), may hold values from -6 to 6
Outputs:
- carry_out: float32 [1024, 256], P('rank')
All inputs are finite; a program needn't handle non-finite values.
Results may differ from a plain program's by a relative error of at most 0.00013.
Values sent between devices are 32-bit elements; how exact they have to be, the bound alone decides.
No kernel may reach another device: no remote copies, remote signals or barrier semaphores. Data moves between devices by JAX's collectives and lax.ppermute only.
A program may use at most 128 MiB of HBM per device.

v0:
```python
import jax
import jax.numpy as jnp
from jax import lax
from jax.sharding import PartitionSpec as P


def chain_step(core, carried, sketch):
    hidden = jnp.einsum("aib,bc->aic", core, carried, precision=lax.Precision.HIGHEST)
    return jnp.einsum("aic,sic->as", hidden, sketch, precision=lax.Precision.HIGHEST)


def shards(core_right, sketch_right, core_left, sketch_left, carry_in):
    sketch_whole_right, sketch_whole_left, carried = (
        lax.all_gather(sketch_right, "rank", axis=0, tiled=True),
        lax.all_gather(sketch_left, "rank", axis=0, tiled=True),
        lax.all_gather(carry_in, "rank", axis=0, tiled=True),
    )
    sketches = (sketch_whole_right, sketch_whole_left)
    cores = (core_right, core_left)
    result = carry_in
    for step in range(2):
        partial_sum = chain_step(cores[step], carried, sketches[step])
        summed = lax.psum(partial_sum, "mode")
        if step == 0:
            carried = lax.all_gather(summed, "rank", axis=0, tiled=True)
        else:
            result = summed
    return result


def solution(mesh):
    in_specs = (
        P("rank", "mode", None),
        P("rank", "mode", None),
        P("rank", "mode", None),
        P("rank", "mode", None),
        P("rank", None),
    )
    out_specs = P("rank", None)
    return jax.shard_map(shards, mesh=mesh, in_specs=in_specs, out_specs=out_specs, check_vma=False)
```

profile of v0, /device:TPU:0, one launch (start us, length us, event | category | flops | bytes accessed | tf_op | source)
XLA Modules:
  0.0 387.6 jit_solution(3806773497062349039)
XLA Ops:
  6.5 0.0 all-gather.5.cloned.1.call-start
  6.5 0.7 all-gather.5.cloned.1.call-update
  7.3 0.0 all-gather.7.cloned.1.call-start
  7.3 0.7 all-gather.7.cloned.1.call-update
  8.0 0.0 all-reduce.3.cloned.1.call-start
  8.1 24.9 %all-gather.5.cloned.1.call-done = f32[1024,256]{1,0:T(8,128)} async-done(((f32[512,256]{1,0:T(8,128)}), f32[1024,256]{1,0:T(8,128)}) %all-gather.5.cloned.1.call-update) | async-done | bytes 1048592 | tf_op jit(solution)/shard_map/all_gather | solution.py:16
  32.9 31.0 %fusion.16 = f32[512,16,256]{2,1,0:T(8,128)} fusion(f32[512,16,1024]{2,1,0:T(8,128)} %param.5, f32[1024,256]{1,0:T(8,128)} %all-gather.5.cloned.1.call-done), kind=kOutput, calls=%fused_computation.10 | convolution fusion | flops 25769803776 | bytes 42991616 | tf_op jit(solution)/shard_map/aib,bc->aic/dot_general | solution.py:8
  63.9 0.0 copy-start
  63.9 27.3 %all-gather.7.cloned.1.call-done = f32[256,16,256]{2,1,0:T(8,128)} async-done(((f32[128,16,256]{2,1,0:T(8,128)}), f32[256,16,256]{2,1,0:T(8,128)}) %all-gather.7.cloned.1.call-update) | async-done | bytes 4194320 | tf_op jit(solution)/shard_map/all_gather | solution.py:14
  91.3 15.1 %fusion.7 = f32[512,256]{1,0:T(8,128)} fusion(f32[256,16,256]{2,1,0:T(8,128)} %all-gather.7.cloned.1.call-done, f32[512,16,256]{2,1,0:T(8,128)} %fusion.16), kind=kOutput, calls=%fused_computation.7 | convolution fusion | flops 6442450944 | bytes 13107200 | tf_op jit(solution)/shard_map/aic,sic->as/dot_general | solution.py:9
  106.4 0.0 all-reduce.3.cloned.1.call-update
  106.4 0.0 all-gather.9.cloned.1.call-start
  106.5 90.2 %all-reduce.3.cloned.1.call-done = f32[512,256]{1,0:T(8,128)} async-done(((f32[512,256]{1,0:T(8,128)}), f32[512,256]{1,0:T(8,128)}) %all-reduce.3.cloned.1.call-update) | async-done | bytes 524304 | tf_op jit(solution)/shard_map/psum | solution.py:23
  196.6 0.0 all-gather.9.cloned.1.call-update
  196.7 0.0 all-gather.11.cloned.1.call-start
  196.7 0.0 copy-done
  196.7 2.5 copy.7
  199.3 0.0 all-gather.11.cloned.1.call-update
  199.3 0.2 all-reduce.5.cloned.1.call-start
  199.5 20.4 %all-gather.9.cloned.1.call-done = f32[1024,256]{1,0:T(8,128)} async-done(((f32[512,256]{1,0:T(8,128)}), f32[1024,256]{1,0:T(8,128)}) %all-gather.9.cloned.1.call-update) | async-done | bytes 1048592 | tf_op jit(solution)/shard_map/all_gather | solution.py:25
  219.9 51.0 %fusion = f32[256,512,16]{0,1,2:T(8,128)} fusion(f32[512,16,1024]{2,1,0:T(8,128)} %param.7, f32[1024,256]{1,0:T(8,128)} %all-gather.9.cloned.1.call-done), kind=kOutput, calls=%fused_computation | convolution fusion | flops 25769803776 | bytes 42991616 | tf_op jit(solution)/shard_map/aib,bc->aic/dot_general | solution.py:8
  270.8 7.2 %all-gather.11.cloned.1.call-done = f32[256,16,256]{2,0,1:T(8,128)} async-done(((f32[128,16,256]{2,0,1:T(8,128)}), f32[256,16,256]{2,0,1:T(8,128)}) %all-gather.11.cloned.1.call-update) | async-done | bytes 4194320 | tf_op jit(solution)/shard_map/all_gather | solution.py:15
  278.0 10.6 %fusion.12 = f32[512,256]{1,0:T(8,128)} fusion(f32[256,16,256]{2,0,1:T(8,128)} %all-gather.11.cloned.1.call-done, f32[256,512,16]{0,1,2:T(8,128)} %fusion), kind=kOutput, calls=%fused_computation.8 | convolution fusion | flops 6442450944 | bytes 13107200 | tf_op jit(solution)/shard_map/aic,sic->as/dot_general | solution.py:9
  288.7 0.0 all-reduce.5.cloned.1.call-update
  288.7 90.2 %all-reduce.5.cloned.1.call-done = f32[512,256]{1,0:T(8,128)} async-done(((f32[512,256]{1,0:T(8,128)}), f32[512,256]{1,0:T(8,128)}) %all-reduce.5.cloned.1.call-update) | async-done | bytes 524304 | tf_op jit(solution)/shard_map/psum | solution.py:23
  378.8 1.9 copy.23
Async XLA Ops:
  6.5 26.4 %all-gather.5.cloned.1.call-start = ((), (), s32[]{:S(2)}) async-start(), calls=%async_computation | async-start | bytes 1572864 | tf_op jit(solution)/shard_map/all_gather | solution.py:16
  7.3 84.0 %all-gather.7.cloned.1.call-start = ((), (), s32[]{:S(2)}) async-start(), calls=%async_computation.1 | async-start | bytes 6291456 | tf_op jit(solution)/shard_map/all_gather | solution.py:14
  8.0 188.6 %all-reduce.3.cloned.1.call-start = ((), (), s32[]{:S(2)}) async-start(), calls=%async_computation.2 | async-start | bytes 1048576 | tf_op jit(solution)/shard_map/psum | solution.py:23
  63.9 132.8 %copy-start = (f32[128,16,256]{2,1,0:T(8,128)S(1)}, f32[128,16,256]{2,1,0:T(8,128)}, u32[]{:S(2)}) copy-start(f32[128,16,256]{2,1,0:T(8,128)} %param.8) | copy-start | bytes 6291460
  106.4 113.5 %all-gather.9.cloned.1.call-start = ((), (), s32[]{:S(2)}) async-start(), calls=%async_computation.3 | async-start | bytes 1572864 | tf_op jit(solution)/shard_map/all_gather | solution.py:25
  196.7 81.4 %all-gather.11.cloned.1.call-start = ((), (), s32[]{:S(2)}) async-start(), calls=%async_computation.4 | async-start | bytes 6291456 | tf_op jit(solution)/shard_map/all_gather | solution.py:15
  199.3 179.6 %all-reduce.5.cloned.1.call-start = ((), (), s32[]{:S(2)}) async-start(), calls=%async_computation.5 | async-start | bytes 1048576 | tf_op jit(solution)/shard_map/psum | solution.py:23
Sparse Core Ops, SparseCore 0:
  8.9 23.9 all-gather.4
  34.5 56.7 all-gather.6
  106.5 90.0 all-reduce.2
  198.0 21.7 all-gather.8
  221.3 56.7 all-gather.10
  288.8 89.9 all-reduce.4
where the time goes:
time: 388 us
  waiting for transfers between devices  262 us (68%)
  matrix products  108 us (28%)
  between operations  13.5 us (3%)
  local copies, waits for them, and re-layouts  4.42 us (1%)
    psum x2, waiting for transfers between devices, shards(): summed = lax.psum(partial_sum, 'mode')  180 us
    dot_general x2, matrix products, chain_step(): jnp.einsum('aib,bc->aic', core, carried, precision=lax.Precision.HIGHEST)  81.9 us
    all_gather x1, waiting for transfers between devices, shards(): lax.all_gather(sketch_right, 'rank', axis=0, tiled=True)  27.3 us
    dot_general x2, matrix products, chain_step(): jnp.einsum('aic,sic->as', hidden, sketch, precision=lax.Precision.HIGHEST)  25.7 us
    all_gather x1, waiting for transfers between devices, shards(): lax.all_gather(carry_in, 'rank', axis=0, tiled=True)  24.9 us
    all_gather x1, waiting for transfers between devices, shards(): carried = lax.all_gather(summed, 'rank', axis=0, tiled=True)  20.4 us
  transfers between devices with their start and end apart: 6, of which 6 were waited for; matrix products, arithmetic and copies ran while one was open for 22% of the time, Pallas kernels for 0%

commit v1 on v0

v1 whole, which is shorter than its diff:
```python
import functools

import jax
import jax.numpy as jnp
from jax import lax
from jax.experimental import pallas as pl
from jax.experimental.pallas import tpu as pltpu
from jax.sharding import PartitionSpec as P

F32, BF16 = jnp.float32, jnp.bfloat16
LANES = 128
HBM = pl.BlockSpec(memory_space=pl.ANY)
VMEM = pl.BlockSpec(memory_space=pltpu.VMEM)


def halves(x):
    high = x.astype(BF16)
    return high, (x - high.astype(F32)).astype(BF16)


def dot(a, b):
    return jnp.dot(a, b, preferred_element_type=F32)


def prepare_kernel(sketch_ref, out_ref):
    depth = sketch_ref.shape[2]
    for i in range(sketch_ref.shape[1]):
        high, low = halves(sketch_ref[:, i, :].T)
        out_ref[i, :depth] = high
        out_ref[i, depth:] = low


def hidden_loop(rows, slots, core_hbm, carried_ref, high, low, buf, sems, weights, tile):
    count, slices, depth = core_hbm.shape
    columns = carried_ref.shape[1]
    steps = count // rows

    def copy(k):
        slot = lax.rem(k, slots)
        return pltpu.make_async_copy(core_hbm.at[pl.ds(k * rows, rows)], buf.at[slot], sems.at[slot])

    for k in range(min(slots - 1, steps)):
        copy(k).start()
    h, l = halves(carried_ref[...])
    weights[0:depth] = h
    weights[depth : 2 * depth] = l
    weights[2 * depth :] = h

    def block(k, _):
        @pl.when(k + slots - 1 < steps)
        def _():
            copy(k + slots - 1).start()

        copy(k).wait()
        h, l = halves(buf[lax.rem(k, slots)].reshape(rows * slices, depth))
        result = dot(jnp.concatenate([h, h, l], axis=1), weights[...])
        for j in range(columns // LANES):
            tile[j] = result[:, j * LANES : (j + 1) * LANES]
        at = pl.ds(pl.multiple_of(k * rows, rows), rows)
        for i in range(slices):
            for j in range(columns // LANES):
                h, l = halves(tile[j, pl.ds(i, rows, stride=slices), :])
                high[i, at, j * LANES : (j + 1) * LANES] = h
                low[i, at, j * LANES : (j + 1) * LANES] = l
        return 0

    lax.fori_loop(0, steps, block, 0)


def multiply(group, first, high, low, sketches, out):
    slices = sketches[0].shape[0]
    depth = high.shape[2]
    group = min(group, slices)

    def body(g, _):
        xs, ys = [], [[] for _ in sketches]
        for t in range(group):
            i = g * group + t
            h = high[first + i]
            xs += [h, h, low[first + i]]
            for y, s in zip(ys, sketches):
                y += [s[i, :depth], s[i, depth:], s[i, :depth]]
        y = jnp.concatenate([jnp.concatenate(y, axis=0) for y in ys], axis=1)
        out[...] += dot(jnp.concatenate(xs, axis=1), y)
        return 0

    lax.fori_loop(0, slices // group, body, 0)


def product_kernel(group, firsts, high, low, *refs):
    base, chunks, out, prepared = refs[0], refs[1:-2], refs[-2], refs[-1]
    out[...] = jnp.zeros_like(out) if base is None else base[...]
    for first, chunk in zip(firsts, chunks):
        if prepared is not None:
            prepare_kernel(chunk, prepared)
            chunk = prepared
        multiply(group, first, high, low, [chunk], out)


def joined_kernel(group, cuts, high, low, *refs):
    out = refs[-1]
    out[...] = jnp.zeros_like(out)
    at = 0
    for first, width in cuts:
        multiply(group, first, high, low, refs[at : at + width], out)
        at += width


def hidden_shape(core, columns):
    return (core.shape[1], core.shape[0], columns)


def loop_scratch(core, columns, rows, slots):
    _, slices, depth = core.shape
    return [
        pltpu.VMEM((slots, rows, slices, depth), F32),
        pltpu.SemaphoreType.DMA((slots,)),
        pltpu.VMEM((3 * depth, columns), BF16),
        pltpu.VMEM((columns // LANES, rows * slices, LANES), F32),
    ]


def limit(mib):
    return pltpu.CompilerParams(vmem_limit_bytes=mib << 20)


ROWS, SLOTS, GROUP = 64, 3, 4


def hidden(core, carried):
    columns = carried.shape[1]
    out = jax.ShapeDtypeStruct(hidden_shape(core, columns), BF16)
    return pl.pallas_call(
        functools.partial(hidden_loop, ROWS, SLOTS),
        out_shape=(out, out),
        in_specs=[HBM, VMEM],
        out_specs=(VMEM, VMEM),
        scratch_shapes=loop_scratch(core, columns, ROWS, SLOTS),
        compiler_params=limit(32),
    )(core, carried)


def product(high, low, sketch, first=0, base=None):
    size, slices, depth = sketch.shape

    def kernel(high, low, *refs):
        product_kernel(GROUP, (first,), high, low, *(() if base is not None else (None,)), *refs)

    return pl.pallas_call(
        kernel,
        out_shape=jax.ShapeDtypeStruct((high.shape[1], size), F32),
        in_specs=[VMEM] * (3 + (base is not None)),
        out_specs=VMEM,
        scratch_shapes=[pltpu.VMEM((slices, 2 * depth, size), BF16)],
        compiler_params=limit(24),
    )(high, low, *(() if base is None else (base,)), sketch)


def joined(high, low, cuts, chunks):
    size = sum(s.shape[2] for s in chunks[: cuts[0][1]])
    return pl.pallas_call(
        functools.partial(joined_kernel, GROUP, cuts),
        out_shape=jax.ShapeDtypeStruct((high.shape[1], size), F32),
        in_specs=[VMEM] * (2 + len(chunks)),
        out_specs=VMEM,
        compiler_params=limit(24),
    )(high, low, *chunks)


def prepare(sketch):
    size, slices, depth = sketch.shape
    return pl.pallas_call(
        prepare_kernel,
        out_shape=jax.ShapeDtypeStruct((slices, 2 * depth, size), BF16),
        in_specs=[VMEM],
        out_specs=VMEM,
        compiler_params=limit(16),
    )(sketch)


def digit_groups(count):
    bits = count.bit_length() - 1
    groups, low = [], 0
    while low < bits:
        width = 1 if low < 2 else min(2, bits - low)
        groups.append((low, width))
        low += width
    return groups


def piece_of(index, groups):
    piece = 0
    for low, width in groups:
        piece = (piece << width) | ((index >> low) & ((1 << width) - 1))
    return piece


def partner(x, count, low, distance):
    return lax.ppermute(x, "mode", [(i, i ^ (distance << low)) for i in range(count)])


def shift(x, ranks, d):
    return lax.ppermute(x, "rank", [(i, (i + d) % ranks) for i in range(ranks)])


def reduce_scatter(x, count, groups):
    for low, width in groups:
        size = x.shape[0] >> width
        arrived = [partner(x[d * size : (d + 1) * size], count, low, d) for d in range(1, 1 << width)]
        x = sum(arrived, x[:size])
    return x


def all_gather(x, count, groups):
    for low, width in reversed(groups):
        x = jnp.concatenate([x] + [partner(x, count, low, d) for d in range(1, 1 << width)], axis=0)
    return x


def in_order(x, own):
    return jnp.take(x, own ^ jnp.arange(x.shape[0]), axis=0)


def by_rank(blocks, rank, axis):
    joined = jnp.concatenate(blocks[::-1], axis=axis)
    return jnp.roll(joined, (rank + 1) * blocks[0].shape[axis], axis=axis)


def quad_part(x, modes, mode):
    groups = digit_groups(modes)[:2]
    size = x.shape[0] >> len(groups)
    return lax.dynamic_slice_in_dim(x, piece_of(mode, groups) * size, size)


def all_rows(x, parts, modes, rank, mode):
    groups = digit_groups(modes)[:2]
    own = piece_of(mode, groups)
    blocks = [in_order(all_gather(part[None], modes, groups), own).reshape(x.shape) for part in parts]
    return by_rank([x] + blocks, rank, 0)


def shards(modes, ranks, core_right, sketch_right, core_left, sketch_left, carry_in):
    mode, rank = lax.axis_index("mode"), lax.axis_index("rank")
    groups = digit_groups(modes)
    own = piece_of(mode, groups)
    middle_slice = core_right.shape[1] // 2

    def pieces(x):
        return in_order(x.reshape((modes, x.shape[0] // modes) + x.shape[1:]), own)

    def cut(sketch):
        return sketch[:, :middle_slice], sketch[:, middle_slice:]

    def shifted(x):
        return [shift(x, ranks, d) for d in range(1, ranks)]

    (right_a, right_b), (left_a, left_b) = cut(sketch_right), cut(sketch_left)
    part = quad_part(carry_in, modes, mode)
    parts = shifted(part)
    parts, right_a, right_b = lax.optimization_barrier((parts, right_a, right_b))
    arrived_a, arrived_b = shifted(right_a), shifted(right_b)
    carried = all_rows(carry_in, parts, modes, rank, mode)
    high, low = hidden(core_right, carried)
    term = [product(high, low, sketch_right)]
    bases = [product(high, low, s) for s in arrived_a]
    arrived_b, left_a = lax.optimization_barrier((arrived_b, left_a))
    left_a_arrived = shifted(left_a)
    term += [product(high, low, s, middle_slice, base) for s, base in zip(arrived_b, bases)]
    middle = reduce_scatter(pieces(by_rank(term, rank, 1)), modes, groups)
    middle, left_a_arrived = lax.optimization_barrier((middle, left_a_arrived))
    middles, left_b = lax.optimization_barrier((shifted(middle), left_b))
    left_b_arrived = shifted(left_b)
    both = by_rank([middle] + middles, rank, 0)
    both = in_order(all_gather(both[None], modes, groups), own)
    carried = jnp.swapaxes(both, 0, 1).reshape(carried.shape)

    high, low = hidden(core_left, carried)
    own_a, own_b = cut(sketch_left)
    first, second = [own_a] + left_a_arrived, [own_b] + left_b_arrived
    if sketch_left.shape[0] % LANES:
        first, second = [jnp.concatenate(first)], [jnp.concatenate(second)]
    chunks = [prepare(s) for s in first + second]
    term = joined(high, low, ((0, len(first)), (middle_slice, len(second))), chunks)
    term = by_rank(jnp.split(term, ranks, axis=1), rank, 1)
    result = all_gather(reduce_scatter(pieces(term), modes, groups), modes, groups)
    return in_order(result, own).reshape(carry_in.shape)


def solution(mesh):
    modes, ranks = mesh.shape["mode"], mesh.shape["rank"]
    in_specs = (P("rank", "mode", None),) * 4 + (P("rank", None),)
    body = functools.partial(shards, modes, ranks)
    return jax.shard_map(body, mesh=mesh, in_specs=in_specs, out_specs=P("rank", None), check_vma=False)
```

time: 388 us -> 178 us (0.46)
  waiting for transfers between devices: 262 us -> 64.5 us
  matrix products: 108 us -> 0 us
  Pallas kernels: 0 us -> 57.2 us
  starting transfers between devices: 0.38 us -> 29.1 us
  local copies, waits for them, and re-layouts: 4.42 us -> 17.6 us
  between operations: 13.5 us -> 0.43 us
  other arithmetic: 0 us -> 8.38 us
    psum x2 -> x0, waiting for transfers between devices: 180 us -> none  [shards(): summed = lax.psum(partial_sum, 'mode')]
    dot_general x4 -> x0, matrix products: 108 us -> none  [the longest x2 81.9 us: chain_step(): jnp.einsum('aib,bc->aic', core, carried, precision=lax.Precision.HIGHEST)]
    all_gather x4 -> x0, waiting for transfers between devices: 79.8 us -> none  [the longest x1 27.3 us: shards(): lax.all_gather(sketch_right, 'rank', axis=0, tiled=True)]
    ppermute x0 -> x28, waiting for transfers between devices: none -> 64.5 us  [the longest x22 43.5 us: partner(): lax.ppermute(x, 'mode', [(i, i ^ distance << low) for i in range(count)])]
    pallas_call x0 -> x10, Pallas kernels: none -> 57.2 us  [the longest x2 39.1 us: hidden(): pl.pallas_call(functools.partial(hidden_loop, ROWS, SLOTS), out_shape=(ou...]
    ppermute x0 -> x28, starting transfers between devices: none -> 29.1 us  [the longest x22 22.5 us: partner(): lax.ppermute(x, 'mode', [(i, i ^ distance << low) for i in range(count)])]
    gather x0 -> x5, local copies, waits for them, and re-layouts: none -> 6.98 us  [in_order(): return jnp.take(x, own ^ jnp.arange(x.shape[0]), axis=0)]
    concatenate x0 -> x7, other arithmetic: none -> 4.55 us  [the longest x4 2.53 us: all_gather(): jnp.concatenate([x] + [partner(x, count, low, d) for d in range(1, 1 << w...]
  transfers between devices with their start and end apart: 6 -> 28, of which waited for: 6 -> 20; matrix products, arithmetic and copies ran while one was open for 22% -> 12% of each run, Pallas kernels for 0% -> 26%
where the time goes in v1:
time: 178 us; the launch traced here: 177 us
  waiting for transfers between devices  64.5 us (36%)
  Pallas kernels  57.2 us (32%)
  starting transfers between devices  29.1 us (16%)
  local copies, waits for them, and re-layouts  17.6 us (10%)
  other arithmetic  8.38 us (5%)
    ppermute x22, waiting for transfers between devices, partner(): lax.ppermute(x, 'mode', [(i, i ^ distance << low) for i in range(count)])  43.5 us
    pallas_call x2, Pallas kernels, hidden(): pl.pallas_call(functools.partial(hidden_loop, ROWS, SLOTS), out_shape=(ou...  39.1 us
    ppermute x22, starting transfers between devices, partner(): lax.ppermute(x, 'mode', [(i, i ^ distance << low) for i in range(count)])  22.5 us
    ppermute x6, waiting for transfers between devices, shift(): return lax.ppermute(x, 'rank', [(i, (i + d) % ranks) for i in range(ranks)])  21 us
    pallas_call x3, Pallas kernels, product(): pl.pallas_call(kernel, out_shape=jax.ShapeDtypeStruct((high.shape[1], siz...  9.91 us
    gather x5, local copies, waits for them, and re-layouts, in_order(): return jnp.take(x, own ^ jnp.arange(x.shape[0]), axis=0)  6.98 us
    ppermute x6, starting transfers between devices, shift(): return lax.ppermute(x, 'rank', [(i, (i + d) % ranks) for i in range(ranks)])  6.64 us
    pallas_call x4, Pallas kernels, prepare(): pl.pallas_call(prepare_kernel, out_shape=jax.ShapeDtypeStruct((slices, 2...  4.31 us
  transfers between devices with their start and end apart: 28, of which 20 were waited for; matrix products, arithmetic and copies ran while one was open for 12% of the time, Pallas kernels for 26%

profile of v1, /device:TPU:0, one launch (start us, length us, event | category | flops | bytes accessed | tf_op | source)
XLA Modules:
  0.0 177.3 jit_solution(13667581076333476592)
XLA Ops:
  0.0 0.9 constant_dynamic-slice_fusion
  0.9 3.0 %collective-permute-start = (f32[128,256]{1,0:T(8,128)S(1)}, f32[128,256]{1,0:T(8,128)S(1)}, u32[]{:S(2)}, u32[]{:S(2)}) collective-permute-start(f32[128,256]{1,0:T(8,128)S(1)} %constant_dynamic-slice_fusion), channel_id=1, source_target_pairs={{0,1},{1,0},{2,3},{3,2},{4,5},{5,4},{6,7},{7,6},{8,9},{9,8},{10,11... | collective-permute-start | bytes 393224 | tf_op jit(solution)/shard_map/ppermute | solution.py:203
  4.0 3.1 %fusion.22 = (f32[128,8,256]{2,1,0:T(8,128)}, f32[128,8,256]{2,1,0:T(8,128)}) fusion(f32[128,16,256]{2,1,0:T(8,128)} %refs_0_.1), kind=kLoop, calls=%fused_computation.89 | loop fusion | bytes 4194304 | tf_op jit(solution)/shard_map/slice | solution.py:252
  7.1 1.1 fusion.21
  8.3 1.6 collective-permute-start.1
  10.7 1.2 collective-permute-start.4
  11.9 1.4 collective-permute-done.1
  14.1 1.8 collective-permute-done.2
  15.9 1.8 %pad_maximum_fusion = f32[4,128,256]{2,1,0:T(8,128)} fusion(f32[2,128,256]{2,1,0:T(8,128)} %collective-permute-done.2, f32[1,128,256]{2,1,0:T(8,128)S(1)} %collective-permute-done.1, f32[1,128,256]{2,1,0:T(8,128)S(1)} %bitcast.23), kind=kLoop, calls=%fused_computation.27 | loop fusion | flops 262144 | bytes 1048576 | tf_op jit(solution)/shard_map/concatenate | solution.py:216
  17.7 2.4 %gather_fusion = f32[4,128,256]{2,1,0:T(8,128)} fusion(f32[4,128,256]{2,1,0:T(8,128)} %pad_maximum_fusion, s32[1024]{0:T(1024)S(1)} %pad_clamp_fusion.2), kind=kCustom, calls=%fused_computation.3 | custom fusion | bytes 1048592 | tf_op jit(solution)/shard_map/jit(_take)/gather | solution.py:221
  20.1 1.2 bitcast_select_fusion
  21.3 1.7 fusion.2.carried_ref
  23.0 19.6 %shard_map.55 = (bf16[16,512,256]{2,1,0:T(8,128)(2,1)S(1)}, bf16[16,512,256]{2,1,0:T(8,128)(2,1)S(1)}) custom-call(f32[512,16,1024]{2,1,0:T(8,128)} %core_hbm.2, f32[1024,256]{1,0:T(8,128)S(1)} %fusion.2.carried_ref), custom_call_target="tpu_custom_call" | custom-call | tf_op jit(solution)/shard_map/pallas_call | solution.py:133
  42.6 5.0 %shard_map.58 = f32[512,128]{1,0:T(8,128)S(1)} custom-call(bf16[16,512,256]{2,1,0:T(8,128)(2,1)S(1)} %get-tuple-element.21.high, bf16[16,512,256]{2,1,0:T(8,128)(2,1)S(1)} %get-tuple-element.22.low, f32[128,16,256]{2,1,0:T(8,128)S(1)} %copy-done), custom_call_target="tpu_custom_call" | custom-call | tf_op jit(solution)/shard_map/pallas_call | solution.py:149
  47.7 9.2 %collective-permute-done.4.refs_1_ = f32[128,8,256]{2,1,0:T(8,128)S(1)} collective-permute-done((f32[128,8,256]{2,1,0:T(8,128)}, f32[128,8,256]{2,1,0:T(8,128)S(1)}, u32[]{:S(2)}, u32[]{:S(2)}) %collective-permute-start.4) | collective-permute-done | bytes 1048608 | tf_op jit(solution)/shard_map/ppermute | solution.py:203
  56.8 2.4 %shard_map.56.refs_0_ = f32[512,128]{1,0:T(8,128)S(1)} custom-call(bf16[16,512,256]{2,1,0:T(8,128)(2,1)S(1)} %get-tuple-element.21.high, bf16[16,512,256]{2,1,0:T(8,128)(2,1)S(1)} %get-tuple-element.22.low, f32[128,8,256]{2,1,0:T(8,128)S(1)} %collective-permute-done.3.refs_0_), custom_call_target="tpu_custom_call" | custom-call | tf_op jit(solution)/shard_map/pallas_call | solution.py:149
  59.3 2.4 %shard_map.57 = f32[512,128]{1,0:T(8,128)S(1)} custom-call(bf16[16,512,256]{2,1,0:T(8,128)(2,1)S(1)} %get-tuple-element.21.high, bf16[16,512,256]{2,1,0:T(8,128)(2,1)S(1)} %get-tuple-element.22.low, f32[512,128]{1,0:T(8,128)S(1)} %shard_map.56.refs_0_, f32[128,8,256]{2,1,0:T(8,128)S(1)} %collective-permute-done.4.refs_1_), custom_call_target="tpu_custom_call" | custom-call | tf_op jit(solution)/shard_map/pallas_call | solution.py:149
  63.3 1.0 collective-permute-done.5
  64.9 5.0 %collective-permute-done.6 = f32[4,32,256]{2,1,0:T(8,128)S(1)} collective-permute-done((f32[4,32,256]{2,1,0:T(8,128)S(1)}, f32[4,32,256]{2,1,0:T(8,128)S(1)}, u32[]{:S(2)}, u32[]{:S(2)}) %collective-permute-start.6) | collective-permute-done | bytes 131104 | tf_op jit(solution)/shard_map/ppermute | solution.py:199
  69.9 1.6 collective-permute-start.7
  71.6 2.6 %collective-permute-start.8 = (f32[1,32,256]{2,1,0:T(8,128)S(1)}, f32[1,32,256]{2,1,0:T(8,128)S(1)}, u32[]{:S(2)}, u32[]{:S(2)}) collective-permute-start(f32[1,32,256]{2,1,0:T(8,128)S(1)} %get-tuple-element.52), channel_id=1, source_target_pairs={{0,16},{2,18},{4,20},{6,22},{8,24},{10,26},{12,28},{14,30},{16,0},... | collective-permute-start | bytes 98312 | tf_op jit(solution)/shard_map/ppermute | solution.py:199
  74.4 2.2 %collective-permute-done.8 = f32[1,32,256]{2,1,0:T(8,128)S(1)} collective-permute-done((f32[1,32,256]{2,1,0:T(8,128)S(1)}, f32[1,32,256]{2,1,0:T(8,128)S(1)}, u32[]{:S(2)}, u32[]{:S(2)}) %collective-permute-start.8) | collective-permute-done | bytes 32800 | tf_op jit(solution)/shard_map/ppermute | solution.py:199
  76.7 3.2 %collective-permute-done.9 = f32[1,32,256]{2,1,0:T(8,128)S(1)} collective-permute-done((f32[1,32,256]{2,1,0:T(8,128)S(1)}, f32[1,32,256]{2,1,0:T(8,128)S(1)}, u32[]{:S(2)}, u32[]{:S(2)}) %collective-permute-start.9) | collective-permute-done | bytes 32800 | tf_op jit(solution)/shard_map/ppermute | solution.py:199
  79.9 8.4 %collective-permute-done.10.sketch_ref = f32[128,8,256]{2,1,0:T(8,128)S(1)} collective-permute-done((f32[128,8,256]{2,1,0:T(8,128)S(1)}, f32[128,8,256]{2,1,0:T(8,128)S(1)}, u32[]{:S(2)}, u32[]{:S(2)}) %collective-permute-start.10) | collective-permute-done | bytes 1048608 | tf_op jit(solution)/shard_map/ppermute | solution.py:203
  88.3 1.0 copy-done.1
  89.8 3.4 %collective-permute-done.11 = f32[1,32,256]{2,1,0:T(8,128)S(1)} collective-permute-done((f32[1,32,256]{2,1,0:T(8,128)S(1)}, f32[1,32,256]{2,1,0:T(8,128)S(1)}, u32[]{:S(2)}, u32[]{:S(2)}) %collective-permute-start.11) | collective-permute-done | bytes 32800 | tf_op jit(solution)/shard_map/ppermute | solution.py:203
  93.2 1.6 collective-permute-start.12
  94.9 2.6 %collective-permute-start.13 = (f32[1,2,32,256]{3,2,1,0:T(8,128)S(1)}, f32[1,2,32,256]{3,2,1,0:T(8,128)S(1)}, u32[]{:S(2)}, u32[]{:S(2)}) collective-permute-start(f32[1,2,32,256]{3,2,1,0:T(8,128)S(1)} %get-tuple-element.36), channel_id=1, source_target_pairs={{0,16},{2,18},{4,20},{6,22},{8,24},{10,26},{12,28},{14,30},{16,0},... | collective-permute-start | bytes 196616 | tf_op jit(solution)/shard_map/ppermute | solution.py:199
  98.8 2.6 %collective-permute-done.13 = f32[1,2,32,256]{3,2,1,0:T(8,128)S(1)} collective-permute-done((f32[1,2,32,256]{3,2,1,0:T(8,128)S(1)}, f32[1,2,32,256]{3,2,1,0:T(8,128)S(1)}, u32[]{:S(2)}, u32[]{:S(2)}) %collective-permute-start.13) | collective-permute-done | bytes 65568 | tf_op jit(solution)/shard_map/ppermute | solution.py:199
  101.4 2.1 %collective-permute-done.14 = f32[1,2,32,256]{3,2,1,0:T(8,128)S(1)} collective-permute-done((f32[1,2,32,256]{3,2,1,0:T(8,128)S(1)}, f32[1,2,32,256]{3,2,1,0:T(8,128)S(1)}, u32[]{:S(2)}, u32[]{:S(2)}) %collective-permute-start.14) | collective-permute-done | bytes 65568 | tf_op jit(solution)/shard_map/ppermute | solution.py:199
  106.0 3.9 %collective-permute-done.15 = f32[4,2,32,256]{3,2,1,0:T(8,128)S(1)} collective-permute-done((f32[4,2,32,256]{3,2,1,0:T(8,128)S(1)}, f32[4,2,32,256]{3,2,1,0:T(8,128)S(1)}, u32[]{:S(2)}, u32[]{:S(2)}) %collective-permute-start.15) | collective-permute-done | bytes 262176 | tf_op jit(solution)/shard_map/ppermute | solution.py:199
  111.2 1.7 shard_map.62.refs_2_
  114.3 2.8 %gather_fusion.1 = f32[16,2,32,256]{3,2,1,0:T(8,128)} fusion(f32[16,2,32,256]{3,2,1,0:T(8,128)} %constant_dynamic-update-slice_fusion.5, s32[1024]{0:T(1024)S(1)} %pad_clamp_fusion), kind=kCustom, calls=%fused_computation.4 | custom fusion | bytes 2097216 | tf_op jit(solution)/shard_map/jit(_take)/gather | solution.py:221
  117.1 1.4 select_bitcast_fusion
  118.5 19.5 %shard_map.59 = (bf16[16,512,256]{2,1,0:T(8,128)(2,1)S(1)}, bf16[16,512,256]{2,1,0:T(8,128)(2,1)S(1)}) custom-call(f32[512,16,1024]{2,1,0:T(8,128)} %core_hbm.3, f32[1024,256]{1,0:T(8,128)S(1)} %bitcast.18), custom_call_target="tpu_custom_call" | custom-call | tf_op jit(solution)/shard_map/pallas_call | solution.py:133
  138.0 1.7 shard_map.63.refs_3_
  139.7 3.9 %shard_map.64 = f32[512,256]{1,0:T(8,128)S(1)} custom-call(bf16[16,512,256]{2,1,0:T(8,128)(2,1)S(1)} %get-tuple-element.29.high, bf16[16,512,256]{2,1,0:T(8,128)(2,1)S(1)} %get-tuple-element.30.low, bf16[8,512,128]{2,1,0:T(8,128)(2,1)S(1)} %shard_map.60.refs_0_, bf16[8,512,128]{2,1,0:T(8,128)(2,1)S(1)} %shard_map.61.refs_1_, ...), custom_call_target="tpu_custom_call" | custom-call | tf_op jit(solution)/shard_map/pallas_call | solution.py:161
  145.2 1.2 collective-permute-done.18
  147.0 5.2 %collective-permute-done.19 = f32[4,32,256]{2,1,0:T(8,128)S(1)} collective-permute-done((f32[4,32,256]{2,1,0:T(8,128)S(1)}, f32[4,32,256]{2,1,0:T(8,128)S(1)}, u32[]{:S(2)}, u32[]{:S(2)}) %collective-permute-start.19) | collective-permute-done | bytes 131104 | tf_op jit(solution)/shard_map/ppermute | solution.py:199
  152.3 1.4 collective-permute-start.21
  153.7 3.0 %collective-permute-start.22 = (f32[1,32,256]{2,1,0:T(8,128)S(1)}, f32[1,32,256]{2,1,0:T(8,128)S(1)}, u32[]{:S(2)}, u32[]{:S(2)}) collective-permute-start(f32[1,32,256]{2,1,0:T(8,128)S(1)} %get-tuple-element.48), channel_id=1, source_target_pairs={{0,24},{2,26},{4,28},{6,30},{8,16},{10,18},{12,20},{14,22},{16,8},... | collective-permute-start | bytes 98312 | tf_op jit(solution)/shard_map/ppermute | solution.py:199
  157.6 1.8 %collective-permute-done.22 = f32[1,32,256]{2,1,0:T(8,128)S(1)} collective-permute-done((f32[1,32,256]{2,1,0:T(8,128)S(1)}, f32[1,32,256]{2,1,0:T(8,128)S(1)}, u32[]{:S(2)}, u32[]{:S(2)}) %collective-permute-start.22) | collective-permute-done | bytes 32800 | tf_op jit(solution)/shard_map/ppermute | solution.py:199
  159.5 3.9 %collective-permute-start.24 = (f32[1,32,256]{2,1,0:T(8,128)S(1)}, f32[1,32,256]{2,1,0:T(8,128)S(1)}, u32[]{:S(2)}, u32[]{:S(2)}) collective-permute-start(f32[1,32,256]{2,1,0:T(8,128)S(1)} %get-tuple-element.34), channel_id=1, source_target_pairs={{0,16},{2,18},{4,20},{6,22},{8,24},{10,26},{12,28},{14,30},{16,0},... | collective-permute-start | bytes 98312 | tf_op jit(solution)/shard_map/ppermute | solution.py:199
  163.9 2.0 %collective-permute-done.24 = f32[1,32,256]{2,1,0:T(8,128)S(1)} collective-permute-done((f32[1,32,256]{2,1,0:T(8,128)S(1)}, f32[1,32,256]{2,1,0:T(8,128)S(1)}, u32[]{:S(2)}, u32[]{:S(2)}) %collective-permute-start.24) | collective-permute-done | bytes 32800 | tf_op jit(solution)/shard_map/ppermute | solution.py:199
  165.8 3.2 %collective-permute-done.25 = f32[1,32,256]{2,1,0:T(8,128)S(1)} collective-permute-done((f32[1,32,256]{2,1,0:T(8,128)S(1)}, f32[1,32,256]{2,1,0:T(8,128)S(1)}, u32[]{:S(2)}, u32[]{:S(2)}) %collective-permute-start.25) | collective-permute-done | bytes 32800 | tf_op jit(solution)/shard_map/ppermute | solution.py:199
  169.7 4.4 %collective-permute-done.26 = f32[4,32,256]{2,1,0:T(8,128)S(1)} collective-permute-done((f32[4,32,256]{2,1,0:T(8,128)S(1)}, f32[4,32,256]{2,1,0:T(8,128)S(1)}, u32[]{:S(2)}, u32[]{:S(2)}) %collective-permute-start.26) | collective-permute-done | bytes 131104 | tf_op jit(solution)/shard_map/ppermute | solution.py:199
  174.2 1.5 collective-permute-done.27
  176.4 0.9 broadcast_select_fusion
  (82 shorter events, 16.2 us)
Async XLA Ops:
  0.9 7.3 %collective-permute-start = (f32[128,256]{1,0:T(8,128)S(1)}, f32[128,256]{1,0:T(8,128)S(1)}, u32[]{:S(2)}, u32[]{:S(2)}) collective-permute-start(f32[128,256]{1,0:T(8,128)S(1)} %constant_dynamic-slice_fusion), channel_id=1, source_target_pairs={{0,1},{1,0},{2,3},{3,2},{4,5},{5,4},{6,7},{7,6},{8,9},{9,8},{10,11... | collective-permute-start | bytes 393224 | tf_op jit(solution)/shard_map/ppermute | solution.py:203
  4.0 3.1 %copy-start.3 = (f32[128,16,256]{2,1,0:T(8,128)S(1)}, f32[128,16,256]{2,1,0:T(8,128)}, u32[]{:S(2)}) copy-start(f32[128,16,256]{2,1,0:T(8,128)} %param.12) | copy-start | bytes 6291460
  8.3 5.0 %collective-permute-start.1 = (f32[1,128,256]{2,1,0:T(8,128)S(1)}, f32[1,128,256]{2,1,0:T(8,128)S(1)}, u32[]{:S(2)}, u32[]{:S(2)}) collective-permute-start(f32[1,128,256]{2,1,0:T(8,128)S(1)} %bitcast.21), channel_id=1, source_target_pairs={{0,4},{2,6},{4,0},{6,2},{8,12},{10,14},{12,8},{14,10},{16,20},{18,... | collective-permute-start | bytes 393224 | tf_op jit(solution)/shard_map/ppermute | solution.py:199
  9.8 47.0 %collective-permute-start.3 = (f32[128,8,256]{2,1,0:T(8,128)}, f32[128,8,256]{2,1,0:T(8,128)S(1)}, u32[]{:S(2)}, u32[]{:S(2)}) collective-permute-start(f32[128,8,256]{2,1,0:T(8,128)} %get-tuple-element.23), channel_id=1, source_target_pairs={{0,1},{1,0},{2,3},{3,2},{4,5},{5,4},{6,7},{7,6},{8,9},{9,8},{10,11... | collective-permute-start | bytes 3145736 | tf_op jit(solution)/shard_map/ppermute | solution.py:203
  10.7 46.2 %collective-permute-start.4 = (f32[128,8,256]{2,1,0:T(8,128)}, f32[128,8,256]{2,1,0:T(8,128)S(1)}, u32[]{:S(2)}, u32[]{:S(2)}) collective-permute-start(f32[128,8,256]{2,1,0:T(8,128)} %get-tuple-element.24), channel_id=1, source_target_pairs={{0,1},{1,0},{2,3},{3,2},{4,5},{5,4},{6,7},{7,6},{8,9},{9,8},{10,11... | collective-permute-start | bytes 3145736 | tf_op jit(solution)/shard_map/ppermute | solution.py:203
  14.0 1.9 %collective-permute-start.2 = (f32[2,128,256]{2,1,0:T(8,128)}, f32[2,128,256]{2,1,0:T(8,128)}, u32[]{:S(2)}, u32[]{:S(2)}) collective-permute-start(f32[2,128,256]{2,1,0:T(8,128)} %pad_maximum_fusion.1), channel_id=1, source_target_pairs={{0,2},{2,0},{4,6},{6,4},{8,10},{10,8},{12,14},{14,12},{16,18},{18,... | collective-permute-start | bytes 786440 | tf_op jit(solution)/shard_map/ppermute | solution.py:199
  23.0 19.6 %copy-start = (f32[128,16,256]{2,1,0:T(8,128)S(1)}, f32[128,16,256]{2,1,0:T(8,128)}, u32[]{:S(2)}) copy-start(f32[128,16,256]{2,1,0:T(8,128)} %refs_0_.1) | copy-start | bytes 6291460
  62.6 1.6 collective-permute-start.5
  62.7 25.6 %collective-permute-start.10 = (f32[128,8,256]{2,1,0:T(8,128)S(1)}, f32[128,8,256]{2,1,0:T(8,128)S(1)}, u32[]{:S(2)}, u32[]{:S(2)}) collective-permute-start(f32[128,8,256]{2,1,0:T(8,128)S(1)} %get-tuple-element.26.sketch_ref), channel_id=1, source_target_pairs={{0,1},{1,0},{2,3},{3,2},{4,5},{5,4},{6,7},{7,6},{8,9},{9,8},{10,11... | collective-permute-start | bytes 3145736 | tf_op jit(solution)/shard_map/ppermute | solution.py:203
  64.3 5.6 %collective-permute-start.6 = (f32[4,32,256]{2,1,0:T(8,128)S(1)}, f32[4,32,256]{2,1,0:T(8,128)S(1)}, u32[]{:S(2)}, u32[]{:S(2)}) collective-permute-start(f32[4,32,256]{2,1,0:T(8,128)S(1)} %slice.95), channel_id=1, source_target_pairs={{0,4},{2,6},{4,0},{6,2},{8,12},{10,14},{12,8},{14,10},{16,20},{18,... | collective-permute-start | bytes 393224 | tf_op jit(solution)/shard_map/ppermute | solution.py:199
  69.9 4.5 %collective-permute-start.7 = (f32[1,32,256]{2,1,0:T(8,128)S(1)}, f32[1,32,256]{2,1,0:T(8,128)S(1)}, u32[]{:S(2)}, u32[]{:S(2)}) collective-permute-start(f32[1,32,256]{2,1,0:T(8,128)S(1)} %get-tuple-element.50), channel_id=1, source_target_pairs={{0,8},{2,10},{4,12},{6,14},{8,0},{10,2},{12,4},{14,6},{16,24},{18,... | collective-permute-start | bytes 98312 | tf_op jit(solution)/shard_map/ppermute | solution.py:199
  71.6 5.1 %collective-permute-start.8 = (f32[1,32,256]{2,1,0:T(8,128)S(1)}, f32[1,32,256]{2,1,0:T(8,128)S(1)}, u32[]{:S(2)}, u32[]{:S(2)}) collective-permute-start(f32[1,32,256]{2,1,0:T(8,128)S(1)} %get-tuple-element.52), channel_id=1, source_target_pairs={{0,16},{2,18},{4,20},{6,22},{8,24},{10,26},{12,28},{14,30},{16,0},... | collective-permute-start | bytes 98312 | tf_op jit(solution)/shard_map/ppermute | solution.py:199
  74.2 5.7 %collective-permute-start.9 = (f32[1,32,256]{2,1,0:T(8,128)S(1)}, f32[1,32,256]{2,1,0:T(8,128)S(1)}, u32[]{:S(2)}, u32[]{:S(2)}) collective-permute-start(f32[1,32,256]{2,1,0:T(8,128)S(1)} %get-tuple-element.51), channel_id=1, source_target_pairs={{0,24},{2,26},{4,28},{6,30},{8,16},{10,18},{12,20},{14,22},{16,8},... | collective-permute-start | bytes 98312 | tf_op jit(solution)/shard_map/ppermute | solution.py:199
  88.3 1.0 copy-start.1
  89.3 3.9 %collective-permute-start.11 = (f32[1,32,256]{2,1,0:T(8,128)S(1)}, f32[1,32,256]{2,1,0:T(8,128)S(1)}, u32[]{:S(2)}, u32[]{:S(2)}) collective-permute-start(f32[1,32,256]{2,1,0:T(8,128)S(1)} %fusion.16), channel_id=1, source_target_pairs={{0,1},{1,0},{2,3},{3,2},{4,5},{5,4},{6,7},{7,6},{8,9},{9,8},{10,11... | collective-permute-start | bytes 98312 | tf_op jit(solution)/shard_map/ppermute | solution.py:203
  93.2 5.6 %collective-permute-start.12 = (f32[1,2,32,256]{3,2,1,0:T(8,128)S(1)}, f32[1,2,32,256]{3,2,1,0:T(8,128)S(1)}, u32[]{:S(2)}, u32[]{:S(2)}) collective-permute-start(f32[1,2,32,256]{3,2,1,0:T(8,128)S(1)} %get-tuple-element.36), channel_id=1, source_target_pairs={{0,8},{2,10},{4,12},{6,14},{8,0},{10,2},{12,4},{14,6},{16,24},{18,... | collective-permute-start | bytes 196616 | tf_op jit(solution)/shard_map/ppermute | solution.py:199
  94.9 6.6 %collective-permute-start.13 = (f32[1,2,32,256]{3,2,1,0:T(8,128)S(1)}, f32[1,2,32,256]{3,2,1,0:T(8,128)S(1)}, u32[]{:S(2)}, u32[]{:S(2)}) collective-permute-start(f32[1,2,32,256]{3,2,1,0:T(8,128)S(1)} %get-tuple-element.36), channel_id=1, source_target_pairs={{0,16},{2,18},{4,20},{6,22},{8,24},{10,26},{12,28},{14,30},{16,0},... | collective-permute-start | bytes 196616 | tf_op jit(solution)/shard_map/ppermute | solution.py:199
  97.4 6.1 %collective-permute-start.14 = (f32[1,2,32,256]{3,2,1,0:T(8,128)S(1)}, f32[1,2,32,256]{3,2,1,0:T(8,128)S(1)}, u32[]{:S(2)}, u32[]{:S(2)}) collective-permute-start(f32[1,2,32,256]{3,2,1,0:T(8,128)S(1)} %get-tuple-element.36), channel_id=1, source_target_pairs={{0,24},{2,26},{4,28},{6,30},{8,16},{10,18},{12,20},{14,22},{16,8},... | collective-permute-start | bytes 196616 | tf_op jit(solution)/shard_map/ppermute | solution.py:199
  97.7 40.3 %collective-permute-start.17 = (f32[128,8,256]{2,1,0:T(8,128)}, f32[128,8,256]{2,1,0:T(8,128)}, u32[]{:S(2)}, u32[]{:S(2)}) collective-permute-start(f32[128,8,256]{2,1,0:T(8,128)} %get-tuple-element.32.sketch_ref), channel_id=1, source_target_pairs={{0,1},{1,0},{2,3},{3,2},{4,5},{5,4},{6,7},{7,6},{8,9},{9,8},{10,11... | collective-permute-start | bytes 3145736 | tf_op jit(solution)/shard_map/ppermute | solution.py:203
  103.5 6.4 %collective-permute-start.15 = (f32[4,2,32,256]{3,2,1,0:T(8,128)S(1)}, f32[4,2,32,256]{3,2,1,0:T(8,128)S(1)}, u32[]{:S(2)}, u32[]{:S(2)}) collective-permute-start(f32[4,2,32,256]{3,2,1,0:T(8,128)S(1)} %pad_maximum_fusion.2), channel_id=1, source_target_pairs={{0,4},{2,6},{4,0},{6,2},{8,12},{10,14},{12,8},{14,10},{16,20},{18,... | collective-permute-start | bytes 786440 | tf_op jit(solution)/shard_map/ppermute | solution.py:199
  110.7 2.2 %copy-start.2 = (f32[128,8,256]{2,1,0:T(8,128)S(1)}, f32[128,8,256]{2,1,0:T(8,128)}, u32[]{:S(2)}) copy-start(f32[128,8,256]{2,1,0:T(8,128)} %copy-done.1) | copy-start | bytes 3145732
  110.7 2.7 %collective-permute-start.16 = (f32[8,2,32,256]{3,2,1,0:T(8,128)S(1)}, f32[8,2,32,256]{3,2,1,0:T(8,128)S(1)}, u32[]{:S(2)}, u32[]{:S(2)}) collective-permute-start(f32[8,2,32,256]{3,2,1,0:T(8,128)S(1)} %get-tuple-element.43), channel_id=1, source_target_pairs={{0,2},{2,0},{4,6},{6,4},{8,10},{10,8},{12,14},{14,12},{16,18},{18,... | collective-permute-start | bytes 1572872 | tf_op jit(solution)/shard_map/ppermute | solution.py:199
  144.6 1.7 collective-permute-start.18
  146.4 5.8 %collective-permute-start.19 = (f32[4,32,256]{2,1,0:T(8,128)S(1)}, f32[4,32,256]{2,1,0:T(8,128)S(1)}, u32[]{:S(2)}, u32[]{:S(2)}) collective-permute-start(f32[4,32,256]{2,1,0:T(8,128)S(1)} %slice.103), channel_id=1, source_target_pairs={{0,4},{2,6},{4,0},{6,2},{8,12},{10,14},{12,8},{14,10},{16,20},{18,... | collective-permute-start | bytes 393224 | tf_op jit(solution)/shard_map/ppermute | solution.py:199
  152.3 4.5 %collective-permute-start.20 = (f32[1,32,256]{2,1,0:T(8,128)S(1)}, f32[1,32,256]{2,1,0:T(8,128)S(1)}, u32[]{:S(2)}, u32[]{:S(2)}) collective-permute-start(f32[1,32,256]{2,1,0:T(8,128)S(1)} %get-tuple-element.47), channel_id=1, source_target_pairs={{0,8},{2,10},{4,12},{6,14},{8,0},{10,2},{12,4},{14,6},{16,24},{18,... | collective-permute-start | bytes 98312 | tf_op jit(solution)/shard_map/ppermute | solution.py:199
  152.3 5.3 %collective-permute-start.21 = (f32[1,32,256]{2,1,0:T(8,128)S(1)}, f32[1,32,256]{2,1,0:T(8,128)S(1)}, u32[]{:S(2)}, u32[]{:S(2)}) collective-permute-start(f32[1,32,256]{2,1,0:T(8,128)S(1)} %get-tuple-element.49), channel_id=1, source_target_pairs={{0,16},{2,18},{4,20},{6,22},{8,24},{10,26},{12,28},{14,30},{16,0},... | collective-permute-start | bytes 98312 | tf_op jit(solution)/shard_map/ppermute | solution.py:199
  153.7 5.7 %collective-permute-start.22 = (f32[1,32,256]{2,1,0:T(8,128)S(1)}, f32[1,32,256]{2,1,0:T(8,128)S(1)}, u32[]{:S(2)}, u32[]{:S(2)}) collective-permute-start(f32[1,32,256]{2,1,0:T(8,128)S(1)} %get-tuple-element.48), channel_id=1, source_target_pairs={{0,24},{2,26},{4,28},{6,30},{8,16},{10,18},{12,20},{14,22},{16,8},... | collective-permute-start | bytes 98312 | tf_op jit(solution)/shard_map/ppermute | solution.py:199
  159.4 4.5 %collective-permute-start.23 = (f32[1,32,256]{2,1,0:T(8,128)S(1)}, f32[1,32,256]{2,1,0:T(8,128)S(1)}, u32[]{:S(2)}, u32[]{:S(2)}) collective-permute-start(f32[1,32,256]{2,1,0:T(8,128)S(1)} %get-tuple-element.34), channel_id=1, source_target_pairs={{0,8},{2,10},{4,12},{6,14},{8,0},{10,2},{12,4},{14,6},{16,24},{18,... | collective-permute-start | bytes 98312 | tf_op jit(solution)/shard_map/ppermute | solution.py:199
  159.5 6.3 %collective-permute-start.24 = (f32[1,32,256]{2,1,0:T(8,128)S(1)}, f32[1,32,256]{2,1,0:T(8,128)S(1)}, u32[]{:S(2)}, u32[]{:S(2)}) collective-permute-start(f32[1,32,256]{2,1,0:T(8,128)S(1)} %get-tuple-element.34), channel_id=1, source_target_pairs={{0,16},{2,18},{4,20},{6,22},{8,24},{10,26},{12,28},{14,30},{16,0},... | collective-permute-start | bytes 98312 | tf_op jit(solution)/shard_map/ppermute | solution.py:199
  163.4 5.7 %collective-permute-start.25 = (f32[1,32,256]{2,1,0:T(8,128)S(1)}, f32[1,32,256]{2,1,0:T(8,128)S(1)}, u32[]{:S(2)}, u32[]{:S(2)}) collective-permute-start(f32[1,32,256]{2,1,0:T(8,128)S(1)} %get-tuple-element.34), channel_id=1, source_target_pairs={{0,24},{2,26},{4,28},{6,30},{8,16},{10,18},{12,20},{14,22},{16,8},... | collective-permute-start | bytes 98312 | tf_op jit(solution)/shard_map/ppermute | solution.py:199
  169.1 5.0 %collective-permute-start.26 = (f32[4,32,256]{2,1,0:T(8,128)S(1)}, f32[4,32,256]{2,1,0:T(8,128)S(1)}, u32[]{:S(2)}, u32[]{:S(2)}) collective-permute-start(f32[4,32,256]{2,1,0:T(8,128)S(1)} %pad_maximum_fusion.3), channel_id=1, source_target_pairs={{0,4},{2,6},{4,0},{6,2},{8,12},{10,14},{12,8},{14,10},{16,20},{18,... | collective-permute-start | bytes 393224 | tf_op jit(solution)/shard_map/ppermute | solution.py:199
  174.1 1.6 collective-permute-start.27

commit v2 on v1

v2 whole, which is shorter than its diff:
```python
import functools

import jax
import jax.numpy as jnp
from jax import lax
from jax.experimental import pallas as pl
from jax.experimental.pallas import tpu as pltpu
from jax.sharding import PartitionSpec as P

F32, BF16 = jnp.float32, jnp.bfloat16
LANES = 128
HBM = pl.BlockSpec(memory_space=pl.ANY)
VMEM = pl.BlockSpec(memory_space=pltpu.VMEM)
SMEM = pl.BlockSpec(memory_space=pltpu.SMEM)


def halves(x):
    high = x.astype(BF16)
    return high, (x - high.astype(F32)).astype(BF16)


def dot(a, b):
    return jnp.dot(a, b, preferred_element_type=F32)


def prepare_kernel(sketch_ref, out_ref, axis=1):
    size = sketch_ref.shape[1 - axis]
    for i in range(sketch_ref.shape[axis]):
        high, low = halves((sketch_ref[:, i, :] if axis else sketch_ref[i]).T)
        out_ref[i, :, :size] = high
        out_ref[i, :, size:] = low


def hidden_loop(rows, slots, core_hbm, spread, high, low, buf, sems, weights, tile):
    count, slices, depth = core_hbm.shape
    columns = high.shape[2]
    steps = count // rows

    def copy(k):
        slot = lax.rem(k, slots)
        return pltpu.make_async_copy(core_hbm.at[pl.ds(k * rows, rows)], buf.at[slot], sems.at[slot])

    for k in range(min(slots - 1, steps)):
        copy(k).start()
    spread(weights)

    def block(k, _):
        @pl.when(k + slots - 1 < steps)
        def _():
            copy(k + slots - 1).start()

        copy(k).wait()
        h, l = halves(buf[lax.rem(k, slots)].reshape(rows * slices, depth))
        result = dot(jnp.concatenate([h, h, l], axis=1), weights[...])
        for j in range(columns // LANES):
            tile[j] = result[:, j * LANES : (j + 1) * LANES]
        at = pl.ds(pl.multiple_of(k * rows, rows), rows)
        for i in range(slices):
            for j in range(columns // LANES):
                h, l = halves(tile[j, pl.ds(i, rows, stride=slices), :])
                high[i, at, j * LANES : (j + 1) * LANES] = h
                low[i, at, j * LANES : (j + 1) * LANES] = l
        return 0

    lax.fori_loop(0, steps, block, 0)


def spread_whole(carried_ref, weights):
    depth = carried_ref.shape[0]
    h, l = halves(carried_ref[...])
    weights[0:depth] = h
    weights[depth : 2 * depth] = l
    weights[2 * depth :] = h


def first_kernel(rows, slots, core_hbm, carried_ref, sketch_ref, high, low, out, prepared, *scratch):
    hidden_loop(rows, slots, core_hbm, functools.partial(spread_whole, carried_ref), high, low, *scratch)
    prepare_kernel(sketch_ref, prepared)
    out[...] = jnp.zeros_like(out)
    multiply(0, sketch_ref.shape[1], high, low, [(prepared, 0)], out)


def hidden_kernel(rows, slots, core_hbm, carried_ref, high, low, *scratch):
    hidden_loop(rows, slots, core_hbm, functools.partial(spread_whole, carried_ref), high, low, *scratch)


def spread_pieces(ranks, place_ref, parts, weights):
    own, rank = place_ref[0], place_ref[1]
    _, _, rows, columns = parts[0].shape
    depth, width = weights.shape[0] // 3, columns // ranks
    position = 0
    for part in parts:
        for p in range(part.shape[0]):
            for d in range(ranks):
                source = lax.rem(rank - d + ranks, ranks)
                at = pl.multiple_of(source * (depth // ranks) + (own ^ position) * rows, rows)
                for e in range(ranks):
                    to = pl.ds(pl.multiple_of(lax.rem(source - e + ranks, ranks) * width, width), width)
                    h, l = halves(part[p, d, :, e * width : (e + 1) * width])
                    weights[pl.ds(at, rows), to] = h
                    weights[pl.ds(at + depth, rows), to] = l
                    weights[pl.ds(at + 2 * depth, rows), to] = h
            position += 1


def hidden_of_pieces_kernel(rows, slots, ranks, core_hbm, place_ref, *refs):
    parts, scratch = refs[:-6], refs[-6:]
    hidden_loop(rows, slots, core_hbm, functools.partial(spread_pieces, ranks, place_ref, parts), *scratch)


def multiply(first, count, high, low, sketches, out):
    def add(start, size):
        slices = range(size)
        h = jnp.concatenate([high[first + start + t] for t in slices], axis=1)
        l = jnp.concatenate([low[first + start + t] for t in slices], axis=1)
        sums, highs = [], []
        for s, at in sketches:
            both = jnp.concatenate([s[at + start + t] for t in slices], axis=0)
            width = both.shape[1] // 2
            result = dot(h, both)
            sums.append(result[:, :width] + result[:, width:])
            highs.append(both[:, :width])
        out[...] += jnp.concatenate(sums, axis=1) + dot(l, jnp.concatenate(highs, axis=1))

    def body(g, _):
        add(g * GROUP, GROUP)
        return 0

    whole = count // GROUP
    lax.fori_loop(0, whole, body, 0)
    if count % GROUP:
        add(whole * GROUP, count % GROUP)


def store(place_ref, acc, out):
    if len(out.shape) == 2:
        out[...] = acc[...]
        return
    count, rows, _ = out.shape
    for p in range(count):
        out[p] = acc[pl.ds(pl.multiple_of((place_ref[0] ^ p) * rows, rows), rows), :]


def second_kernel(place_ref, high, low, own_ref, *refs):
    sketches, (out, prepared, acc) = refs[:-3], refs[-3:]
    width = own_ref.shape[1]
    acc[:, :width] = own_ref[...]
    for d, sketch in enumerate(sketches):
        at = slice((d + 1) * width, (d + 2) * width)
        acc[:, at] = jnp.zeros_like(own_ref)
        prepare_kernel(sketch, prepared)
        multiply(0, sketch.shape[1], high, low, [(prepared, 0)], acc.at[:, at])
    store(place_ref, acc, out)


def joined_kernel(early, place_ref, high, low, *refs):
    sketches, (out, acc) = refs[:-2], refs[-2:]
    acc[...] = jnp.zeros_like(acc)
    slices = high.shape[0]
    firsts, rests, at = [], [], 0
    while at < len(sketches):
        if sketches[at].shape[0] == slices:
            firsts.append((sketches[at], 0))
            rests.append((sketches[at], early))
            at += 1
        else:
            firsts.append((sketches[at], 0))
            rests.append((sketches[at + 1], 0))
            at += 2
    multiply(0, early, high, low, firsts, acc)
    multiply(early, slices - early, high, low, rests, acc)
    store(place_ref, acc, out)


def settle_kernel(ranks, place_ref, *refs):
    parts, out = refs[:-1], refs[-1]
    _, rows, columns = parts[0].shape
    width = columns // ranks
    position = 0
    for part in parts:
        for p in range(part.shape[0]):
            at = pl.ds(pl.multiple_of((place_ref[0] ^ position) * rows, rows), rows)
            for e in range(ranks):
                to = lax.rem(place_ref[1] - e + ranks, ranks) * width
                out[at, pl.ds(pl.multiple_of(to, width), width)] = part[p, :, e * width : (e + 1) * width]
            position += 1


def hidden_shape(core, columns):
    return (core.shape[1], core.shape[0], columns)


def loop_scratch(core, columns, rows, slots):
    _, slices, depth = core.shape
    return [
        pltpu.VMEM((slots, rows, slices, depth), F32),
        pltpu.SemaphoreType.DMA((slots,)),
        pltpu.VMEM((3 * depth, columns), BF16),
        pltpu.VMEM((columns // LANES, rows * slices, LANES), F32),
    ]


def limit(mib):
    return pltpu.CompilerParams(vmem_limit_bytes=mib << 20)


ROWS, SLOTS, GROUP = 64, 3, 4


def cost(flops, size):
    return pl.CostEstimate(flops=flops, bytes_accessed=size, transcendentals=0)


def hidden(core, carried, place=None):
    count, slices, depth = core.shape
    columns = (carried if place is None else carried[0]).shape[-1]
    out = jax.ShapeDtypeStruct(hidden_shape(core, columns), BF16)
    if place is None:
        kernel, operands = functools.partial(hidden_kernel, ROWS, SLOTS), (carried,)
    else:
        ranks = carried[0].shape[1]
        kernel, operands = functools.partial(hidden_of_pieces_kernel, ROWS, SLOTS, ranks), (place, *carried)
    return pl.pallas_call(
        kernel,
        out_shape=(out, out),
        in_specs=[HBM] + ([VMEM] if place is None else [SMEM] + [VMEM] * len(carried)),
        out_specs=(VMEM, VMEM),
        scratch_shapes=loop_scratch(core, columns, ROWS, SLOTS),
        compiler_params=limit(32),
        cost_estimate=cost(6 * count * slices * depth * columns, 4 * core.size) if place is None else cost(1, 1),
    )(core, *operands)


def product_cost(high, slices, columns):
    return cost(6 * high.shape[1] * slices * high.shape[2] * columns, 4 * high.size)


def first_step(core, carried, sketch):
    size, slices, depth = sketch.shape
    columns = carried.shape[1]
    out = jax.ShapeDtypeStruct(hidden_shape(core, columns), BF16)
    return pl.pallas_call(
        functools.partial(first_kernel, ROWS, SLOTS),
        out_shape=(out, out, jax.ShapeDtypeStruct((core.shape[0], size), F32)),
        in_specs=[HBM, VMEM, VMEM],
        out_specs=(VMEM,) * 3,
        scratch_shapes=[pltpu.VMEM((slices, depth, 2 * size), BF16)] + loop_scratch(core, columns, ROWS, SLOTS),
        compiler_params=limit(36),
        cost_estimate=cost(6 * core.size * columns, 4 * core.size),
    )(core, carried, sketch)


def out_shape(rows, columns, count):
    return jax.ShapeDtypeStruct((count, rows // count, columns) if count else (rows, columns), F32)


def second_product(place, high, low, own, sketches, count):
    size, slices, depth = sketches[0].shape
    rows, columns = high.shape[1], size * (1 + len(sketches))
    return pl.pallas_call(
        second_kernel,
        out_shape=out_shape(rows, columns, count),
        in_specs=[SMEM] + [VMEM] * (3 + len(sketches)),
        out_specs=VMEM,
        scratch_shapes=[pltpu.VMEM((slices, depth, 2 * size), BF16), pltpu.VMEM((rows, columns), F32)],
        compiler_params=limit(24),
        cost_estimate=product_cost(high, slices, columns - size),
    )(place, high, low, own, *sketches)


def joined(place, high, low, early, chunks, columns, count):
    rows = high.shape[1]
    return pl.pallas_call(
        functools.partial(joined_kernel, early),
        out_shape=out_shape(rows, columns, count),
        in_specs=[SMEM] + [VMEM] * (2 + len(chunks)),
        out_specs=VMEM,
        scratch_shapes=[pltpu.VMEM((rows, columns), F32)],
        compiler_params=limit(24),
        cost_estimate=product_cost(high, high.shape[0], columns),
    )(place, high, low, *chunks)


def settle(place, parts, ranks):
    _, rows, columns = parts[0].shape
    return pl.pallas_call(
        functools.partial(settle_kernel, ranks),
        out_shape=jax.ShapeDtypeStruct((rows * sum(p.shape[0] for p in parts), columns), F32),
        in_specs=[SMEM] + [VMEM] * len(parts),
        out_specs=VMEM,
        compiler_params=limit(8),
    )(place, *parts)


def prepare(sketch, axis=1):
    slices, size, depth = sketch.shape[axis], sketch.shape[1 - axis], sketch.shape[2]
    return pl.pallas_call(
        functools.partial(prepare_kernel, axis=axis),
        out_shape=jax.ShapeDtypeStruct((slices, depth, 2 * size), BF16),
        in_specs=[VMEM],
        out_specs=VMEM,
        compiler_params=limit(16),
        cost_estimate=cost(0, 8 * sketch.size),
    )(sketch)


def digit_groups(count):
    bits = count.bit_length() - 1
    groups, low = [], 0
    while low < bits:
        width = 1 if low < 2 else min(2, bits - low)
        groups.append((low, width))
        low += width
    return groups


def piece_of(index, groups):
    piece = 0
    for low, width in groups:
        piece = (piece << width) | ((index >> low) & ((1 << width) - 1))
    return piece


def partner(x, count, low, distance):
    return lax.ppermute(x, "mode", [(i, i ^ (distance << low)) for i in range(count)])


def shift(x, ranks, d):
    return lax.ppermute(x, "rank", [(i, (i + d) % ranks) for i in range(ranks)])


def reduce_scatter(x, count, groups):
    for low, width in groups:
        size = x.shape[0] >> width
        arrived = [partner(x[d * size : (d + 1) * size], count, low, d) for d in range(1, 1 << width)]
        x = sum(arrived, x[:size])
    return x


def all_gather_parts(x, count, groups):
    parts = [x]
    for low, width in reversed(groups):
        x = jnp.concatenate(parts, axis=0)
        parts = [x] + [partner(x, count, low, d) for d in range(1, 1 << width)]
    return parts


def all_gather(x, count, groups):
    return jnp.concatenate(all_gather_parts(x, count, groups), axis=0)


def in_order(x, own):
    return jnp.take(x, own ^ jnp.arange(x.shape[0]), axis=0)


def by_rank(blocks, rank, axis):
    joined = jnp.concatenate(blocks[::-1], axis=axis)
    return jnp.roll(joined, (rank + 1) * blocks[0].shape[axis], axis=axis)


def quad_part(x, modes, mode):
    groups = digit_groups(modes)[:2]
    size = x.shape[0] >> len(groups)
    return lax.dynamic_slice_in_dim(x, piece_of(mode, groups) * size, size)


def all_rows(x, parts, modes, rank, mode):
    groups = digit_groups(modes)[:2]
    own = piece_of(mode, groups)
    blocks = [in_order(all_gather(part[None], modes, groups), own).reshape(x.shape) for part in parts]
    return by_rank([x] + blocks, rank, 0)


def shards(modes, ranks, core_right, sketch_right, core_left, sketch_left, carry_in):
    mode, rank = lax.axis_index("mode"), lax.axis_index("rank")
    groups = digit_groups(modes)
    own = piece_of(mode, groups)
    place = jnp.stack([own, rank])
    slices, size = core_right.shape[1], sketch_right.shape[0]
    early = max(1, slices // 8)
    count = modes if carry_in.shape[0] % (16 * modes) == 0 and size % LANES == 0 else 0

    def shifted(x):
        return [shift(x, ranks, d) for d in range(1, ranks)]

    def scattered(term):
        if not count:
            term = by_rank(jnp.split(term, ranks, axis=1), rank, 1)
            term = in_order(term.reshape((modes, term.shape[0] // modes) + term.shape[1:]), own)
        return reduce_scatter(term, modes, groups)

    sketch_slices = jnp.swapaxes(sketch_left, 0, 1)
    left_a, left_b = sketch_slices[:early], sketch_slices[early:]
    part = quad_part(carry_in, modes, mode)
    parts = shifted(part)
    _, right = lax.optimization_barrier((part, sketch_right))
    arrived = shifted(right)
    carried = all_rows(carry_in, parts, modes, rank, mode)
    high, low, term = first_step(core_right, carried, sketch_right)
    arrived, left_a = lax.optimization_barrier((arrived, left_a))
    left_a_arrived = shifted(left_a)
    term = second_product(place, high, low, term, arrived, count)
    middle = scattered(term)
    middle, left_a_arrived = lax.optimization_barrier((middle, left_a_arrived))
    middles, left_b = lax.optimization_barrier((shifted(middle), left_b))
    left_b_arrived = shifted(left_b)
    if count:
        both = jnp.concatenate([middle] + middles)[None]
        high, low = hidden(core_left, all_gather_parts(both, modes, groups), place)
    else:
        both = by_rank([middle] + middles, rank, 0)[None]
        both = in_order(all_gather(both, modes, groups), own)
        high, low = hidden(core_left, jnp.swapaxes(both, 0, 1).reshape(carried.shape))

    if count:
        chunks = [prepare(sketch_left)]
        for pair in zip(left_a_arrived, left_b_arrived):
            chunks += [prepare(x, 0) for x in pair]
    else:
        whole = [jnp.concatenate(pair) for pair in zip(left_a_arrived, left_b_arrived)]
        chunks = [prepare(jnp.concatenate([sketch_slices] + whole, axis=1), 0)]
    term = joined(place, high, low, early, chunks, size * ranks, count)
    result = all_gather_parts(scattered(term), modes, groups)
    if count:
        return settle(place, result, ranks)
    return in_order(jnp.concatenate(result, axis=0), own).reshape(carry_in.shape)


def solution(mesh):
    modes, ranks = mesh.shape["mode"], mesh.shape["rank"]
    in_specs = (P("rank", "mode", None),) * 4 + (P("rank", None),)
    body = functools.partial(shards, modes, ranks)
    return jax.shard_map(body, mesh=mesh, in_specs=in_specs, out_specs=P("rank", None), check_vma=False)
```

time: 178 us -> 155 us (0.87)
  local copies, waits for them, and re-layouts: 17.6 us -> 6.01 us
  waiting for transfers between devices: 64.5 us -> 53.2 us
  starting transfers between devices: 29.1 us -> 34.3 us
  other arithmetic: 8.38 us -> 3.27 us
    ppermute x6 -> x5, waiting for transfers between devices: 21 us -> 14.1 us  [shift(): return lax.ppermute(x, 'rank', [(i, (i + d) % ranks) for i in range(ranks)])]
    gather x5 -> x1, local copies, waits for them, and re-layouts: 6.98 us -> 0.58 us  [in_order(): return jnp.take(x, own ^ jnp.arange(x.shape[0]), axis=0)]
    ppermute x22, waiting for transfers between devices: 43.5 us -> 39.1 us  [partner(): lax.ppermute(x, 'mode', [(i, i ^ distance << low) for i in range(count)])]
    slice x2, local copies, waits for them, and re-layouts: 4.28 us -> 0.14 us  [shards(): left_a, left_b = (sketch_slices[:early], sketch_slices[early:])]
    ppermute x22, starting transfers between devices: 22.5 us -> 26.6 us  [partner(): lax.ppermute(x, 'mode', [(i, i ^ distance << low) for i in range(count)])]
    select_n x8 -> x2, other arithmetic: 3.65 us -> 0.14 us  [in_order(): return jnp.take(x, own ^ jnp.arange(x.shape[0]), axis=0)]
    ppermute x6 -> x5, starting transfers between devices: 6.64 us -> 7.75 us  [shift(): return lax.ppermute(x, 'rank', [(i, (i + d) % ranks) for i in range(ranks)])]
    unnamed x16 -> x15, local copies, waits for them, and re-layouts: 3.53 us -> 4.2 us
  transfers between devices with their start and end apart: 28 -> 27, of which waited for: 20 -> 21; matrix products, arithmetic and copies ran while one was open for 12% -> 4% of each run, Pallas kernels for 26% -> 30%
where the time goes in v2:
time: 155 us; the launch traced here: 154 us
  Pallas kernels  57.2 us (37%)
  waiting for transfers between devices  53.2 us (34%)
  starting transfers between devices  34.3 us (22%)
  local copies, waits for them, and re-layouts  6.01 us (4%)
  other arithmetic  3.27 us (2%)
    ppermute x22, waiting for transfers between devices, partner(): lax.ppermute(x, 'mode', [(i, i ^ distance << low) for i in range(count)])  39.1 us
    ppermute x22, starting transfers between devices, partner(): lax.ppermute(x, 'mode', [(i, i ^ distance << low) for i in range(count)])  26.6 us
    pallas_call x1, Pallas kernels, first_step(): pl.pallas_call(functools.partial(first_kernel, ROWS, SLOTS), out_shape=(o...  24 us
    pallas_call x1, Pallas kernels, hidden(): pl.pallas_call(kernel, out_shape=(out, out), in_specs=[HBM] + ([VMEM] if...  20.8 us
    ppermute x5, waiting for transfers between devices, shift(): return lax.ppermute(x, 'rank', [(i, (i + d) % ranks) for i in range(ranks)])  14.1 us
    ppermute x5, starting transfers between devices, shift(): return lax.ppermute(x, 'rank', [(i, (i + d) % ranks) for i in range(ranks)])  7.75 us
    pallas_call x1, Pallas kernels, joined(): pl.pallas_call(functools.partial(joined_kernel, early), out_shape=out_sha...  4.68 us
    pallas_call x1, Pallas kernels, second_product(): pl.pallas_call(second_kernel, out_shape=out_shape(rows, columns, count),...  4.53 us
  transfers between devices with their start and end apart: 27, of which 21 were waited for; matrix products, arithmetic and copies ran while one was open for 4% of the time, Pallas kernels for 30%

profile of v2, /device:TPU:0, one launch (start us, length us, event | category | flops | bytes accessed | tf_op | source)
XLA Modules:
  0.0 154.3 jit_solution(9537938529108828054)
XLA Ops:
  0.0 0.9 constant_dynamic-slice_fusion
  0.9 3.0 %collective-permute-start = (f32[128,256]{1,0:T(8,128)S(1)}, f32[128,256]{1,0:T(8,128)S(1)}, u32[]{:S(2)}, u32[]{:S(2)}) collective-permute-start(f32[128,256]{1,0:T(8,128)S(1)} %constant_dynamic-slice_fusion), channel_id=1, source_target_pairs={{0,1},{1,0},{2,3},{3,2},{4,5},{5,4},{6,7},{7,6},{8,9},{9,8},{10,11... | collective-permute-start | bytes 393224 | tf_op jit(solution)/shard_map/ppermute | solution.py:329
  4.0 4.2 %collective-permute-done = f32[128,256]{1,0:T(8,128)S(1)} collective-permute-done((f32[128,256]{1,0:T(8,128)S(1)}, f32[128,256]{1,0:T(8,128)S(1)}, u32[]{:S(2)}, u32[]{:S(2)}) %collective-permute-start) | collective-permute-done | bytes 131104 | tf_op jit(solution)/shard_map/ppermute | solution.py:329
  8.3 2.0 %collective-permute-start.1 = (f32[1,128,256]{2,1,0:T(8,128)S(1)}, f32[1,128,256]{2,1,0:T(8,128)S(1)}, u32[]{:S(2)}, u32[]{:S(2)}) collective-permute-start(f32[1,128,256]{2,1,0:T(8,128)S(1)} %bitcast.18), channel_id=1, source_target_pairs={{0,4},{2,6},{4,0},{6,2},{8,12},{10,14},{12,8},{14,10},{16,20},{18,... | collective-permute-start | bytes 393224 | tf_op jit(solution)/shard_map/ppermute | solution.py:325
  10.3 2.9 %collective-permute-done.1 = f32[1,128,256]{2,1,0:T(8,128)S(1)} collective-permute-done((f32[1,128,256]{2,1,0:T(8,128)S(1)}, f32[1,128,256]{2,1,0:T(8,128)S(1)}, u32[]{:S(2)}, u32[]{:S(2)}) %collective-permute-start.1) | collective-permute-done | bytes 131104 | tf_op jit(solution)/shard_map/ppermute | solution.py:325
  13.4 2.8 %copy.8 = f32[128,16,256]{2,0,1:T(8,128)S(1)} copy(f32[128,16,256]{2,1,0:T(8,128)} %sketch_ref.3) | data formatting | bytes 4194304 | tf_op args[3]
  16.3 1.3 copy-done.2
  17.7 1.0 pad_maximum_fusion
  18.7 0.6 gather_fusion
  19.4 1.8 %fusion.2.carried_ref = f32[1024,256]{1,0:T(8,128)S(1)} fusion(s32[]{:T(128)S(6)} %select_n.42, f32[512,256]{1,0:T(8,128)S(1)} %bitcast_select_fusion, f32[512,256]{1,0:T(8,128)} %param.9), kind=kLoop, calls=%fused_computation.8 | loop fusion | flops 786432 | bytes 2097156 | tf_op jit(solution)/shard_map/jit(_roll_dynamic)/concatenate | solution.py:358
  21.3 24.0 %shard_map.55 = (bf16[16,512,256]{2,1,0:T(8,128)(2,1)S(1)}, bf16[16,512,256]{2,1,0:T(8,128)(2,1)S(1)}, f32[512,128]{1,0:T(8,128)S(1)}) custom-call(f32[512,16,1024]{2,1,0:T(8,128)} %core_hbm.2, f32[1024,256]{1,0:T(8,128)S(1)} %fusion.2.carried_ref, f32[128,16,256]{2,1,0:T(8,128)S(1)} %copy-done.1), custom_call_target="tpu_custom_call" | custom-call | flops 12884901888 | bytes 33554432 | tf_op jit(solution)/shard_map/pallas_call | solution.py:242
  45.3 7.1 %collective-permute-done.3.refs_0_ = f32[128,16,256]{2,1,0:T(8,128)S(1)} collective-permute-done((f32[128,16,256]{2,1,0:T(8,128)}, f32[128,16,256]{2,1,0:T(8,128)S(1)}, u32[]{:S(2)}, u32[]{:S(2)}) %collective-permute-start.3) | collective-permute-done | bytes 2097184 | tf_op jit(solution)/shard_map/ppermute | solution.py:329
  52.4 4.5 %shard_map.56 = f32[16,32,256]{2,1,0:T(8,128)S(1)} custom-call(s32[2]{0:T(128)S(1)} %pad_add_fusion.place_ref, bf16[16,512,256]{2,1,0:T(8,128)(2,1)S(1)} %get-tuple-element.17.high, bf16[16,512,256]{2,1,0:T(8,128)(2,1)S(1)} %get-tuple-element.18.low, f32[512,128]{1,0:T(8,128)S(1)} %get-tuple-element.19.own_ref, ...), custom_call_target="tpu_custom_call" | custom-call | flops 1610612736 | bytes 8388608 | tf_op jit(solution)/shard_map/pallas_call | solution.py:260
  57.0 1.5 collective-permute-done.4
  58.6 1.8 %collective-permute-start.5 = (f32[4,32,256]{2,1,0:T(8,128)S(1)}, f32[4,32,256]{2,1,0:T(8,128)S(1)}, u32[]{:S(2)}, u32[]{:S(2)}) collective-permute-start(f32[4,32,256]{2,1,0:T(8,128)S(1)} %slice.78), channel_id=1, source_target_pairs={{0,4},{2,6},{4,0},{6,2},{8,12},{10,14},{12,8},{14,10},{16,20},{18,... | collective-permute-start | bytes 393224 | tf_op jit(solution)/shard_map/ppermute | solution.py:325
  60.4 1.5 collective-permute-start.9
  61.9 2.3 %collective-permute-done.5 = f32[4,32,256]{2,1,0:T(8,128)S(1)} collective-permute-done((f32[4,32,256]{2,1,0:T(8,128)S(1)}, f32[4,32,256]{2,1,0:T(8,128)S(1)}, u32[]{:S(2)}, u32[]{:S(2)}) %collective-permute-start.5) | collective-permute-done | bytes 131104 | tf_op jit(solution)/shard_map/ppermute | solution.py:325
  64.3 1.9 %collective-permute-start.6 = (f32[1,32,256]{2,1,0:T(8,128)S(1)}, f32[1,32,256]{2,1,0:T(8,128)S(1)}, u32[]{:S(2)}, u32[]{:S(2)}) collective-permute-start(f32[1,32,256]{2,1,0:T(8,128)S(1)} %get-tuple-element.34), channel_id=1, source_target_pairs={{0,8},{2,10},{4,12},{6,14},{8,0},{10,2},{12,4},{14,6},{16,24},{18,... | collective-permute-start | bytes 98312 | tf_op jit(solution)/shard_map/ppermute | solution.py:325
  66.1 2.6 %collective-permute-start.7 = (f32[1,32,256]{2,1,0:T(8,128)S(1)}, f32[1,32,256]{2,1,0:T(8,128)S(1)}, u32[]{:S(2)}, u32[]{:S(2)}) collective-permute-start(f32[1,32,256]{2,1,0:T(8,128)S(1)} %get-tuple-element.36), channel_id=1, source_target_pairs={{0,16},{2,18},{4,20},{6,22},{8,24},{10,26},{12,28},{14,30},{16,0},... | collective-permute-start | bytes 98312 | tf_op jit(solution)/shard_map/ppermute | solution.py:325
  68.7 2.5 %collective-permute-done.7 = f32[1,32,256]{2,1,0:T(8,128)S(1)} collective-permute-done((f32[1,32,256]{2,1,0:T(8,128)S(1)}, f32[1,32,256]{2,1,0:T(8,128)S(1)}, u32[]{:S(2)}, u32[]{:S(2)}) %collective-permute-start.7) | collective-permute-done | bytes 32800 | tf_op jit(solution)/shard_map/ppermute | solution.py:325
  71.2 3.2 %collective-permute-done.8 = f32[1,32,256]{2,1,0:T(8,128)S(1)} collective-permute-done((f32[1,32,256]{2,1,0:T(8,128)S(1)}, f32[1,32,256]{2,1,0:T(8,128)S(1)}, u32[]{:S(2)}, u32[]{:S(2)}) %collective-permute-start.8) | collective-permute-done | bytes 32800 | tf_op jit(solution)/shard_map/ppermute | solution.py:325
  74.5 1.6 %collective-permute-start.10 = (f32[1,32,256]{2,1,0:T(8,128)S(1)}, f32[1,32,256]{2,1,0:T(8,128)S(1)}, u32[]{:S(2)}, u32[]{:S(2)}) collective-permute-start(f32[1,32,256]{2,1,0:T(8,128)S(1)} %fusion.6), channel_id=1, source_target_pairs={{0,1},{1,0},{2,3},{3,2},{4,5},{5,4},{6,7},{7,6},{8,9},{9,8},{10,11... | collective-permute-start | bytes 98312 | tf_op jit(solution)/shard_map/ppermute | solution.py:329
  76.2 2.6 %collective-permute-done.10 = f32[1,32,256]{2,1,0:T(8,128)S(1)} collective-permute-done((f32[1,32,256]{2,1,0:T(8,128)S(1)}, f32[1,32,256]{2,1,0:T(8,128)S(1)}, u32[]{:S(2)}, u32[]{:S(2)}) %collective-permute-start.10) | collective-permute-done | bytes 32800 | tf_op jit(solution)/shard_map/ppermute | solution.py:329
  78.8 1.5 collective-permute-start.16
  80.3 1.0 collective-permute-start.12
  81.2 3.4 %collective-permute-start.13 = (f32[1,2,32,256]{3,2,1,0:T(8,128)S(1)}, f32[1,2,32,256]{3,2,1,0:T(8,128)S(1)}, u32[]{:S(2)}, u32[]{:S(2)}) collective-permute-start(f32[1,2,32,256]{3,2,1,0:T(8,128)S(1)} %maximum_bitcast_fusion), channel_id=1, source_target_pairs={{0,24},{2,26},{4,28},{6,30},{8,16},{10,18},{12,20},{14,22},{16,8},... | collective-permute-start | bytes 196616 | tf_op jit(solution)/shard_map/ppermute | solution.py:325
  84.7 0.8 collective-permute-done.12
  85.5 2.1 %collective-permute-done.13 = f32[1,2,32,256]{3,2,1,0:T(8,128)S(1)} collective-permute-done((f32[1,2,32,256]{3,2,1,0:T(8,128)S(1)}, f32[1,2,32,256]{3,2,1,0:T(8,128)S(1)}, u32[]{:S(2)}, u32[]{:S(2)}) %collective-permute-start.13) | collective-permute-done | bytes 65568 | tf_op jit(solution)/shard_map/ppermute | solution.py:325
  87.6 1.6 %collective-permute-start.14 = (f32[4,2,32,256]{3,2,1,0:T(8,128)S(1)}, f32[4,2,32,256]{3,2,1,0:T(8,128)S(1)}, u32[]{:S(2)}, u32[]{:S(2)}) collective-permute-start(f32[4,2,32,256]{3,2,1,0:T(8,128)S(1)} %pad_maximum_fusion.2), channel_id=1, source_target_pairs={{0,4},{2,6},{4,0},{6,2},{8,12},{10,14},{12,8},{14,10},{16,20},{18,... | collective-permute-start | bytes 786440 | tf_op jit(solution)/shard_map/ppermute | solution.py:325
  89.2 4.9 %collective-permute-done.14 = f32[4,2,32,256]{3,2,1,0:T(8,128)S(1)} collective-permute-done((f32[4,2,32,256]{3,2,1,0:T(8,128)S(1)}, f32[4,2,32,256]{3,2,1,0:T(8,128)S(1)}, u32[]{:S(2)}, u32[]{:S(2)}) %collective-permute-start.14) | collective-permute-done | bytes 262176 | tf_op jit(solution)/shard_map/ppermute | solution.py:325
  94.2 1.1 shard_map.58.refs_0_
  95.4 0.6 collective-permute-done.15.refs_1_
  96.1 20.8 %shard_map.57 = (bf16[16,512,256]{2,1,0:T(8,128)(2,1)S(1)}, bf16[16,512,256]{2,1,0:T(8,128)(2,1)S(1)}) custom-call(f32[512,16,1024]{2,1,0:T(8,128)} %core_hbm.3, s32[2]{0:T(128)S(1)} %pad_add_fusion.place_ref, f32[8,2,32,256]{3,2,1,0:T(8,128)S(1)} %constant_dynamic-update-slice_fusion.refs_0_, f32[8,2,32,256]{3,2,1,0:T(8,128)S(1)} %collective-permute-done.15.refs_1_), custom_call_target="tpu_custom_call" | custom-call | flops 1 | bytes 1 | tf_op jit(solution)/shard_map/pallas_call | solution.py:223
  117.7 4.7 %shard_map.61 = f32[16,32,256]{2,1,0:T(8,128)S(1)} custom-call(s32[2]{0:T(128)S(1)} %pad_add_fusion.place_ref, bf16[16,512,256]{2,1,0:T(8,128)(2,1)S(1)} %get-tuple-element.25.high, bf16[16,512,256]{2,1,0:T(8,128)(2,1)S(1)} %get-tuple-element.26.low, bf16[16,256,256]{2,1,0:T(8,128)(2,1)S(1)} %shard_map.58.refs_0_, ...), custom_call_target="tpu_custom_call" | custom-call | flops 3221225472 | bytes 8388608 | tf_op jit(solution)/shard_map/pallas_call | solution.py:273
  122.5 1.5 collective-permute-done.17
  124.1 1.6 %collective-permute-start.18 = (f32[4,32,256]{2,1,0:T(8,128)S(1)}, f32[4,32,256]{2,1,0:T(8,128)S(1)}, u32[]{:S(2)}, u32[]{:S(2)}) collective-permute-start(f32[4,32,256]{2,1,0:T(8,128)S(1)} %slice.87), channel_id=1, source_target_pairs={{0,4},{2,6},{4,0},{6,2},{8,12},{10,14},{12,8},{14,10},{16,20},{18,... | collective-permute-start | bytes 393224 | tf_op jit(solution)/shard_map/ppermute | solution.py:325
  125.6 4.0 %collective-permute-done.18 = f32[4,32,256]{2,1,0:T(8,128)S(1)} collective-permute-done((f32[4,32,256]{2,1,0:T(8,128)S(1)}, f32[4,32,256]{2,1,0:T(8,128)S(1)}, u32[]{:S(2)}, u32[]{:S(2)}) %collective-permute-start.18) | collective-permute-done | bytes 131104 | tf_op jit(solution)/shard_map/ppermute | solution.py:325
  129.8 3.4 %collective-permute-start.20 = (f32[1,32,256]{2,1,0:T(8,128)S(1)}, f32[1,32,256]{2,1,0:T(8,128)S(1)}, u32[]{:S(2)}, u32[]{:S(2)}) collective-permute-start(f32[1,32,256]{2,1,0:T(8,128)S(1)} %get-tuple-element.33), channel_id=1, source_target_pairs={{0,16},{2,18},{4,20},{6,22},{8,24},{10,26},{12,28},{14,30},{16,0},... | collective-permute-start | bytes 98312 | tf_op jit(solution)/shard_map/ppermute | solution.py:325
  133.2 0.9 collective-permute-start.21
  134.2 0.9 collective-permute-done.20
  135.1 4.1 %collective-permute-done.21 = f32[1,32,256]{2,1,0:T(8,128)S(1)} collective-permute-done((f32[1,32,256]{2,1,0:T(8,128)S(1)}, f32[1,32,256]{2,1,0:T(8,128)S(1)}, u32[]{:S(2)}, u32[]{:S(2)}) %collective-permute-start.21) | collective-permute-done | bytes 32800 | tf_op jit(solution)/shard_map/ppermute | solution.py:325
  139.3 1.2 collective-permute-start.23
  140.5 3.2 %collective-permute-start.24 = (f32[1,32,256]{2,1,0:T(8,128)S(1)}, f32[1,32,256]{2,1,0:T(8,128)S(1)}, u32[]{:S(2)}, u32[]{:S(2)}) collective-permute-start(f32[1,32,256]{2,1,0:T(8,128)S(1)} %get-tuple-element.30), channel_id=1, source_target_pairs={{0,24},{2,26},{4,28},{6,30},{8,16},{10,18},{12,20},{14,22},{16,8},... | collective-permute-start | bytes 98312 | tf_op jit(solution)/shard_map/ppermute | solution.py:325
  144.2 2.0 %collective-permute-done.24 = f32[1,32,256]{2,1,0:T(8,128)S(1)} collective-permute-done((f32[1,32,256]{2,1,0:T(8,128)S(1)}, f32[1,32,256]{2,1,0:T(8,128)S(1)}, u32[]{:S(2)}, u32[]{:S(2)}) %collective-permute-start.24) | collective-permute-done | bytes 32800 | tf_op jit(solution)/shard_map/ppermute | solution.py:325
  146.3 1.6 %collective-permute-start.25 = (f32[4,32,256]{2,1,0:T(8,128)S(1)}, f32[4,32,256]{2,1,0:T(8,128)S(1)}, u32[]{:S(2)}, u32[]{:S(2)}) collective-permute-start(f32[4,32,256]{2,1,0:T(8,128)S(1)} %pad_maximum_fusion.3), channel_id=1, source_target_pairs={{0,4},{2,6},{4,0},{6,2},{8,12},{10,14},{12,8},{14,10},{16,20},{18,... | collective-permute-start | bytes 393224 | tf_op jit(solution)/shard_map/ppermute | solution.py:325
  147.8 3.5 %collective-permute-done.25 = f32[4,32,256]{2,1,0:T(8,128)S(1)} collective-permute-done((f32[4,32,256]{2,1,0:T(8,128)S(1)}, f32[4,32,256]{2,1,0:T(8,128)S(1)}, u32[]{:S(2)}, u32[]{:S(2)}) %collective-permute-start.25) | collective-permute-done | bytes 131104 | tf_op jit(solution)/shard_map/ppermute | solution.py:325
  151.4 1.5 collective-permute-done.26.refs_1_
  152.9 1.4 shard_map.62
  (60 shorter events, 2.8 us)
Async XLA Ops:
  0.9 7.4 %collective-permute-start = (f32[128,256]{1,0:T(8,128)S(1)}, f32[128,256]{1,0:T(8,128)S(1)}, u32[]{:S(2)}, u32[]{:S(2)}) collective-permute-start(f32[128,256]{1,0:T(8,128)S(1)} %constant_dynamic-slice_fusion), channel_id=1, source_target_pairs={{0,1},{1,0},{2,3},{3,2},{4,5},{5,4},{6,7},{7,6},{8,9},{9,8},{10,11... | collective-permute-start | bytes 393224 | tf_op jit(solution)/shard_map/ppermute | solution.py:329
  3.9 48.4 %collective-permute-start.3 = (f32[128,16,256]{2,1,0:T(8,128)}, f32[128,16,256]{2,1,0:T(8,128)S(1)}, u32[]{:S(2)}, u32[]{:S(2)}) collective-permute-start(f32[128,16,256]{2,1,0:T(8,128)} %sketch_ref.2), channel_id=1, source_target_pairs={{0,1},{1,0},{2,3},{3,2},{4,5},{5,4},{6,7},{7,6},{8,9},{9,8},{10,11... | collective-permute-start | bytes 6291464 | tf_op jit(solution)/shard_map/ppermute | solution.py:329
  8.3 5.0 %collective-permute-start.1 = (f32[1,128,256]{2,1,0:T(8,128)S(1)}, f32[1,128,256]{2,1,0:T(8,128)S(1)}, u32[]{:S(2)}, u32[]{:S(2)}) collective-permute-start(f32[1,128,256]{2,1,0:T(8,128)S(1)} %bitcast.18), channel_id=1, source_target_pairs={{0,4},{2,6},{4,0},{6,2},{8,12},{10,14},{12,8},{14,10},{16,20},{18,... | collective-permute-start | bytes 393224 | tf_op jit(solution)/shard_map/ppermute | solution.py:325
  13.3 4.4 %collective-permute-start.2 = (f32[2,128,256]{2,1,0:T(8,128)S(1)}, f32[2,128,256]{2,1,0:T(8,128)}, u32[]{:S(2)}, u32[]{:S(2)}) collective-permute-start(f32[2,128,256]{2,1,0:T(8,128)S(1)} %pad_maximum_fusion.1), channel_id=1, source_target_pairs={{0,2},{2,0},{4,6},{6,4},{8,10},{10,8},{12,14},{14,12},{16,18},{18,... | collective-permute-start | bytes 786440 | tf_op jit(solution)/shard_map/ppermute | solution.py:325
  16.2 1.3 copy-start.2
  19.3 2.0 %copy-start.1 = (f32[128,16,256]{2,1,0:T(8,128)S(1)}, f32[128,16,256]{2,1,0:T(8,128)}, u32[]{:S(2)}) copy-start(f32[128,16,256]{2,1,0:T(8,128)} %sketch_ref.2) | copy-start | bytes 6291460
  56.9 19.1 %copy-start.3 = (f32[128,16,256]{2,0,1:T(8,128)S(1)}, f32[128,16,256]{2,0,1:T(8,128)}, u32[]{:S(2)}) copy-start(f32[128,16,256]{2,0,1:T(8,128)} %copy-done.2) | copy-start | bytes 6291460
  57.0 1.6 %collective-permute-start.4 = (f32[8,32,256]{2,1,0:T(8,128)S(1)}, f32[8,32,256]{2,1,0:T(8,128)S(1)}, u32[]{:S(2)}, u32[]{:S(2)}) collective-permute-start(f32[8,32,256]{2,1,0:T(8,128)S(1)} %slice.76), channel_id=1, source_target_pairs={{0,2},{2,0},{4,6},{6,4},{8,10},{10,8},{12,14},{14,12},{16,18},{18,... | collective-permute-start | bytes 786440 | tf_op jit(solution)/shard_map/ppermute | solution.py:325
  58.6 5.6 %collective-permute-start.5 = (f32[4,32,256]{2,1,0:T(8,128)S(1)}, f32[4,32,256]{2,1,0:T(8,128)S(1)}, u32[]{:S(2)}, u32[]{:S(2)}) collective-permute-start(f32[4,32,256]{2,1,0:T(8,128)S(1)} %slice.78), channel_id=1, source_target_pairs={{0,4},{2,6},{4,0},{6,2},{8,12},{10,14},{12,8},{14,10},{16,20},{18,... | collective-permute-start | bytes 393224 | tf_op jit(solution)/shard_map/ppermute | solution.py:325
  60.4 14.1 %collective-permute-start.9 = (f32[2,128,256]{2,1,0:T(8,128)S(1)}, f32[2,128,256]{2,1,0:T(8,128)S(1)}, u32[]{:S(2)}, u32[]{:S(2)}) collective-permute-start(f32[2,128,256]{2,1,0:T(8,128)S(1)} %slice.74), channel_id=1, source_target_pairs={{0,1},{1,0},{2,3},{3,2},{4,5},{5,4},{6,7},{7,6},{8,9},{9,8},{10,11... | collective-permute-start | bytes 786440 | tf_op jit(solution)/shard_map/ppermute | solution.py:329
  64.3 4.5 %collective-permute-start.6 = (f32[1,32,256]{2,1,0:T(8,128)S(1)}, f32[1,32,256]{2,1,0:T(8,128)S(1)}, u32[]{:S(2)}, u32[]{:S(2)}) collective-permute-start(f32[1,32,256]{2,1,0:T(8,128)S(1)} %get-tuple-element.34), channel_id=1, source_target_pairs={{0,8},{2,10},{4,12},{6,14},{8,0},{10,2},{12,4},{14,6},{16,24},{18,... | collective-permute-start | bytes 98312 | tf_op jit(solution)/shard_map/ppermute | solution.py:325
  66.1 5.1 %collective-permute-start.7 = (f32[1,32,256]{2,1,0:T(8,128)S(1)}, f32[1,32,256]{2,1,0:T(8,128)S(1)}, u32[]{:S(2)}, u32[]{:S(2)}) collective-permute-start(f32[1,32,256]{2,1,0:T(8,128)S(1)} %get-tuple-element.36), channel_id=1, source_target_pairs={{0,16},{2,18},{4,20},{6,22},{8,24},{10,26},{12,28},{14,30},{16,0},... | collective-permute-start | bytes 98312 | tf_op jit(solution)/shard_map/ppermute | solution.py:325
  68.7 5.7 %collective-permute-start.8 = (f32[1,32,256]{2,1,0:T(8,128)S(1)}, f32[1,32,256]{2,1,0:T(8,128)S(1)}, u32[]{:S(2)}, u32[]{:S(2)}) collective-permute-start(f32[1,32,256]{2,1,0:T(8,128)S(1)} %get-tuple-element.35), channel_id=1, source_target_pairs={{0,24},{2,26},{4,28},{6,30},{8,16},{10,18},{12,20},{14,22},{16,8},... | collective-permute-start | bytes 98312 | tf_op jit(solution)/shard_map/ppermute | solution.py:325
  74.4 19.7 %copy-start = (f32[128,16,256]{2,1,0:T(8,128)S(1)}, f32[128,16,256]{2,1,0:T(8,128)}, u32[]{:S(2)}) copy-start(f32[128,16,256]{2,1,0:T(8,128)} %sketch_ref.3) | copy-start | bytes 6291460
  74.5 4.3 %collective-permute-start.10 = (f32[1,32,256]{2,1,0:T(8,128)S(1)}, f32[1,32,256]{2,1,0:T(8,128)S(1)}, u32[]{:S(2)}, u32[]{:S(2)}) collective-permute-start(f32[1,32,256]{2,1,0:T(8,128)S(1)} %fusion.6), channel_id=1, source_target_pairs={{0,1},{1,0},{2,3},{3,2},{4,5},{5,4},{6,7},{7,6},{8,9},{9,8},{10,11... | collective-permute-start | bytes 98312 | tf_op jit(solution)/shard_map/ppermute | solution.py:329
  78.8 38.4 %collective-permute-start.16 = (f32[14,128,256]{2,1,0:T(8,128)S(1)}, f32[14,128,256]{2,1,0:T(8,128)S(1)}, u32[]{:S(2)}, u32[]{:S(2)}) collective-permute-start(f32[14,128,256]{2,1,0:T(8,128)S(1)} %slice.83), channel_id=1, source_target_pairs={{0,1},{1,0},{2,3},{3,2},{4,5},{5,4},{6,7},{7,6},{8,9},{9,8},{10,11... | collective-permute-start | bytes 5505032 | tf_op jit(solution)/shard_map/ppermute | solution.py:329
  80.3 4.4 %collective-permute-start.11 = (f32[1,2,32,256]{3,2,1,0:T(8,128)S(1)}, f32[1,2,32,256]{3,2,1,0:T(8,128)S(1)}, u32[]{:S(2)}, u32[]{:S(2)}) collective-permute-start(f32[1,2,32,256]{3,2,1,0:T(8,128)S(1)} %maximum_bitcast_fusion), channel_id=1, source_target_pairs={{0,8},{2,10},{4,12},{6,14},{8,0},{10,2},{12,4},{14,6},{16,24},{18,... | collective-permute-start | bytes 196616 | tf_op jit(solution)/shard_map/ppermute | solution.py:325
  80.3 5.2 %collective-permute-start.12 = (f32[1,2,32,256]{3,2,1,0:T(8,128)S(1)}, f32[1,2,32,256]{3,2,1,0:T(8,128)S(1)}, u32[]{:S(2)}, u32[]{:S(2)}) collective-permute-start(f32[1,2,32,256]{3,2,1,0:T(8,128)S(1)} %maximum_bitcast_fusion), channel_id=1, source_target_pairs={{0,16},{2,18},{4,20},{6,22},{8,24},{10,26},{12,28},{14,30},{16,0},... | collective-permute-start | bytes 196616 | tf_op jit(solution)/shard_map/ppermute | solution.py:325
  81.2 6.4 %collective-permute-start.13 = (f32[1,2,32,256]{3,2,1,0:T(8,128)S(1)}, f32[1,2,32,256]{3,2,1,0:T(8,128)S(1)}, u32[]{:S(2)}, u32[]{:S(2)}) collective-permute-start(f32[1,2,32,256]{3,2,1,0:T(8,128)S(1)} %maximum_bitcast_fusion), channel_id=1, source_target_pairs={{0,24},{2,26},{4,28},{6,30},{8,16},{10,18},{12,20},{14,22},{16,8},... | collective-permute-start | bytes 196616 | tf_op jit(solution)/shard_map/ppermute | solution.py:325
  87.6 6.4 %collective-permute-start.14 = (f32[4,2,32,256]{3,2,1,0:T(8,128)S(1)}, f32[4,2,32,256]{3,2,1,0:T(8,128)S(1)}, u32[]{:S(2)}, u32[]{:S(2)}) collective-permute-start(f32[4,2,32,256]{3,2,1,0:T(8,128)S(1)} %pad_maximum_fusion.2), channel_id=1, source_target_pairs={{0,4},{2,6},{4,0},{6,2},{8,12},{10,14},{12,8},{14,10},{16,20},{18,... | collective-permute-start | bytes 786440 | tf_op jit(solution)/shard_map/ppermute | solution.py:325
  94.1 2.0 %collective-permute-start.15 = (f32[8,2,32,256]{3,2,1,0:T(8,128)S(1)}, f32[8,2,32,256]{3,2,1,0:T(8,128)S(1)}, u32[]{:S(2)}, u32[]{:S(2)}) collective-permute-start(f32[8,2,32,256]{3,2,1,0:T(8,128)S(1)} %constant_dynamic-update-slice_fusion.refs_0_), channel_id=1, source_target_pairs={{0,2},{2,0},{4,6},{6,4},{8,10},{10,8},{12,14},{14,12},{16,18},{18,... | collective-permute-start | bytes 1572872 | tf_op jit(solution)/shard_map/ppermute | solution.py:325
  122.4 1.6 %collective-permute-start.17 = (f32[8,32,256]{2,1,0:T(8,128)S(1)}, f32[8,32,256]{2,1,0:T(8,128)S(1)}, u32[]{:S(2)}, u32[]{:S(2)}) collective-permute-start(f32[8,32,256]{2,1,0:T(8,128)S(1)} %slice.85), channel_id=1, source_target_pairs={{0,2},{2,0},{4,6},{6,4},{8,10},{10,8},{12,14},{14,12},{16,18},{18,... | collective-permute-start | bytes 786440 | tf_op jit(solution)/shard_map/ppermute | solution.py:325
  124.1 5.6 %collective-permute-start.18 = (f32[4,32,256]{2,1,0:T(8,128)S(1)}, f32[4,32,256]{2,1,0:T(8,128)S(1)}, u32[]{:S(2)}, u32[]{:S(2)}) collective-permute-start(f32[4,32,256]{2,1,0:T(8,128)S(1)} %slice.87), channel_id=1, source_target_pairs={{0,4},{2,6},{4,0},{6,2},{8,12},{10,14},{12,8},{14,10},{16,20},{18,... | collective-permute-start | bytes 393224 | tf_op jit(solution)/shard_map/ppermute | solution.py:325
  129.7 4.5 %collective-permute-start.19 = (f32[1,32,256]{2,1,0:T(8,128)S(1)}, f32[1,32,256]{2,1,0:T(8,128)S(1)}, u32[]{:S(2)}, u32[]{:S(2)}) collective-permute-start(f32[1,32,256]{2,1,0:T(8,128)S(1)} %get-tuple-element.31), channel_id=1, source_target_pairs={{0,8},{2,10},{4,12},{6,14},{8,0},{10,2},{12,4},{14,6},{16,24},{18,... | collective-permute-start | bytes 98312 | tf_op jit(solution)/shard_map/ppermute | solution.py:325
  129.8 5.3 %collective-permute-start.20 = (f32[1,32,256]{2,1,0:T(8,128)S(1)}, f32[1,32,256]{2,1,0:T(8,128)S(1)}, u32[]{:S(2)}, u32[]{:S(2)}) collective-permute-start(f32[1,32,256]{2,1,0:T(8,128)S(1)} %get-tuple-element.33), channel_id=1, source_target_pairs={{0,16},{2,18},{4,20},{6,22},{8,24},{10,26},{12,28},{14,30},{16,0},... | collective-permute-start | bytes 98312 | tf_op jit(solution)/shard_map/ppermute | solution.py:325
  133.2 6.0 %collective-permute-start.21 = (f32[1,32,256]{2,1,0:T(8,128)S(1)}, f32[1,32,256]{2,1,0:T(8,128)S(1)}, u32[]{:S(2)}, u32[]{:S(2)}) collective-permute-start(f32[1,32,256]{2,1,0:T(8,128)S(1)} %get-tuple-element.32), channel_id=1, source_target_pairs={{0,24},{2,26},{4,28},{6,30},{8,16},{10,18},{12,20},{14,22},{16,8},... | collective-permute-start | bytes 98312 | tf_op jit(solution)/shard_map/ppermute | solution.py:325
  139.2 4.5 %collective-permute-start.22 = (f32[1,32,256]{2,1,0:T(8,128)S(1)}, f32[1,32,256]{2,1,0:T(8,128)S(1)}, u32[]{:S(2)}, u32[]{:S(2)}) collective-permute-start(f32[1,32,256]{2,1,0:T(8,128)S(1)} %get-tuple-element.30), channel_id=1, source_target_pairs={{0,8},{2,10},{4,12},{6,14},{8,0},{10,2},{12,4},{14,6},{16,24},{18,... | collective-permute-start | bytes 98312 | tf_op jit(solution)/shard_map/ppermute | solution.py:325
  139.3 4.9 %collective-permute-start.23 = (f32[1,32,256]{2,1,0:T(8,128)S(1)}, f32[1,32,256]{2,1,0:T(8,128)S(1)}, u32[]{:S(2)}, u32[]{:S(2)}) collective-permute-start(f32[1,32,256]{2,1,0:T(8,128)S(1)} %get-tuple-element.30), channel_id=1, source_target_pairs={{0,16},{2,18},{4,20},{6,22},{8,24},{10,26},{12,28},{14,30},{16,0},... | collective-permute-start | bytes 98312 | tf_op jit(solution)/shard_map/ppermute | solution.py:325
  140.5 5.7 %collective-permute-start.24 = (f32[1,32,256]{2,1,0:T(8,128)S(1)}, f32[1,32,256]{2,1,0:T(8,128)S(1)}, u32[]{:S(2)}, u32[]{:S(2)}) collective-permute-start(f32[1,32,256]{2,1,0:T(8,128)S(1)} %get-tuple-element.30), channel_id=1, source_target_pairs={{0,24},{2,26},{4,28},{6,30},{8,16},{10,18},{12,20},{14,22},{16,8},... | collective-permute-start | bytes 98312 | tf_op jit(solution)/shard_map/ppermute | solution.py:325
  146.3 5.0 %collective-permute-start.25 = (f32[4,32,256]{2,1,0:T(8,128)S(1)}, f32[4,32,256]{2,1,0:T(8,128)S(1)}, u32[]{:S(2)}, u32[]{:S(2)}) collective-permute-start(f32[4,32,256]{2,1,0:T(8,128)S(1)} %pad_maximum_fusion.3), channel_id=1, source_target_pairs={{0,4},{2,6},{4,0},{6,2},{8,12},{10,14},{12,8},{14,10},{16,20},{18,... | collective-permute-start | bytes 393224 | tf_op jit(solution)/shard_map/ppermute | solution.py:325
  151.3 1.6 %collective-permute-start.26 = (f32[8,32,256]{2,1,0:T(8,128)S(1)}, f32[8,32,256]{2,1,0:T(8,128)S(1)}, u32[]{:S(2)}, u32[]{:S(2)}) collective-permute-start(f32[8,32,256]{2,1,0:T(8,128)S(1)} %constant_dynamic-update-slice_fusion.5.refs_0_), channel_id=1, source_target_pairs={{0,2},{2,0},{4,6},{6,4},{8,10},{10,8},{12,14},{14,12},{16,18},{18,... | collective-permute-start | bytes 786440 | tf_op jit(solution)/shard_map/ppermute | solution.py:325

commit v3 on v2

--- a/solution.py
+++ b/solution.py
@@ -31,35 +31,36 @@
         out_ref[i, :, size:] = low
 
 
-def hidden_loop(rows, slots, core_hbm, spread, high, low, buf, sems, weights, tile):
-    count, slices, depth = core_hbm.shape
-    columns = high.shape[2]
-    steps = count // rows
-
-    def copy(k):
+def hidden_loop(core_hbm, spread, high, low, buf, sems, weights):
+    rows, slices, _ = core_hbm.shape
+    slots, width = buf.shape[0], buf.shape[1] // rows
+    steps = slices // width
+
+    def copies(k):
         slot = lax.rem(k, slots)
-        return pltpu.make_async_copy(core_hbm.at[pl.ds(k * rows, rows)], buf.at[slot], sems.at[slot])
+        return [
+            pltpu.make_async_copy(core_hbm.at[:, k * width + u, :], buf.at[slot, pl.ds(u * rows, rows)], sems.at[slot, u])
+            for u in range(width)
+        ]
 
     for k in range(min(slots - 1, steps)):
-        copy(k).start()
+        for copy in copies(k):
+            copy.start()
     spread(weights)
 
     def block(k, _):
         @pl.when(k + slots - 1 < steps)
         def _():
-            copy(k + slots - 1).start()
-
-        copy(k).wait()
-        h, l = halves(buf[lax.rem(k, slots)].reshape(rows * slices, depth))
-        result = dot(jnp.concatenate([h, h, l], axis=1), weights[...])
-        for j in range(columns // LANES):
-            tile[j] = result[:, j * LANES : (j + 1) * LANES]
-        at = pl.ds(pl.multiple_of(k * rows, rows), rows)
-        for i in range(slices):
-            for j in range(columns // LANES):
-                h, l = halves(tile[j, pl.ds(i, rows, stride=slices), :])
-                high[i, at, j * LANES : (j + 1) * LANES] = h
-                low[i, at, j * LANES : (j + 1) * LANES] = l
+            for copy in copies(k + slots - 1):
+                copy.start()
+
+        for copy in copies(k):
+            copy.wait()
+        h, l = halves(buf[lax.rem(k, slots)])
+        h, l = halves(dot(jnp.concatenate([h, h, l], axis=1), weights[...]))
+        for u in range(width):
+            high[k * width + u] = h[u * rows : (u + 1) * rows]
+            low[k * width + u] = l[u * rows : (u + 1) * rows]
         return 0
 
     lax.fori_loop(0, steps, block, 0)
@@ -73,15 +74,15 @@
     weights[2 * depth :] = h
 
 
-def first_kernel(rows, slots, core_hbm, carried_ref, sketch_ref, high, low, out, prepared, *scratch):
-    hidden_loop(rows, slots, core_hbm, functools.partial(spread_whole, carried_ref), high, low, *scratch)
+def first_kernel(core_hbm, carried_ref, sketch_ref, high, low, out, prepared, *scratch):
+    hidden_loop(core_hbm, functools.partial(spread_whole, carried_ref), high, low, *scratch)
     prepare_kernel(sketch_ref, prepared)
     out[...] = jnp.zeros_like(out)
-    multiply(0, sketch_ref.shape[1], high, low, [(prepared, 0)], out)
-
-
-def hidden_kernel(rows, slots, core_hbm, carried_ref, high, low, *scratch):
-    hidden_loop(rows, slots, core_hbm, functools.partial(spread_whole, carried_ref), high, low, *scratch)
+    multiply(high, low, [[prepared]], out)
+
+
+def hidden_kernel(core_hbm, carried_ref, high, low, *scratch):
+    hidden_loop(core_hbm, functools.partial(spread_whole, carried_ref), high, low, *scratch)
 
 
 def spread_pieces(ranks, place_ref, parts, weights):
@@ -103,33 +104,25 @@
             position += 1
 
 
-def hidden_of_pieces_kernel(rows, slots, ranks, core_hbm, place_ref, *refs):
-    parts, scratch = refs[:-6], refs[-6:]
-    hidden_loop(rows, slots, core_hbm, functools.partial(spread_pieces, ranks, place_ref, parts), *scratch)
-
-
-def multiply(first, count, high, low, sketches, out):
-    def add(start, size):
-        slices = range(size)
-        h = jnp.concatenate([high[first + start + t] for t in slices], axis=1)
-        l = jnp.concatenate([low[first + start + t] for t in slices], axis=1)
+def hidden_of_pieces_kernel(ranks, core_hbm, place_ref, *refs):
+    parts, scratch = refs[:-5], refs[-5:]
+    hidden_loop(core_hbm, functools.partial(spread_pieces, ranks, place_ref, parts), *scratch)
+
+
+def multiply(high, low, sketches, out):
+    where = [[(ref, i) for ref in refs for i in range(ref.shape[0])] for refs in sketches]
+    for start in range(0, high.shape[0], GROUP):
+        slices = range(start, min(start + GROUP, high.shape[0]))
+        h = jnp.concatenate([high[i] for i in slices], axis=1)
+        l = jnp.concatenate([low[i] for i in slices], axis=1)
         sums, highs = [], []
-        for s, at in sketches:
-            both = jnp.concatenate([s[at + start + t] for t in slices], axis=0)
+        for places in where:
+            both = jnp.concatenate([places[i][0][places[i][1]] for i in slices], axis=0)
             width = both.shape[1] // 2
             result = dot(h, both)
             sums.append(result[:, :width] + result[:, width:])
             highs.append(both[:, :width])
         out[...] += jnp.concatenate(sums, axis=1) + dot(l, jnp.concatenate(highs, axis=1))
-
-    def body(g, _):
-        add(g * GROUP, GROUP)
-        return 0
-
-    whole = count // GROUP
-    lax.fori_loop(0, whole, body, 0)
-    if count % GROUP:
-        add(whole * GROUP, count % GROUP)
 
 
 def store(place_ref, acc, out):
@@ -149,26 +142,14 @@
         at = slice((d + 1) * width, (d + 2) * width)
         acc[:, at] = jnp.zeros_like(own_ref)
         prepare_kernel(sketch, prepared)
-        multiply(0, sketch.shape[1], high, low, [(prepared, 0)], acc.at[:, at])
+        multiply(high, low, [[prepared]], acc.at[:, at])
     store(place_ref, acc, out)
 
 
-def joined_kernel(early, place_ref, high, low, *refs):
-    sketches, (out, acc) = refs[:-2], refs[-2:]
+def joined_kernel(counts, place_ref, high, low, *refs):
+    chunks, (out, acc) = list(refs[:-2]), refs[-2:]
     acc[...] = jnp.zeros_like(acc)
-    slices = high.shape[0]
-    firsts, rests, at = [], [], 0
-    while at < len(sketches):
-        if sketches[at].shape[0] == slices:
-            firsts.append((sketches[at], 0))
-            rests.append((sketches[at], early))
-            at += 1
-        else:
-            firsts.append((sketches[at], 0))
-            rests.append((sketches[at + 1], 0))
-            at += 2
-    multiply(0, early, high, low, firsts, acc)
-    multiply(early, slices - early, high, low, rests, acc)
+    multiply(high, low, [[chunks.pop(0) for _ in range(count)] for count in counts], acc)
     store(place_ref, acc, out)
 
 
@@ -190,13 +171,13 @@
     return (core.shape[1], core.shape[0], columns)
 
 
-def loop_scratch(core, columns, rows, slots):
-    _, slices, depth = core.shape
+def loop_scratch(core, columns):
+    rows, slices, depth = core.shape
+    width = 2 - slices % 2
     return [
-        pltpu.VMEM((slots, rows, slices, depth), F32),
-        pltpu.SemaphoreType.DMA((slots,)),
+        pltpu.VMEM((SLOTS, width * rows, depth), F32),
+        pltpu.SemaphoreType.DMA((SLOTS, width)),
         pltpu.VMEM((3 * depth, columns), BF16),
-        pltpu.VMEM((columns // LANES, rows * slices, LANES), F32),
     ]
 
 
@@ -204,7 +185,7 @@
     return pltpu.CompilerParams(vmem_limit_bytes=mib << 20)
 
 
-ROWS, SLOTS, GROUP = 64, 3, 4
+SLOTS, GROUP = 3, 8
 
 
 def cost(flops, size):
@@ -216,16 +197,16 @@
     columns = (carried if place is None else carried[0]).shape[-1]
     out = jax.ShapeDtypeStruct(hidden_shape(core, columns), BF16)
     if place is None:
-        kernel, operands = functools.partial(hidden_kernel, ROWS, SLOTS), (carried,)
+        kernel, operands = hidden_kernel, (carried,)
     else:
         ranks = carried[0].shape[1]
-        kernel, operands = functools.partial(hidden_of_pieces_kernel, ROWS, SLOTS, ranks), (place, *carried)
+        kernel, operands = functools.partial(hidden_of_pieces_kernel, ranks), (place, *carried)
     return pl.pallas_call(
         kernel,
         out_shape=(out, out),
         in_specs=[HBM] + ([VMEM] if place is None else [SMEM] + [VMEM] * len(carried)),
         out_specs=(VMEM, VMEM),
-        scratch_shapes=loop_scratch(core, columns, ROWS, SLOTS),
+        scratch_shapes=loop_scratch(core, columns),
         compiler_params=limit(32),
         cost_estimate=cost(6 * count * slices * depth * columns, 4 * core.size) if place is None else cost(1, 1),
     )(core, *operands)
@@ -240,11 +221,11 @@
     columns = carried.shape[1]
     out = jax.ShapeDtypeStruct(hidden_shape(core, columns), BF16)
     return pl.pallas_call(
-        functools.partial(first_kernel, ROWS, SLOTS),
+        first_kernel,
         out_shape=(out, out, jax.ShapeDtypeStruct((core.shape[0], size), F32)),
         in_specs=[HBM, VMEM, VMEM],
         out_specs=(VMEM,) * 3,
-        scratch_shapes=[pltpu.VMEM((slices, depth, 2 * size), BF16)] + loop_scratch(core, columns, ROWS, SLOTS),
+        scratch_shapes=[pltpu.VMEM((slices, depth, 2 * size), BF16)] + loop_scratch(core, columns),
         compiler_params=limit(36),
         cost_estimate=cost(6 * core.size * columns, 4 * core.size),
     )(core, carried, sketch)
@@ -268,10 +249,10 @@
     )(place, high, low, own, *sketches)
 
 
-def joined(place, high, low, early, chunks, columns, count):
+def joined(place, high, low, counts, chunks, columns, count):
     rows = high.shape[1]
     return pl.pallas_call(
-        functools.partial(joined_kernel, early),
+        functools.partial(joined_kernel, counts),
         out_shape=out_shape(rows, columns, count),
         in_specs=[SMEM] + [VMEM] * (2 + len(chunks)),
         out_specs=VMEM,
@@ -314,15 +295,20 @@
     return groups
 
 
+def far_first(digit, width):
+    return digit ^ ((digit & 1) << 1) if width == 2 else digit
+
+
 def piece_of(index, groups):
     piece = 0
     for low, width in groups:
-        piece = (piece << width) | ((index >> low) & ((1 << width) - 1))
+        piece = (piece << width) | far_first((index >> low) & ((1 << width) - 1), width)
     return piece
 
 
-def partner(x, count, low, distance):
-    return lax.ppermute(x, "mode", [(i, i ^ (distance << low)) for i in range(count)])
+def partner(x, count, low, width, position):
+    distance = far_first(position, width) << low
+    return lax.ppermute(x, "mode", [(i, i ^ distance) for i in range(count)])
 
 
 def shift(x, ranks, d):
@@ -332,7 +318,7 @@
 def reduce_scatter(x, count, groups):
     for low, width in groups:
         size = x.shape[0] >> width
-        arrived = [partner(x[d * size : (d + 1) * size], count, low, d) for d in range(1, 1 << width)]
+        arrived = [partner(x[d * size : (d + 1) * size], count, low, width, d) for d in range(1, 1 << width)]
         x = sum(arrived, x[:size])
     return x
 
@@ -341,7 +327,7 @@
     parts = [x]
     for low, width in reversed(groups):
         x = jnp.concatenate(parts, axis=0)
-        parts = [x] + [partner(x, count, low, d) for d in range(1, 1 << width)]
+        parts = [x] + [partner(x, count, low, width, d) for d in range(1, 1 << width)]
     return parts
 
 
@@ -377,7 +363,7 @@
     own = piece_of(mode, groups)
     place = jnp.stack([own, rank])
     slices, size = core_right.shape[1], sketch_right.shape[0]
-    early = max(1, slices // 8)
+    early = max(1, slices // 4)
     count = modes if carry_in.shape[0] % (16 * modes) == 0 and size % LANES == 0 else 0
 
     def shifted(x):
@@ -413,13 +399,14 @@
         high, low = hidden(core_left, jnp.swapaxes(both, 0, 1).reshape(carried.shape))
 
     if count:
-        chunks = [prepare(sketch_left)]
+        chunks, counts = [prepare(sketch_left)], [1]
         for pair in zip(left_a_arrived, left_b_arrived):
             chunks += [prepare(x, 0) for x in pair]
+            counts.append(2)
     else:
         whole = [jnp.concatenate(pair) for pair in zip(left_a_arrived, left_b_arrived)]
-        chunks = [prepare(jnp.concatenate([sketch_slices] + whole, axis=1), 0)]
-    term = joined(place, high, low, early, chunks, size * ranks, count)
+        chunks, counts = [prepare(jnp.concatenate([sketch_slices] + whole, axis=1), 0)], [1]
+    term = joined(place, high, low, counts, chunks, size * ranks, count)
     result = all_gather_parts(scattered(term), modes, groups)
     if count:
         return settle(place, result, ranks)

time: 155 us -> 148 us (0.955)
  Pallas kernels: 57.2 us -> 48.8 us
  waiting for transfers between devices: 53.2 us -> 58 us
  starting transfers between devices: 34.3 us -> 31.6 us
    ppermute x5, waiting for transfers between devices: 14.1 us -> 18.8 us  [shift(): return lax.ppermute(x, 'rank', [(i, (i + d) % ranks) for i in range(ranks)])]
    pallas_call x2, Pallas kernels: 28.7 us -> 24.1 us  [the longest x1 20.1 us: first_step(): pl.pallas_call(first_kernel, out_shape=(out, out, jax.ShapeDtypeStruct((c...]
    pallas_call x1, Pallas kernels: 20.8 us -> 18.1 us  [hidden(): pl.pallas_call(kernel, out_shape=(out, out), in_specs=[HBM] + ([VMEM] if...]
    ppermute x22, starting transfers between devices: 26.6 us -> 23.9 us  [partner(): return lax.ppermute(x, 'mode', [(i, i ^ distance) for i in range(count)])]
    unnamed x15 -> x17, local copies, waits for them, and re-layouts: 4.2 us -> 4.19 us
  transfers between devices with their start and end apart: 27 -> 27, of which waited for: 21 -> 23; matrix products, arithmetic and copies ran while one was open for 4% -> 4% of each run, Pallas kernels for 30% -> 27%
where the time goes in v3:
time: 148 us
  waiting for transfers between devices  58 us (39%)
  Pallas kernels  48.8 us (33%)
  starting transfers between devices  31.6 us (21%)
  local copies, waits for them, and re-layouts  6.8 us (5%)
  other arithmetic  2.3 us (2%)
    ppermute x22, waiting for transfers between devices, partner(): return lax.ppermute(x, 'mode', [(i, i ^ distance) for i in range(count)])  39.3 us
    ppermute x22, starting transfers between devices, partner(): return lax.ppermute(x, 'mode', [(i, i ^ distance) for i in range(count)])  23.9 us
    pallas_call x1, Pallas kernels, first_step(): pl.pallas_call(first_kernel, out_shape=(out, out, jax.ShapeDtypeStruct((c...  20.1 us
    ppermute x5, waiting for transfers between devices, shift(): return lax.ppermute(x, 'rank', [(i, (i + d) % ranks) for i in range(ranks)])  18.8 us
    pallas_call x1, Pallas kernels, hidden(): pl.pallas_call(kernel, out_shape=(out, out), in_specs=[HBM] + ([VMEM] if...  18.1 us
    ppermute x5, starting transfers between devices, shift(): return lax.ppermute(x, 'rank', [(i, (i + d) % ranks) for i in range(ranks)])  7.67 us
    unnamed x17, local copies, waits for them, and re-layouts  4.19 us
    pallas_call x1, Pallas kernels, joined(): pl.pallas_call(functools.partial(joined_kernel, counts), out_shape=out_sh...  3.98 us
  transfers between devices with their start and end apart: 27, of which 23 were waited for; matrix products, arithmetic and copies ran while one was open for 4% of the time, Pallas kernels for 27%

profile of v3, /device:TPU:0, one launch (start us, length us, event | category | flops | bytes accessed | tf_op | source)
XLA Modules:
  0.0 147.8 jit_solution(11983600039609022498)
XLA Ops:
  0.0 0.9 constant_dynamic-slice_fusion
  0.9 3.0 %collective-permute-start = (f32[128,256]{1,0:T(8,128)S(1)}, f32[128,256]{1,0:T(8,128)S(1)}, u32[]{:S(2)}, u32[]{:S(2)}) collective-permute-start(f32[128,256]{1,0:T(8,128)S(1)} %constant_dynamic-slice_fusion), channel_id=1, source_target_pairs={{0,1},{1,0},{2,3},{3,2},{4,5},{5,4},{6,7},{7,6},{8,9},{9,8},{10,11... | collective-permute-start | bytes 393224 | tf_op jit(solution)/shard_map/ppermute | solution.py:315
  4.0 4.2 %collective-permute-done = f32[128,256]{1,0:T(8,128)S(1)} collective-permute-done((f32[128,256]{1,0:T(8,128)S(1)}, f32[128,256]{1,0:T(8,128)S(1)}, u32[]{:S(2)}, u32[]{:S(2)}) %collective-permute-start) | collective-permute-done | bytes 131104 | tf_op jit(solution)/shard_map/ppermute | solution.py:315
  8.3 2.0 %collective-permute-start.1 = (f32[1,128,256]{2,1,0:T(8,128)S(1)}, f32[1,128,256]{2,1,0:T(8,128)S(1)}, u32[]{:S(2)}, u32[]{:S(2)}) collective-permute-start(f32[1,128,256]{2,1,0:T(8,128)S(1)} %bitcast.18), channel_id=1, source_target_pairs={{0,4},{2,6},{4,0},{6,2},{8,12},{10,14},{12,8},{14,10},{16,20},{18,... | collective-permute-start | bytes 393224 | tf_op jit(solution)/shard_map/ppermute | solution.py:311
  10.3 2.9 %collective-permute-done.1 = f32[1,128,256]{2,1,0:T(8,128)S(1)} collective-permute-done((f32[1,128,256]{2,1,0:T(8,128)S(1)}, f32[1,128,256]{2,1,0:T(8,128)S(1)}, u32[]{:S(2)}, u32[]{:S(2)}) %collective-permute-start.1) | collective-permute-done | bytes 131104 | tf_op jit(solution)/shard_map/ppermute | solution.py:311
  13.4 2.8 %copy.8 = f32[128,16,256]{2,0,1:T(8,128)S(1)} copy(f32[128,16,256]{2,1,0:T(8,128)} %sketch_ref.3) | data formatting | bytes 4194304 | tf_op args[3]
  16.3 1.3 copy-done.2
  17.6 0.8 slice.74
  19.3 1.8 %fusion.2.carried_ref = f32[1024,256]{1,0:T(8,128)S(1)} fusion(s32[]{:T(128)S(6)} %select_n.42, f32[512,256]{1,0:T(8,128)S(1)} %bitcast_select_fusion, f32[512,256]{1,0:T(8,128)} %param.9), kind=kLoop, calls=%fused_computation.8 | loop fusion | flops 786432 | bytes 2097156 | tf_op jit(solution)/shard_map/jit(_roll_dynamic)/concatenate | solution.py:344
  21.1 20.1 %shard_map.55 = (bf16[16,512,256]{2,1,0:T(8,128)(2,1)S(1)}, bf16[16,512,256]{2,1,0:T(8,128)(2,1)S(1)}, f32[512,128]{1,0:T(8,128)S(1)}) custom-call(f32[512,16,1024]{2,1,0:T(8,128)} %core_hbm.2, f32[1024,256]{1,0:T(8,128)S(1)} %fusion.2.carried_ref, f32[128,16,256]{2,1,0:T(8,128)S(1)} %copy-done.1), custom_call_target="tpu_custom_call" | custom-call | flops 12884901888 | bytes 33554432 | tf_op jit(solution)/shard_map/pallas_call | solution.py:223
  41.3 11.1 %collective-permute-done.3.refs_0_ = f32[128,16,256]{2,1,0:T(8,128)S(1)} collective-permute-done((f32[128,16,256]{2,1,0:T(8,128)}, f32[128,16,256]{2,1,0:T(8,128)S(1)}, u32[]{:S(2)}, u32[]{:S(2)}) %collective-permute-start.3) | collective-permute-done | bytes 2097184 | tf_op jit(solution)/shard_map/ppermute | solution.py:315
  52.4 3.4 %shard_map.56 = f32[16,32,256]{2,1,0:T(8,128)S(1)} custom-call(s32[2]{0:T(128)S(1)} %pad_add_fusion.place_ref, bf16[16,512,256]{2,1,0:T(8,128)(2,1)S(1)} %get-tuple-element.17.high, bf16[16,512,256]{2,1,0:T(8,128)(2,1)S(1)} %get-tuple-element.18.low, f32[512,128]{1,0:T(8,128)S(1)} %get-tuple-element.19.own_ref, ...), custom_call_target="tpu_custom_call" | custom-call | flops 1610612736 | bytes 8388608 | tf_op jit(solution)/shard_map/pallas_call | solution.py:241
  55.9 1.5 %collective-permute-done.4 = f32[8,32,256]{2,1,0:T(8,128)S(1)} collective-permute-done((f32[8,32,256]{2,1,0:T(8,128)S(1)}, f32[8,32,256]{2,1,0:T(8,128)S(1)}, u32[]{:S(2)}, u32[]{:S(2)}) %collective-permute-start.4) | collective-permute-done | bytes 262176 | tf_op jit(solution)/shard_map/ppermute | solution.py:311
  57.5 1.8 %collective-permute-start.5 = (f32[4,32,256]{2,1,0:T(8,128)S(1)}, f32[4,32,256]{2,1,0:T(8,128)S(1)}, u32[]{:S(2)}, u32[]{:S(2)}) collective-permute-start(f32[4,32,256]{2,1,0:T(8,128)S(1)} %slice.78), channel_id=1, source_target_pairs={{0,4},{2,6},{4,0},{6,2},{8,12},{10,14},{12,8},{14,10},{16,20},{18,... | collective-permute-start | bytes 393224 | tf_op jit(solution)/shard_map/ppermute | solution.py:311
  59.3 1.5 %collective-permute-start.9 = (f32[4,128,256]{2,1,0:T(8,128)S(1)}, f32[4,128,256]{2,1,0:T(8,128)S(1)}, u32[]{:S(2)}, u32[]{:S(2)}) collective-permute-start(f32[4,128,256]{2,1,0:T(8,128)S(1)} %copy-done.4), channel_id=1, source_target_pairs={{0,1},{1,0},{2,3},{3,2},{4,5},{5,4},{6,7},{7,6},{8,9},{9,8},{10,11... | collective-permute-start | bytes 1572872 | tf_op jit(solution)/shard_map/ppermute | solution.py:315
  60.8 2.3 %collective-permute-done.5 = f32[4,32,256]{2,1,0:T(8,128)S(1)} collective-permute-done((f32[4,32,256]{2,1,0:T(8,128)S(1)}, f32[4,32,256]{2,1,0:T(8,128)S(1)}, u32[]{:S(2)}, u32[]{:S(2)}) %collective-permute-start.5) | collective-permute-done | bytes 131104 | tf_op jit(solution)/shard_map/ppermute | solution.py:311
  63.1 3.9 %collective-permute-start.6 = (f32[1,32,256]{2,1,0:T(8,128)S(1)}, f32[1,32,256]{2,1,0:T(8,128)S(1)}, u32[]{:S(2)}, u32[]{:S(2)}) collective-permute-start(f32[1,32,256]{2,1,0:T(8,128)S(1)} %get-tuple-element.34), channel_id=1, source_target_pairs={{0,24},{2,26},{4,28},{6,30},{8,16},{10,18},{12,20},{14,22},{16,8},... | collective-permute-start | bytes 98312 | tf_op jit(solution)/shard_map/ppermute | solution.py:311
  67.0 0.6 collective-permute-start.8
  67.7 1.6 %collective-permute-done.6 = f32[1,32,256]{2,1,0:T(8,128)S(1)} collective-permute-done((f32[1,32,256]{2,1,0:T(8,128)S(1)}, f32[1,32,256]{2,1,0:T(8,128)S(1)}, u32[]{:S(2)}, u32[]{:S(2)}) %collective-permute-start.6) | collective-permute-done | bytes 32800 | tf_op jit(solution)/shard_map/ppermute | solution.py:311
  69.3 2.5 %collective-permute-done.7 = f32[1,32,256]{2,1,0:T(8,128)S(1)} collective-permute-done((f32[1,32,256]{2,1,0:T(8,128)S(1)}, f32[1,32,256]{2,1,0:T(8,128)S(1)}, u32[]{:S(2)}, u32[]{:S(2)}) %collective-permute-start.7) | collective-permute-done | bytes 32800 | tf_op jit(solution)/shard_map/ppermute | solution.py:311
  71.9 1.1 collective-permute-done.9.sketch_ref
  73.0 1.5 %collective-permute-start.10 = (f32[1,32,256]{2,1,0:T(8,128)S(1)}, f32[1,32,256]{2,1,0:T(8,128)S(1)}, u32[]{:S(2)}, u32[]{:S(2)}) collective-permute-start(f32[1,32,256]{2,1,0:T(8,128)S(1)} %fusion.6), channel_id=1, source_target_pairs={{0,1},{1,0},{2,3},{3,2},{4,5},{5,4},{6,7},{7,6},{8,9},{9,8},{10,11... | collective-permute-start | bytes 98312 | tf_op jit(solution)/shard_map/ppermute | solution.py:315
  74.6 2.3 %collective-permute-done.10 = f32[1,32,256]{2,1,0:T(8,128)S(1)} collective-permute-done((f32[1,32,256]{2,1,0:T(8,128)S(1)}, f32[1,32,256]{2,1,0:T(8,128)S(1)}, u32[]{:S(2)}, u32[]{:S(2)}) %collective-permute-start.10) | collective-permute-done | bytes 32800 | tf_op jit(solution)/shard_map/ppermute | solution.py:315
  76.9 1.5 %collective-permute-start.16 = (f32[12,128,256]{2,1,0:T(8,128)S(1)}, f32[12,128,256]{2,1,0:T(8,128)S(1)}, u32[]{:S(2)}, u32[]{:S(2)}) collective-permute-start(f32[12,128,256]{2,1,0:T(8,128)S(1)} %slice.83), channel_id=1, source_target_pairs={{0,1},{1,0},{2,3},{3,2},{4,5},{5,4},{6,7},{7,6},{8,9},{9,8},{10,11... | collective-permute-start | bytes 4718600 | tf_op jit(solution)/shard_map/ppermute | solution.py:315
  78.4 3.6 %collective-permute-start.11 = (f32[1,2,32,256]{3,2,1,0:T(8,128)S(1)}, f32[1,2,32,256]{3,2,1,0:T(8,128)S(1)}, u32[]{:S(2)}, u32[]{:S(2)}) collective-permute-start(f32[1,2,32,256]{3,2,1,0:T(8,128)S(1)} %maximum_bitcast_fusion), channel_id=1, source_target_pairs={{0,24},{2,26},{4,28},{6,30},{8,16},{10,18},{12,20},{14,22},{16,8},... | collective-permute-start | bytes 196616 | tf_op jit(solution)/shard_map/ppermute | solution.py:311
  82.0 0.8 collective-permute-start.13
  82.8 2.2 %collective-permute-done.11 = f32[1,2,32,256]{3,2,1,0:T(8,128)S(1)} collective-permute-done((f32[1,2,32,256]{3,2,1,0:T(8,128)S(1)}, f32[1,2,32,256]{3,2,1,0:T(8,128)S(1)}, u32[]{:S(2)}, u32[]{:S(2)}) %collective-permute-start.11) | collective-permute-done | bytes 65568 | tf_op jit(solution)/shard_map/ppermute | solution.py:311
  85.0 2.2 %collective-permute-done.12 = f32[1,2,32,256]{3,2,1,0:T(8,128)S(1)} collective-permute-done((f32[1,2,32,256]{3,2,1,0:T(8,128)S(1)}, f32[1,2,32,256]{3,2,1,0:T(8,128)S(1)}, u32[]{:S(2)}, u32[]{:S(2)}) %collective-permute-start.12) | collective-permute-done | bytes 65568 | tf_op jit(solution)/shard_map/ppermute | solution.py:311
  87.2 0.6 collective-permute-start.14
  87.8 5.8 %collective-permute-done.14 = f32[4,2,32,256]{3,2,1,0:T(8,128)S(1)} collective-permute-done((f32[4,2,32,256]{3,2,1,0:T(8,128)S(1)}, f32[4,2,32,256]{3,2,1,0:T(8,128)S(1)}, u32[]{:S(2)}, u32[]{:S(2)}) %collective-permute-start.14) | collective-permute-done | bytes 262176 | tf_op jit(solution)/shard_map/ppermute | solution.py:311
  93.7 1.1 shard_map.58.refs_0_
  95.6 18.1 %shard_map.57 = (bf16[16,512,256]{2,1,0:T(8,128)(2,1)S(1)}, bf16[16,512,256]{2,1,0:T(8,128)(2,1)S(1)}) custom-call(f32[512,16,1024]{2,1,0:T(8,128)} %core_hbm.3, s32[2]{0:T(128)S(1)} %pad_add_fusion.place_ref, f32[8,2,32,256]{3,2,1,0:T(8,128)S(1)} %constant_dynamic-update-slice_fusion.refs_0_, f32[8,2,32,256]{3,2,1,0:T(8,128)S(1)} %collective-permute-done.15.refs_1_), custom_call_target="tpu_custom_call" | custom-call | flops 1 | bytes 1 | tf_op jit(solution)/shard_map/pallas_call | solution.py:204
  114.3 4.0 %shard_map.61 = f32[16,32,256]{2,1,0:T(8,128)S(1)} custom-call(s32[2]{0:T(128)S(1)} %pad_add_fusion.place_ref, bf16[16,512,256]{2,1,0:T(8,128)(2,1)S(1)} %get-tuple-element.25.high, bf16[16,512,256]{2,1,0:T(8,128)(2,1)S(1)} %get-tuple-element.26.low, bf16[16,256,256]{2,1,0:T(8,128)(2,1)S(1)} %shard_map.58.refs_0_, ...), custom_call_target="tpu_custom_call" | custom-call | flops 3221225472 | bytes 8388608 | tf_op jit(solution)/shard_map/pallas_call | solution.py:254
  118.5 1.4 collective-permute-done.17
  120.0 0.6 collective-permute-start.18
  120.6 5.0 %collective-permute-done.18 = f32[4,32,256]{2,1,0:T(8,128)S(1)} collective-permute-done((f32[4,32,256]{2,1,0:T(8,128)S(1)}, f32[4,32,256]{2,1,0:T(8,128)S(1)}, u32[]{:S(2)}, u32[]{:S(2)}) %collective-permute-start.18) | collective-permute-done | bytes 131104 | tf_op jit(solution)/shard_map/ppermute | solution.py:311
  125.6 1.7 %collective-permute-start.19 = (f32[1,32,256]{2,1,0:T(8,128)S(1)}, f32[1,32,256]{2,1,0:T(8,128)S(1)}, u32[]{:S(2)}, u32[]{:S(2)}) collective-permute-start(f32[1,32,256]{2,1,0:T(8,128)S(1)} %get-tuple-element.31), channel_id=1, source_target_pairs={{0,24},{2,26},{4,28},{6,30},{8,16},{10,18},{12,20},{14,22},{16,8},... | collective-permute-start | bytes 98312 | tf_op jit(solution)/shard_map/ppermute | solution.py:311
  127.8 2.3 %collective-permute-start.21 = (f32[1,32,256]{2,1,0:T(8,128)S(1)}, f32[1,32,256]{2,1,0:T(8,128)S(1)}, u32[]{:S(2)}, u32[]{:S(2)}) collective-permute-start(f32[1,32,256]{2,1,0:T(8,128)S(1)} %get-tuple-element.32), channel_id=1, source_target_pairs={{0,8},{2,10},{4,12},{6,14},{8,0},{10,2},{12,4},{14,6},{16,24},{18,... | collective-permute-start | bytes 98312 | tf_op jit(solution)/shard_map/ppermute | solution.py:311
  130.1 1.6 %collective-permute-done.19 = f32[1,32,256]{2,1,0:T(8,128)S(1)} collective-permute-done((f32[1,32,256]{2,1,0:T(8,128)S(1)}, f32[1,32,256]{2,1,0:T(8,128)S(1)}, u32[]{:S(2)}, u32[]{:S(2)}) %collective-permute-start.19) | collective-permute-done | bytes 32800 | tf_op jit(solution)/shard_map/ppermute | solution.py:311
  132.4 2.4 %collective-permute-start.22 = (f32[1,32,256]{2,1,0:T(8,128)S(1)}, f32[1,32,256]{2,1,0:T(8,128)S(1)}, u32[]{:S(2)}, u32[]{:S(2)}) collective-permute-start(f32[1,32,256]{2,1,0:T(8,128)S(1)} %get-tuple-element.30), channel_id=1, source_target_pairs={{0,24},{2,26},{4,28},{6,30},{8,16},{10,18},{12,20},{14,22},{16,8},... | collective-permute-start | bytes 98312 | tf_op jit(solution)/shard_map/ppermute | solution.py:311
  134.7 0.8 collective-permute-start.23
  135.5 1.3 collective-permute-start.24
  136.8 1.3 collective-permute-done.22
  138.2 1.5 %collective-permute-done.23 = f32[1,32,256]{2,1,0:T(8,128)S(1)} collective-permute-done((f32[1,32,256]{2,1,0:T(8,128)S(1)}, f32[1,32,256]{2,1,0:T(8,128)S(1)}, u32[]{:S(2)}, u32[]{:S(2)}) %collective-permute-start.23) | collective-permute-done | bytes 32800 | tf_op jit(solution)/shard_map/ppermute | solution.py:311
  139.8 0.6 collective-permute-start.25
  140.4 4.4 %collective-permute-done.25 = f32[4,32,256]{2,1,0:T(8,128)S(1)} collective-permute-done((f32[4,32,256]{2,1,0:T(8,128)S(1)}, f32[4,32,256]{2,1,0:T(8,128)S(1)}, u32[]{:S(2)}, u32[]{:S(2)}) %collective-permute-start.25) | collective-permute-done | bytes 131104 | tf_op jit(solution)/shard_map/ppermute | solution.py:311
  144.9 1.5 %collective-permute-done.26.refs_1_ = f32[8,32,256]{2,1,0:T(8,128)S(1)} collective-permute-done((f32[8,32,256]{2,1,0:T(8,128)S(1)}, f32[8,32,256]{2,1,0:T(8,128)S(1)}, u32[]{:S(2)}, u32[]{:S(2)}) %collective-permute-start.26) | collective-permute-done | bytes 262176 | tf_op jit(solution)/shard_map/ppermute | solution.py:311
  146.4 1.4 shard_map.62
  (62 shorter events, 4.5 us)
Async XLA Ops:
  0.9 7.4 %collective-permute-start = (f32[128,256]{1,0:T(8,128)S(1)}, f32[128,256]{1,0:T(8,128)S(1)}, u32[]{:S(2)}, u32[]{:S(2)}) collective-permute-start(f32[128,256]{1,0:T(8,128)S(1)} %constant_dynamic-slice_fusion), channel_id=1, source_target_pairs={{0,1},{1,0},{2,3},{3,2},{4,5},{5,4},{6,7},{7,6},{8,9},{9,8},{10,11... | collective-permute-start | bytes 393224 | tf_op jit(solution)/shard_map/ppermute | solution.py:315
  3.9 48.4 %collective-permute-start.3 = (f32[128,16,256]{2,1,0:T(8,128)}, f32[128,16,256]{2,1,0:T(8,128)S(1)}, u32[]{:S(2)}, u32[]{:S(2)}) collective-permute-start(f32[128,16,256]{2,1,0:T(8,128)} %sketch_ref.2), channel_id=1, source_target_pairs={{0,1},{1,0},{2,3},{3,2},{4,5},{5,4},{6,7},{7,6},{8,9},{9,8},{10,11... | collective-permute-start | bytes 6291464 | tf_op jit(solution)/shard_map/ppermute | solution.py:315
  8.3 5.0 %collective-permute-start.1 = (f32[1,128,256]{2,1,0:T(8,128)S(1)}, f32[1,128,256]{2,1,0:T(8,128)S(1)}, u32[]{:S(2)}, u32[]{:S(2)}) collective-permute-start(f32[1,128,256]{2,1,0:T(8,128)S(1)} %bitcast.18), channel_id=1, source_target_pairs={{0,4},{2,6},{4,0},{6,2},{8,12},{10,14},{12,8},{14,10},{16,20},{18,... | collective-permute-start | bytes 393224 | tf_op jit(solution)/shard_map/ppermute | solution.py:311
  13.3 5.2 %collective-permute-start.2 = (f32[2,128,256]{2,1,0:T(8,128)S(1)}, f32[2,128,256]{2,1,0:T(8,128)S(1)}, u32[]{:S(2)}, u32[]{:S(2)}) collective-permute-start(f32[2,128,256]{2,1,0:T(8,128)S(1)} %pad_maximum_fusion.1), channel_id=1, source_target_pairs={{0,2},{2,0},{4,6},{6,4},{8,10},{10,8},{12,14},{14,12},{16,18},{18,... | collective-permute-start | bytes 786440 | tf_op jit(solution)/shard_map/ppermute | solution.py:311
  16.2 1.3 copy-start.2
  19.1 2.0 %copy-start.1 = (f32[128,16,256]{2,1,0:T(8,128)S(1)}, f32[128,16,256]{2,1,0:T(8,128)}, u32[]{:S(2)}) copy-start(f32[128,16,256]{2,1,0:T(8,128)} %sketch_ref.2) | copy-start | bytes 6291460
  52.4 6.9 %copy-start.4 = (f32[4,128,256]{2,1,0:T(8,128)S(1)}, f32[4,128,256]{2,1,0:T(8,128)}, u32[]{:S(2)}) copy-start(f32[4,128,256]{2,1,0:T(8,128)} %slice.74) | copy-start | bytes 1572868
  55.8 18.7 %copy-start.3 = (f32[128,16,256]{2,0,1:T(8,128)S(1)}, f32[128,16,256]{2,0,1:T(8,128)}, u32[]{:S(2)}) copy-start(f32[128,16,256]{2,0,1:T(8,128)} %copy-done.2) | copy-start | bytes 6291460
  55.8 1.6 %collective-permute-start.4 = (f32[8,32,256]{2,1,0:T(8,128)S(1)}, f32[8,32,256]{2,1,0:T(8,128)S(1)}, u32[]{:S(2)}, u32[]{:S(2)}) collective-permute-start(f32[8,32,256]{2,1,0:T(8,128)S(1)} %slice.76), channel_id=1, source_target_pairs={{0,2},{2,0},{4,6},{6,4},{8,10},{10,8},{12,14},{14,12},{16,18},{18,... | collective-permute-start | bytes 786440 | tf_op jit(solution)/shard_map/ppermute | solution.py:311
  57.5 5.6 %collective-permute-start.5 = (f32[4,32,256]{2,1,0:T(8,128)S(1)}, f32[4,32,256]{2,1,0:T(8,128)S(1)}, u32[]{:S(2)}, u32[]{:S(2)}) collective-permute-start(f32[4,32,256]{2,1,0:T(8,128)S(1)} %slice.78), channel_id=1, source_target_pairs={{0,4},{2,6},{4,0},{6,2},{8,12},{10,14},{12,8},{14,10},{16,20},{18,... | collective-permute-start | bytes 393224 | tf_op jit(solution)/shard_map/ppermute | solution.py:311
  59.3 13.7 %collective-permute-start.9 = (f32[4,128,256]{2,1,0:T(8,128)S(1)}, f32[4,128,256]{2,1,0:T(8,128)S(1)}, u32[]{:S(2)}, u32[]{:S(2)}) collective-permute-start(f32[4,128,256]{2,1,0:T(8,128)S(1)} %copy-done.4), channel_id=1, source_target_pairs={{0,1},{1,0},{2,3},{3,2},{4,5},{5,4},{6,7},{7,6},{8,9},{9,8},{10,11... | collective-permute-start | bytes 1572872 | tf_op jit(solution)/shard_map/ppermute | solution.py:315
  63.1 6.2 %collective-permute-start.6 = (f32[1,32,256]{2,1,0:T(8,128)S(1)}, f32[1,32,256]{2,1,0:T(8,128)S(1)}, u32[]{:S(2)}, u32[]{:S(2)}) collective-permute-start(f32[1,32,256]{2,1,0:T(8,128)S(1)} %get-tuple-element.34), channel_id=1, source_target_pairs={{0,24},{2,26},{4,28},{6,30},{8,16},{10,18},{12,20},{14,22},{16,8},... | collective-permute-start | bytes 98312 | tf_op jit(solution)/shard_map/ppermute | solution.py:311
  67.0 4.8 %collective-permute-start.7 = (f32[1,32,256]{2,1,0:T(8,128)S(1)}, f32[1,32,256]{2,1,0:T(8,128)S(1)}, u32[]{:S(2)}, u32[]{:S(2)}) collective-permute-start(f32[1,32,256]{2,1,0:T(8,128)S(1)} %get-tuple-element.36), channel_id=1, source_target_pairs={{0,16},{2,18},{4,20},{6,22},{8,24},{10,26},{12,28},{14,30},{16,0},... | collective-permute-start | bytes 98312 | tf_op jit(solution)/shard_map/ppermute | solution.py:311
  67.0 4.8 %collective-permute-start.8 = (f32[1,32,256]{2,1,0:T(8,128)S(1)}, f32[1,32,256]{2,1,0:T(8,128)S(1)}, u32[]{:S(2)}, u32[]{:S(2)}) collective-permute-start(f32[1,32,256]{2,1,0:T(8,128)S(1)} %get-tuple-element.35), channel_id=1, source_target_pairs={{0,8},{2,10},{4,12},{6,14},{8,0},{10,2},{12,4},{14,6},{16,24},{18,... | collective-permute-start | bytes 98312 | tf_op jit(solution)/shard_map/ppermute | solution.py:311
  71.9 21.9 %copy-start = (f32[128,16,256]{2,1,0:T(8,128)S(1)}, f32[128,16,256]{2,1,0:T(8,128)}, u32[]{:S(2)}) copy-start(f32[128,16,256]{2,1,0:T(8,128)} %sketch_ref.3) | copy-start | bytes 6291460
  73.0 3.9 %collective-permute-start.10 = (f32[1,32,256]{2,1,0:T(8,128)S(1)}, f32[1,32,256]{2,1,0:T(8,128)S(1)}, u32[]{:S(2)}, u32[]{:S(2)}) collective-permute-start(f32[1,32,256]{2,1,0:T(8,128)S(1)} %fusion.6), channel_id=1, source_target_pairs={{0,1},{1,0},{2,3},{3,2},{4,5},{5,4},{6,7},{7,6},{8,9},{9,8},{10,11... | collective-permute-start | bytes 98312 | tf_op jit(solution)/shard_map/ppermute | solution.py:315
  76.9 36.9 %collective-permute-start.16 = (f32[12,128,256]{2,1,0:T(8,128)S(1)}, f32[12,128,256]{2,1,0:T(8,128)S(1)}, u32[]{:S(2)}, u32[]{:S(2)}) collective-permute-start(f32[12,128,256]{2,1,0:T(8,128)S(1)} %slice.83), channel_id=1, source_target_pairs={{0,1},{1,0},{2,3},{3,2},{4,5},{5,4},{6,7},{7,6},{8,9},{9,8},{10,11... | collective-permute-start | bytes 4718600 | tf_op jit(solution)/shard_map/ppermute | solution.py:315
  78.4 6.6 %collective-permute-start.11 = (f32[1,2,32,256]{3,2,1,0:T(8,128)S(1)}, f32[1,2,32,256]{3,2,1,0:T(8,128)S(1)}, u32[]{:S(2)}, u32[]{:S(2)}) collective-permute-start(f32[1,2,32,256]{3,2,1,0:T(8,128)S(1)} %maximum_bitcast_fusion), channel_id=1, source_target_pairs={{0,24},{2,26},{4,28},{6,30},{8,16},{10,18},{12,20},{14,22},{16,8},... | collective-permute-start | bytes 196616 | tf_op jit(solution)/shard_map/ppermute | solution.py:311
  82.0 5.2 %collective-permute-start.12 = (f32[1,2,32,256]{3,2,1,0:T(8,128)S(1)}, f32[1,2,32,256]{3,2,1,0:T(8,128)S(1)}, u32[]{:S(2)}, u32[]{:S(2)}) collective-permute-start(f32[1,2,32,256]{3,2,1,0:T(8,128)S(1)} %maximum_bitcast_fusion), channel_id=1, source_target_pairs={{0,16},{2,18},{4,20},{6,22},{8,24},{10,26},{12,28},{14,30},{16,0},... | collective-permute-start | bytes 196616 | tf_op jit(solution)/shard_map/ppermute | solution.py:311
  82.0 5.2 %collective-permute-start.13 = (f32[1,2,32,256]{3,2,1,0:T(8,128)S(1)}, f32[1,2,32,256]{3,2,1,0:T(8,128)S(1)}, u32[]{:S(2)}, u32[]{:S(2)}) collective-permute-start(f32[1,2,32,256]{3,2,1,0:T(8,128)S(1)} %maximum_bitcast_fusion), channel_id=1, source_target_pairs={{0,8},{2,10},{4,12},{6,14},{8,0},{10,2},{12,4},{14,6},{16,24},{18,... | collective-permute-start | bytes 196616 | tf_op jit(solution)/shard_map/ppermute | solution.py:311
  87.2 6.4 %collective-permute-start.14 = (f32[4,2,32,256]{3,2,1,0:T(8,128)S(1)}, f32[4,2,32,256]{3,2,1,0:T(8,128)S(1)}, u32[]{:S(2)}, u32[]{:S(2)}) collective-permute-start(f32[4,2,32,256]{3,2,1,0:T(8,128)S(1)} %pad_maximum_fusion.2), channel_id=1, source_target_pairs={{0,4},{2,6},{4,0},{6,2},{8,12},{10,14},{12,8},{14,10},{16,20},{18,... | collective-permute-start | bytes 786440 | tf_op jit(solution)/shard_map/ppermute | solution.py:311
  93.7 2.0 %collective-permute-start.15 = (f32[8,2,32,256]{3,2,1,0:T(8,128)S(1)}, f32[8,2,32,256]{3,2,1,0:T(8,128)S(1)}, u32[]{:S(2)}, u32[]{:S(2)}) collective-permute-start(f32[8,2,32,256]{3,2,1,0:T(8,128)S(1)} %constant_dynamic-update-slice_fusion.refs_0_), channel_id=1, source_target_pairs={{0,2},{2,0},{4,6},{6,4},{8,10},{10,8},{12,14},{14,12},{16,18},{18,... | collective-permute-start | bytes 1572872 | tf_op jit(solution)/shard_map/ppermute | solution.py:311
  118.3 1.6 %collective-permute-start.17 = (f32[8,32,256]{2,1,0:T(8,128)S(1)}, f32[8,32,256]{2,1,0:T(8,128)S(1)}, u32[]{:S(2)}, u32[]{:S(2)}) collective-permute-start(f32[8,32,256]{2,1,0:T(8,128)S(1)} %slice.85), channel_id=1, source_target_pairs={{0,2},{2,0},{4,6},{6,4},{8,10},{10,8},{12,14},{14,12},{16,18},{18,... | collective-permute-start | bytes 786440 | tf_op jit(solution)/shard_map/ppermute | solution.py:311
  120.0 5.6 %collective-permute-start.18 = (f32[4,32,256]{2,1,0:T(8,128)S(1)}, f32[4,32,256]{2,1,0:T(8,128)S(1)}, u32[]{:S(2)}, u32[]{:S(2)}) collective-permute-start(f32[4,32,256]{2,1,0:T(8,128)S(1)} %slice.87), channel_id=1, source_target_pairs={{0,4},{2,6},{4,0},{6,2},{8,12},{10,14},{12,8},{14,10},{16,20},{18,... | collective-permute-start | bytes 393224 | tf_op jit(solution)/shard_map/ppermute | solution.py:311
  125.6 6.1 %collective-permute-start.19 = (f32[1,32,256]{2,1,0:T(8,128)S(1)}, f32[1,32,256]{2,1,0:T(8,128)S(1)}, u32[]{:S(2)}, u32[]{:S(2)}) collective-permute-start(f32[1,32,256]{2,1,0:T(8,128)S(1)} %get-tuple-element.31), channel_id=1, source_target_pairs={{0,24},{2,26},{4,28},{6,30},{8,16},{10,18},{12,20},{14,22},{16,8},... | collective-permute-start | bytes 98312 | tf_op jit(solution)/shard_map/ppermute | solution.py:311
  127.3 4.9 %collective-permute-start.20 = (f32[1,32,256]{2,1,0:T(8,128)S(1)}, f32[1,32,256]{2,1,0:T(8,128)S(1)}, u32[]{:S(2)}, u32[]{:S(2)}) collective-permute-start(f32[1,32,256]{2,1,0:T(8,128)S(1)} %get-tuple-element.33), channel_id=1, source_target_pairs={{0,16},{2,18},{4,20},{6,22},{8,24},{10,26},{12,28},{14,30},{16,0},... | collective-permute-start | bytes 98312 | tf_op jit(solution)/shard_map/ppermute | solution.py:311
  127.8 4.6 %collective-permute-start.21 = (f32[1,32,256]{2,1,0:T(8,128)S(1)}, f32[1,32,256]{2,1,0:T(8,128)S(1)}, u32[]{:S(2)}, u32[]{:S(2)}) collective-permute-start(f32[1,32,256]{2,1,0:T(8,128)S(1)} %get-tuple-element.32), channel_id=1, source_target_pairs={{0,8},{2,10},{4,12},{6,14},{8,0},{10,2},{12,4},{14,6},{16,24},{18,... | collective-permute-start | bytes 98312 | tf_op jit(solution)/shard_map/ppermute | solution.py:311
  132.4 5.8 %collective-permute-start.22 = (f32[1,32,256]{2,1,0:T(8,128)S(1)}, f32[1,32,256]{2,1,0:T(8,128)S(1)}, u32[]{:S(2)}, u32[]{:S(2)}) collective-permute-start(f32[1,32,256]{2,1,0:T(8,128)S(1)} %get-tuple-element.30), channel_id=1, source_target_pairs={{0,24},{2,26},{4,28},{6,30},{8,16},{10,18},{12,20},{14,22},{16,8},... | collective-permute-start | bytes 98312 | tf_op jit(solution)/shard_map/ppermute | solution.py:311
  134.7 4.9 %collective-permute-start.23 = (f32[1,32,256]{2,1,0:T(8,128)S(1)}, f32[1,32,256]{2,1,0:T(8,128)S(1)}, u32[]{:S(2)}, u32[]{:S(2)}) collective-permute-start(f32[1,32,256]{2,1,0:T(8,128)S(1)} %get-tuple-element.30), channel_id=1, source_target_pairs={{0,16},{2,18},{4,20},{6,22},{8,24},{10,26},{12,28},{14,30},{16,0},... | collective-permute-start | bytes 98312 | tf_op jit(solution)/shard_map/ppermute | solution.py:311
  135.5 4.3 %collective-permute-start.24 = (f32[1,32,256]{2,1,0:T(8,128)S(1)}, f32[1,32,256]{2,1,0:T(8,128)S(1)}, u32[]{:S(2)}, u32[]{:S(2)}) collective-permute-start(f32[1,32,256]{2,1,0:T(8,128)S(1)} %get-tuple-element.30), channel_id=1, source_target_pairs={{0,8},{2,10},{4,12},{6,14},{8,0},{10,2},{12,4},{14,6},{16,24},{18,... | collective-permute-start | bytes 98312 | tf_op jit(solution)/shard_map/ppermute | solution.py:311
  139.8 5.0 %collective-permute-start.25 = (f32[4,32,256]{2,1,0:T(8,128)S(1)}, f32[4,32,256]{2,1,0:T(8,128)S(1)}, u32[]{:S(2)}, u32[]{:S(2)}) collective-permute-start(f32[4,32,256]{2,1,0:T(8,128)S(1)} %pad_maximum_fusion.3), channel_id=1, source_target_pairs={{0,4},{2,6},{4,0},{6,2},{8,12},{10,14},{12,8},{14,10},{16,20},{18,... | collective-permute-start | bytes 393224 | tf_op jit(solution)/shard_map/ppermute | solution.py:311
  144.8 1.6 %collective-permute-start.26 = (f32[8,32,256]{2,1,0:T(8,128)S(1)}, f32[8,32,256]{2,1,0:T(8,128)S(1)}, u32[]{:S(2)}, u32[]{:S(2)}) collective-permute-start(f32[8,32,256]{2,1,0:T(8,128)S(1)} %constant_dynamic-update-slice_fusion.5.refs_0_), channel_id=1, source_target_pairs={{0,2},{2,0},{4,6},{6,4},{8,10},{10,8},{12,14},{14,12},{16,18},{18,... | collective-permute-start | bytes 786440 | tf_op jit(solution)/shard_map/ppermute | solution.py:311

commit v4 on v3

--- a/solution.py
+++ b/solution.py
@@ -208,7 +208,7 @@
         out_specs=(VMEM, VMEM),
         scratch_shapes=loop_scratch(core, columns),
         compiler_params=limit(32),
-        cost_estimate=cost(6 * count * slices * depth * columns, 4 * core.size) if place is None else cost(1, 1),
+        cost_estimate=cost(6 * count * slices * depth * columns, 4 * core.size) if place is None else cost(2 * core.size * columns, 1),
     )(core, *operands)
 
 
@@ -227,7 +227,7 @@
         out_specs=(VMEM,) * 3,
         scratch_shapes=[pltpu.VMEM((slices, depth, 2 * size), BF16)] + loop_scratch(core, columns),
         compiler_params=limit(36),
-        cost_estimate=cost(6 * core.size * columns, 4 * core.size),
+        cost_estimate=cost(4 * core.size * columns, 1),
     )(core, carried, sketch)
 
 
@@ -344,14 +344,18 @@
     return jnp.roll(joined, (rank + 1) * blocks[0].shape[axis], axis=axis)
 
 
-def quad_part(x, modes, mode):
-    groups = digit_groups(modes)[:2]
+def part_groups(modes):
+    return [(low, 1) for low in range(min(3, modes.bit_length() - 1))]
+
+
+def own_part(x, modes, mode):
+    groups = part_groups(modes)
     size = x.shape[0] >> len(groups)
     return lax.dynamic_slice_in_dim(x, piece_of(mode, groups) * size, size)
 
 
 def all_rows(x, parts, modes, rank, mode):
-    groups = digit_groups(modes)[:2]
+    groups = part_groups(modes)
     own = piece_of(mode, groups)
     blocks = [in_order(all_gather(part[None], modes, groups), own).reshape(x.shape) for part in parts]
     return by_rank([x] + blocks, rank, 0)
@@ -377,7 +381,7 @@
 
     sketch_slices = jnp.swapaxes(sketch_left, 0, 1)
     left_a, left_b = sketch_slices[:early], sketch_slices[early:]
-    part = quad_part(carry_in, modes, mode)
+    part = own_part(carry_in, modes, mode)
     parts = shifted(part)
     _, right = lax.optimization_barrier((part, sketch_right))
     arrived = shifted(right)
@@ -387,8 +391,8 @@
     left_a_arrived = shifted(left_a)
     term = second_product(place, high, low, term, arrived, count)
     middle = scattered(term)
-    middle, left_a_arrived = lax.optimization_barrier((middle, left_a_arrived))
-    middles, left_b = lax.optimization_barrier((shifted(middle), left_b))
+    middle, left_a_arrived, left_b = lax.optimization_barrier((middle, left_a_arrived, left_b))
+    middles = shifted(middle)
     left_b_arrived = shifted(left_b)
     if count:
         both = jnp.concatenate([middle] + middles)[None]

time: 148 us -> 146 us (0.986)
  waiting for transfers between devices: 58 us -> 55.5 us
    ppermute x5, waiting for transfers between devices: 18.8 us -> 13.6 us  [shift(): return lax.ppermute(x, 'rank', [(i, (i + d) % ranks) for i in range(ranks)])]
    ppermute x22 -> x23, waiting for transfers between devices: 39.3 us -> 41.9 us  [partner(): return lax.ppermute(x, 'mode', [(i, i ^ distance) for i in range(count)])]
    ppermute x22 -> x23, starting transfers between devices: 23.9 us -> 26.3 us  [partner(): return lax.ppermute(x, 'mode', [(i, i ^ distance) for i in range(count)])]
    ppermute x5, starting transfers between devices: 7.67 us -> 6.11 us  [shift(): return lax.ppermute(x, 'rank', [(i, (i + d) % ranks) for i in range(ranks)])]
  transfers between devices with their start and end apart: 27 -> 28, of which waited for: 23 -> 24; matrix products, arithmetic and copies ran while one was open for 4% -> 5% of each run, Pallas kernels for 27% -> 26%
where the time goes in v4:
time: 146 us
  waiting for transfers between devices  55.5 us (38%)
  Pallas kernels  49 us (34%)
  starting transfers between devices  32.4 us (22%)
  local copies, waits for them, and re-layouts  6.81 us (5%)
  other arithmetic  2.17 us (1%)
    ppermute x23, waiting for transfers between devices, partner(): return lax.ppermute(x, 'mode', [(i, i ^ distance) for i in range(count)])  41.9 us
    ppermute x23, starting transfers between devices, partner(): return lax.ppermute(x, 'mode', [(i, i ^ distance) for i in range(count)])  26.3 us
    pallas_call x1, Pallas kernels, first_step(): pl.pallas_call(first_kernel, out_shape=(out, out, jax.ShapeDtypeStruct((c...  19.8 us
    pallas_call x1, Pallas kernels, hidden(): pl.pallas_call(kernel, out_shape=(out, out), in_specs=[HBM] + ([VMEM] if...  17.6 us
    ppermute x5, waiting for transfers between devices, shift(): return lax.ppermute(x, 'rank', [(i, (i + d) % ranks) for i in range(ranks)])  13.6 us
    ppermute x5, starting transfers between devices, shift(): return lax.ppermute(x, 'rank', [(i, (i + d) % ranks) for i in range(ranks)])  6.11 us
    pallas_call x1, Pallas kernels, second_product(): pl.pallas_call(second_kernel, out_shape=out_shape(rows, columns, count),...  4.51 us
    unnamed x17, local copies, waits for them, and re-layouts  4.19 us
  transfers between devices with their start and end apart: 28, of which 24 were waited for; matrix products, arithmetic and copies ran while one was open for 5% of the time, Pallas kernels for 26%

profile of v4, /device:TPU:0, one launch (start us, length us, event | category | flops | bytes accessed | tf_op | source)
XLA Modules:
  0.0 146.2 jit_solution(17707869159342346469)
XLA Ops:
  0.0 0.8 constant_dynamic-slice_fusion
  0.8 3.0 %collective-permute-start = (f32[64,256]{1,0:T(8,128)S(1)}, f32[64,256]{1,0:T(8,128)S(1)}, u32[]{:S(2)}, u32[]{:S(2)}) collective-permute-start(f32[64,256]{1,0:T(8,128)S(1)} %constant_dynamic-slice_fusion), channel_id=1, source_target_pairs={{0,1},{1,0},{2,3},{3,2},{4,5},{5,4},{6,7},{7,6},{8,9},{9,8},{10,11... | collective-permute-start | bytes 196616 | tf_op jit(solution)/shard_map/ppermute | solution.py:315
  3.8 2.5 %collective-permute-done = f32[64,256]{1,0:T(8,128)S(1)} collective-permute-done((f32[64,256]{1,0:T(8,128)S(1)}, f32[64,256]{1,0:T(8,128)S(1)}, u32[]{:S(2)}, u32[]{:S(2)}) %collective-permute-start) | collective-permute-done | bytes 65568 | tf_op jit(solution)/shard_map/ppermute | solution.py:315
  6.3 2.2 %collective-permute-start.1 = (f32[1,64,256]{2,1,0:T(8,128)S(1)}, f32[1,64,256]{2,1,0:T(8,128)S(1)}, u32[]{:S(2)}, u32[]{:S(2)}) collective-permute-start(f32[1,64,256]{2,1,0:T(8,128)S(1)} %bitcast.16), channel_id=1, source_target_pairs={{0,8},{2,10},{4,12},{6,14},{8,0},{10,2},{12,4},{14,6},{16,24},{18,... | collective-permute-start | bytes 196616 | tf_op jit(solution)/shard_map/ppermute | solution.py:311
  8.5 2.2 %collective-permute-done.1 = f32[1,64,256]{2,1,0:T(8,128)S(1)} collective-permute-done((f32[1,64,256]{2,1,0:T(8,128)S(1)}, f32[1,64,256]{2,1,0:T(8,128)S(1)}, u32[]{:S(2)}, u32[]{:S(2)}) %collective-permute-start.1) | collective-permute-done | bytes 65568 | tf_op jit(solution)/shard_map/ppermute | solution.py:311
  10.8 2.0 %collective-permute-start.2 = (f32[2,64,256]{2,1,0:T(8,128)S(1)}, f32[2,64,256]{2,1,0:T(8,128)S(1)}, u32[]{:S(2)}, u32[]{:S(2)}) collective-permute-start(f32[2,64,256]{2,1,0:T(8,128)S(1)} %pad_maximum_fusion.3), channel_id=1, source_target_pairs={{0,4},{2,6},{4,0},{6,2},{8,12},{10,14},{12,8},{14,10},{16,20},{18,... | collective-permute-start | bytes 393224 | tf_op jit(solution)/shard_map/ppermute | solution.py:311
  12.8 3.0 %collective-permute-done.2 = f32[2,64,256]{2,1,0:T(8,128)S(1)} collective-permute-done((f32[2,64,256]{2,1,0:T(8,128)S(1)}, f32[2,64,256]{2,1,0:T(8,128)S(1)}, u32[]{:S(2)}, u32[]{:S(2)}) %collective-permute-start.2) | collective-permute-done | bytes 131104 | tf_op jit(solution)/shard_map/ppermute | solution.py:311
  16.1 2.8 %copy.8 = f32[128,16,256]{2,0,1:T(8,128)S(1)} copy(f32[128,16,256]{2,1,0:T(8,128)} %sketch_ref.3) | data formatting | bytes 4194304 | tf_op args[3]
  18.9 1.3 copy-done.2
  20.2 0.8 slice.74
  22.0 1.7 %fusion.2.carried_ref = f32[1024,256]{1,0:T(8,128)S(1)} fusion(s32[]{:T(128)S(6)} %select_n.42, f32[512,256]{1,0:T(8,128)S(1)} %bitcast_select_fusion, f32[512,256]{1,0:T(8,128)} %param.9), kind=kLoop, calls=%fused_computation.8 | loop fusion | flops 786432 | bytes 2097156 | tf_op jit(solution)/shard_map/jit(_roll_dynamic)/concatenate | solution.py:344
  23.7 19.8 %shard_map.55 = (bf16[16,512,256]{2,1,0:T(8,128)(2,1)S(1)}, bf16[16,512,256]{2,1,0:T(8,128)(2,1)S(1)}, f32[512,128]{1,0:T(8,128)S(1)}) custom-call(f32[512,16,1024]{2,1,0:T(8,128)} %core_hbm.2, f32[1024,256]{1,0:T(8,128)S(1)} %fusion.2.carried_ref, f32[128,16,256]{2,1,0:T(8,128)S(1)} %copy-done.1), custom_call_target="tpu_custom_call" | custom-call | flops 8589934592 | bytes 1 | tf_op jit(solution)/shard_map/pallas_call | solution.py:223
  43.4 7.8 %collective-permute-done.4.refs_0_ = f32[128,16,256]{2,1,0:T(8,128)} collective-permute-done((f32[128,16,256]{2,1,0:T(8,128)}, f32[128,16,256]{2,1,0:T(8,128)}, u32[]{:S(2)}, u32[]{:S(2)}) %collective-permute-start.4) | collective-permute-done | bytes 2097184 | tf_op jit(solution)/shard_map/ppermute | solution.py:315
  51.2 4.5 %shard_map.56 = f32[16,32,256]{2,1,0:T(8,128)S(1)} custom-call(s32[2]{0:T(128)S(1)} %pad_add_fusion.place_ref, bf16[16,512,256]{2,1,0:T(8,128)(2,1)S(1)} %get-tuple-element.16.high, bf16[16,512,256]{2,1,0:T(8,128)(2,1)S(1)} %get-tuple-element.17.low, f32[512,128]{1,0:T(8,128)S(1)} %get-tuple-element.18.own_ref, f32[128,16,256]{2,1,0:T(8,128)} %collective-permute-done.4.refs_0_), custom_call_target="tpu_custom_call" | custom-call | flops 1610612736 | bytes 8388608 | tf_op jit(solution)/shard_map/pallas_call | solution.py:241
  55.9 1.5 %collective-permute-done.5 = f32[8,32,256]{2,1,0:T(8,128)S(1)} collective-permute-done((f32[8,32,256]{2,1,0:T(8,128)S(1)}, f32[8,32,256]{2,1,0:T(8,128)S(1)}, u32[]{:S(2)}, u32[]{:S(2)}) %collective-permute-start.5) | collective-permute-done | bytes 262176 | tf_op jit(solution)/shard_map/ppermute | solution.py:311
  57.4 1.9 %collective-permute-start.6 = (f32[4,32,256]{2,1,0:T(8,128)S(1)}, f32[4,32,256]{2,1,0:T(8,128)S(1)}, u32[]{:S(2)}, u32[]{:S(2)}) collective-permute-start(f32[4,32,256]{2,1,0:T(8,128)S(1)} %slice.78), channel_id=1, source_target_pairs={{0,4},{2,6},{4,0},{6,2},{8,12},{10,14},{12,8},{14,10},{16,20},{18,... | collective-permute-start | bytes 393224 | tf_op jit(solution)/shard_map/ppermute | solution.py:311
  59.4 1.1 collective-permute-start.10
  60.5 2.7 %collective-permute-done.6 = f32[4,32,256]{2,1,0:T(8,128)S(1)} collective-permute-done((f32[4,32,256]{2,1,0:T(8,128)S(1)}, f32[4,32,256]{2,1,0:T(8,128)S(1)}, u32[]{:S(2)}, u32[]{:S(2)}) %collective-permute-start.6) | collective-permute-done | bytes 131104 | tf_op jit(solution)/shard_map/ppermute | solution.py:311
  63.2 3.9 %collective-permute-start.7 = (f32[1,32,256]{2,1,0:T(8,128)S(1)}, f32[1,32,256]{2,1,0:T(8,128)S(1)}, u32[]{:S(2)}, u32[]{:S(2)}) collective-permute-start(f32[1,32,256]{2,1,0:T(8,128)S(1)} %get-tuple-element.32), channel_id=1, source_target_pairs={{0,24},{2,26},{4,28},{6,30},{8,16},{10,18},{12,20},{14,22},{16,8},... | collective-permute-start | bytes 98312 | tf_op jit(solution)/shard_map/ppermute | solution.py:311
  67.1 0.6 collective-permute-start.9
  67.9 1.5 %collective-permute-done.7 = f32[1,32,256]{2,1,0:T(8,128)S(1)} collective-permute-done((f32[1,32,256]{2,1,0:T(8,128)S(1)}, f32[1,32,256]{2,1,0:T(8,128)S(1)}, u32[]{:S(2)}, u32[]{:S(2)}) %collective-permute-start.7) | collective-permute-done | bytes 32800 | tf_op jit(solution)/shard_map/ppermute | solution.py:311
  69.4 2.5 %collective-permute-done.8 = f32[1,32,256]{2,1,0:T(8,128)S(1)} collective-permute-done((f32[1,32,256]{2,1,0:T(8,128)S(1)}, f32[1,32,256]{2,1,0:T(8,128)S(1)}, u32[]{:S(2)}, u32[]{:S(2)}) %collective-permute-start.8) | collective-permute-done | bytes 32800 | tf_op jit(solution)/shard_map/ppermute | solution.py:311
  72.0 1.1 collective-permute-done.10.sketch_ref
  73.1 1.1 collective-permute-start.11
  74.2 0.9 collective-permute-start.17
  75.1 2.3 %collective-permute-done.11 = f32[1,32,256]{2,1,0:T(8,128)S(1)} collective-permute-done((f32[1,32,256]{2,1,0:T(8,128)S(1)}, f32[1,32,256]{2,1,0:T(8,128)S(1)}, u32[]{:S(2)}, u32[]{:S(2)}) %collective-permute-start.11) | collective-permute-done | bytes 32800 | tf_op jit(solution)/shard_map/ppermute | solution.py:315
  77.4 3.6 %collective-permute-start.12 = (f32[1,2,32,256]{3,2,1,0:T(8,128)S(1)}, f32[1,2,32,256]{3,2,1,0:T(8,128)S(1)}, u32[]{:S(2)}, u32[]{:S(2)}) collective-permute-start(f32[1,2,32,256]{3,2,1,0:T(8,128)S(1)} %maximum_bitcast_fusion), channel_id=1, source_target_pairs={{0,24},{2,26},{4,28},{6,30},{8,16},{10,18},{12,20},{14,22},{16,8},... | collective-permute-start | bytes 196616 | tf_op jit(solution)/shard_map/ppermute | solution.py:311
  81.0 0.8 collective-permute-start.14
  81.8 2.3 %collective-permute-done.12 = f32[1,2,32,256]{3,2,1,0:T(8,128)S(1)} collective-permute-done((f32[1,2,32,256]{3,2,1,0:T(8,128)S(1)}, f32[1,2,32,256]{3,2,1,0:T(8,128)S(1)}, u32[]{:S(2)}, u32[]{:S(2)}) %collective-permute-start.12) | collective-permute-done | bytes 65568 | tf_op jit(solution)/shard_map/ppermute | solution.py:311
  84.0 2.1 %collective-permute-done.13 = f32[1,2,32,256]{3,2,1,0:T(8,128)S(1)} collective-permute-done((f32[1,2,32,256]{3,2,1,0:T(8,128)S(1)}, f32[1,2,32,256]{3,2,1,0:T(8,128)S(1)}, u32[]{:S(2)}, u32[]{:S(2)}) %collective-permute-start.13) | collective-permute-done | bytes 65568 | tf_op jit(solution)/shard_map/ppermute | solution.py:311
  86.8 5.8 %collective-permute-done.15 = f32[4,2,32,256]{3,2,1,0:T(8,128)S(1)} collective-permute-done((f32[4,2,32,256]{3,2,1,0:T(8,128)S(1)}, f32[4,2,32,256]{3,2,1,0:T(8,128)S(1)}, u32[]{:S(2)}, u32[]{:S(2)}) %collective-permute-start.15) | collective-permute-done | bytes 262176 | tf_op jit(solution)/shard_map/ppermute | solution.py:311
  92.7 1.1 shard_map.58.refs_0_
  94.6 17.6 %shard_map.57 = (bf16[16,512,256]{2,1,0:T(8,128)(2,1)S(1)}, bf16[16,512,256]{2,1,0:T(8,128)(2,1)S(1)}) custom-call(f32[512,16,1024]{2,1,0:T(8,128)} %core_hbm.3, s32[2]{0:T(128)S(1)} %pad_add_fusion.place_ref, f32[8,2,32,256]{3,2,1,0:T(8,128)S(1)} %constant_dynamic-update-slice_fusion.refs_0_, f32[8,2,32,256]{3,2,1,0:T(8,128)S(1)} %collective-permute-done.16.refs_1_), custom_call_target="tpu_custom_call" | custom-call | flops 4294967296 | bytes 1 | tf_op jit(solution)/shard_map/pallas_call | solution.py:204
  112.7 4.0 %shard_map.61 = f32[16,32,256]{2,1,0:T(8,128)S(1)} custom-call(s32[2]{0:T(128)S(1)} %pad_add_fusion.place_ref, bf16[16,512,256]{2,1,0:T(8,128)(2,1)S(1)} %get-tuple-element.23.high, bf16[16,512,256]{2,1,0:T(8,128)(2,1)S(1)} %get-tuple-element.24.low, bf16[16,256,256]{2,1,0:T(8,128)(2,1)S(1)} %shard_map.58.refs_0_, ...), custom_call_target="tpu_custom_call" | custom-call | flops 3221225472 | bytes 8388608 | tf_op jit(solution)/shard_map/pallas_call | solution.py:254
  116.9 1.4 collective-permute-done.18
  118.4 0.6 collective-permute-start.19
  119.0 5.0 %collective-permute-done.19 = f32[4,32,256]{2,1,0:T(8,128)S(1)} collective-permute-done((f32[4,32,256]{2,1,0:T(8,128)S(1)}, f32[4,32,256]{2,1,0:T(8,128)S(1)}, u32[]{:S(2)}, u32[]{:S(2)}) %collective-permute-start.19) | collective-permute-done | bytes 131104 | tf_op jit(solution)/shard_map/ppermute | solution.py:311
  124.0 1.7 %collective-permute-start.20 = (f32[1,32,256]{2,1,0:T(8,128)S(1)}, f32[1,32,256]{2,1,0:T(8,128)S(1)}, u32[]{:S(2)}, u32[]{:S(2)}) collective-permute-start(f32[1,32,256]{2,1,0:T(8,128)S(1)} %get-tuple-element.29), channel_id=1, source_target_pairs={{0,24},{2,26},{4,28},{6,30},{8,16},{10,18},{12,20},{14,22},{16,8},... | collective-permute-start | bytes 98312 | tf_op jit(solution)/shard_map/ppermute | solution.py:311
  126.2 2.3 %collective-permute-start.22 = (f32[1,32,256]{2,1,0:T(8,128)S(1)}, f32[1,32,256]{2,1,0:T(8,128)S(1)}, u32[]{:S(2)}, u32[]{:S(2)}) collective-permute-start(f32[1,32,256]{2,1,0:T(8,128)S(1)} %get-tuple-element.30), channel_id=1, source_target_pairs={{0,8},{2,10},{4,12},{6,14},{8,0},{10,2},{12,4},{14,6},{16,24},{18,... | collective-permute-start | bytes 98312 | tf_op jit(solution)/shard_map/ppermute | solution.py:311
  128.5 1.6 %collective-permute-done.20 = f32[1,32,256]{2,1,0:T(8,128)S(1)} collective-permute-done((f32[1,32,256]{2,1,0:T(8,128)S(1)}, f32[1,32,256]{2,1,0:T(8,128)S(1)}, u32[]{:S(2)}, u32[]{:S(2)}) %collective-permute-start.20) | collective-permute-done | bytes 32800 | tf_op jit(solution)/shard_map/ppermute | solution.py:311
  130.8 2.4 %collective-permute-start.23 = (f32[1,32,256]{2,1,0:T(8,128)S(1)}, f32[1,32,256]{2,1,0:T(8,128)S(1)}, u32[]{:S(2)}, u32[]{:S(2)}) collective-permute-start(f32[1,32,256]{2,1,0:T(8,128)S(1)} %get-tuple-element.28), channel_id=1, source_target_pairs={{0,24},{2,26},{4,28},{6,30},{8,16},{10,18},{12,20},{14,22},{16,8},... | collective-permute-start | bytes 98312 | tf_op jit(solution)/shard_map/ppermute | solution.py:311
  133.2 0.8 collective-permute-start.24
  133.9 1.3 collective-permute-start.25
  135.3 1.3 collective-permute-done.23
  136.6 1.5 %collective-permute-done.24 = f32[1,32,256]{2,1,0:T(8,128)S(1)} collective-permute-done((f32[1,32,256]{2,1,0:T(8,128)S(1)}, f32[1,32,256]{2,1,0:T(8,128)S(1)}, u32[]{:S(2)}, u32[]{:S(2)}) %collective-permute-start.24) | collective-permute-done | bytes 32800 | tf_op jit(solution)/shard_map/ppermute | solution.py:311
  138.8 4.4 %collective-permute-done.26 = f32[4,32,256]{2,1,0:T(8,128)S(1)} collective-permute-done((f32[4,32,256]{2,1,0:T(8,128)S(1)}, f32[4,32,256]{2,1,0:T(8,128)S(1)}, u32[]{:S(2)}, u32[]{:S(2)}) %collective-permute-start.26) | collective-permute-done | bytes 131104 | tf_op jit(solution)/shard_map/ppermute | solution.py:311
  143.3 1.5 %collective-permute-done.27.refs_1_ = f32[8,32,256]{2,1,0:T(8,128)S(1)} collective-permute-done((f32[8,32,256]{2,1,0:T(8,128)S(1)}, f32[8,32,256]{2,1,0:T(8,128)S(1)}, u32[]{:S(2)}, u32[]{:S(2)}) %collective-permute-start.27) | collective-permute-done | bytes 262176 | tf_op jit(solution)/shard_map/ppermute | solution.py:311
  144.9 1.4 shard_map.62
  (66 shorter events, 5.7 us)
Async XLA Ops:
  0.8 5.5 %collective-permute-start = (f32[64,256]{1,0:T(8,128)S(1)}, f32[64,256]{1,0:T(8,128)S(1)}, u32[]{:S(2)}, u32[]{:S(2)}) collective-permute-start(f32[64,256]{1,0:T(8,128)S(1)} %constant_dynamic-slice_fusion), channel_id=1, source_target_pairs={{0,1},{1,0},{2,3},{3,2},{4,5},{5,4},{6,7},{7,6},{8,9},{9,8},{10,11... | collective-permute-start | bytes 196616 | tf_op jit(solution)/shard_map/ppermute | solution.py:315
  3.8 47.4 %collective-permute-start.4 = (f32[128,16,256]{2,1,0:T(8,128)}, f32[128,16,256]{2,1,0:T(8,128)}, u32[]{:S(2)}, u32[]{:S(2)}) collective-permute-start(f32[128,16,256]{2,1,0:T(8,128)} %sketch_ref.2), channel_id=1, source_target_pairs={{0,1},{1,0},{2,3},{3,2},{4,5},{5,4},{6,7},{7,6},{8,9},{9,8},{10,11... | collective-permute-start | bytes 6291464 | tf_op jit(solution)/shard_map/ppermute | solution.py:315
  6.3 4.5 %collective-permute-start.1 = (f32[1,64,256]{2,1,0:T(8,128)S(1)}, f32[1,64,256]{2,1,0:T(8,128)S(1)}, u32[]{:S(2)}, u32[]{:S(2)}) collective-permute-start(f32[1,64,256]{2,1,0:T(8,128)S(1)} %bitcast.16), channel_id=1, source_target_pairs={{0,8},{2,10},{4,12},{6,14},{8,0},{10,2},{12,4},{14,6},{16,24},{18,... | collective-permute-start | bytes 196616 | tf_op jit(solution)/shard_map/ppermute | solution.py:311
  10.8 5.0 %collective-permute-start.2 = (f32[2,64,256]{2,1,0:T(8,128)S(1)}, f32[2,64,256]{2,1,0:T(8,128)S(1)}, u32[]{:S(2)}, u32[]{:S(2)}) collective-permute-start(f32[2,64,256]{2,1,0:T(8,128)S(1)} %pad_maximum_fusion.3), channel_id=1, source_target_pairs={{0,4},{2,6},{4,0},{6,2},{8,12},{10,14},{12,8},{14,10},{16,20},{18,... | collective-permute-start | bytes 393224 | tf_op jit(solution)/shard_map/ppermute | solution.py:311
  15.8 5.3 %collective-permute-start.3 = (f32[4,64,256]{2,1,0:T(8,128)S(1)}, f32[4,64,256]{2,1,0:T(8,128)S(1)}, u32[]{:S(2)}, u32[]{:S(2)}) collective-permute-start(f32[4,64,256]{2,1,0:T(8,128)S(1)} %pad_maximum_fusion.1), channel_id=1, source_target_pairs={{0,2},{2,0},{4,6},{6,4},{8,10},{10,8},{12,14},{14,12},{16,18},{18,... | collective-permute-start | bytes 786440 | tf_op jit(solution)/shard_map/ppermute | solution.py:311
  18.9 1.3 copy-start.2
  21.2 2.5 %copy-start.1 = (f32[128,16,256]{2,1,0:T(8,128)S(1)}, f32[128,16,256]{2,1,0:T(8,128)}, u32[]{:S(2)}) copy-start(f32[128,16,256]{2,1,0:T(8,128)} %sketch_ref.2) | copy-start | bytes 6291460
  51.2 8.2 %copy-start.4 = (f32[4,128,256]{2,1,0:T(8,128)S(1)}, f32[4,128,256]{2,1,0:T(8,128)}, u32[]{:S(2)}) copy-start(f32[4,128,256]{2,1,0:T(8,128)} %slice.74) | copy-start | bytes 1572868
  55.7 12.0 %copy-start.3 = (f32[128,16,256]{2,0,1:T(8,128)S(1)}, f32[128,16,256]{2,0,1:T(8,128)}, u32[]{:S(2)}) copy-start(f32[128,16,256]{2,0,1:T(8,128)} %copy-done.2) | copy-start | bytes 6291460
  55.8 1.6 %collective-permute-start.5 = (f32[8,32,256]{2,1,0:T(8,128)S(1)}, f32[8,32,256]{2,1,0:T(8,128)S(1)}, u32[]{:S(2)}, u32[]{:S(2)}) collective-permute-start(f32[8,32,256]{2,1,0:T(8,128)S(1)} %slice.76), channel_id=1, source_target_pairs={{0,2},{2,0},{4,6},{6,4},{8,10},{10,8},{12,14},{14,12},{16,18},{18,... | collective-permute-start | bytes 786440 | tf_op jit(solution)/shard_map/ppermute | solution.py:311
  57.4 5.7 %collective-permute-start.6 = (f32[4,32,256]{2,1,0:T(8,128)S(1)}, f32[4,32,256]{2,1,0:T(8,128)S(1)}, u32[]{:S(2)}, u32[]{:S(2)}) collective-permute-start(f32[4,32,256]{2,1,0:T(8,128)S(1)} %slice.78), channel_id=1, source_target_pairs={{0,4},{2,6},{4,0},{6,2},{8,12},{10,14},{12,8},{14,10},{16,20},{18,... | collective-permute-start | bytes 393224 | tf_op jit(solution)/shard_map/ppermute | solution.py:311
  59.4 13.7 %collective-permute-start.10 = (f32[4,128,256]{2,1,0:T(8,128)S(1)}, f32[4,128,256]{2,1,0:T(8,128)S(1)}, u32[]{:S(2)}, u32[]{:S(2)}) collective-permute-start(f32[4,128,256]{2,1,0:T(8,128)S(1)} %copy-done.4), channel_id=1, source_target_pairs={{0,1},{1,0},{2,3},{3,2},{4,5},{5,4},{6,7},{7,6},{8,9},{9,8},{10,11... | collective-permute-start | bytes 1572872 | tf_op jit(solution)/shard_map/ppermute | solution.py:315
  63.2 6.2 %collective-permute-start.7 = (f32[1,32,256]{2,1,0:T(8,128)S(1)}, f32[1,32,256]{2,1,0:T(8,128)S(1)}, u32[]{:S(2)}, u32[]{:S(2)}) collective-permute-start(f32[1,32,256]{2,1,0:T(8,128)S(1)} %get-tuple-element.32), channel_id=1, source_target_pairs={{0,24},{2,26},{4,28},{6,30},{8,16},{10,18},{12,20},{14,22},{16,8},... | collective-permute-start | bytes 98312 | tf_op jit(solution)/shard_map/ppermute | solution.py:311
  67.1 4.8 %collective-permute-start.8 = (f32[1,32,256]{2,1,0:T(8,128)S(1)}, f32[1,32,256]{2,1,0:T(8,128)S(1)}, u32[]{:S(2)}, u32[]{:S(2)}) collective-permute-start(f32[1,32,256]{2,1,0:T(8,128)S(1)} %get-tuple-element.34), channel_id=1, source_target_pairs={{0,16},{2,18},{4,20},{6,22},{8,24},{10,26},{12,28},{14,30},{16,0},... | collective-permute-start | bytes 98312 | tf_op jit(solution)/shard_map/ppermute | solution.py:311
  67.1 25.6 %copy-start = (f32[128,16,256]{2,1,0:T(8,128)S(1)}, f32[128,16,256]{2,1,0:T(8,128)}, u32[]{:S(2)}) copy-start(f32[128,16,256]{2,1,0:T(8,128)} %sketch_ref.3) | copy-start | bytes 6291460
  67.1 4.8 %collective-permute-start.9 = (f32[1,32,256]{2,1,0:T(8,128)S(1)}, f32[1,32,256]{2,1,0:T(8,128)S(1)}, u32[]{:S(2)}, u32[]{:S(2)}) collective-permute-start(f32[1,32,256]{2,1,0:T(8,128)S(1)} %get-tuple-element.33), channel_id=1, source_target_pairs={{0,8},{2,10},{4,12},{6,14},{8,0},{10,2},{12,4},{14,6},{16,24},{18,... | collective-permute-start | bytes 98312 | tf_op jit(solution)/shard_map/ppermute | solution.py:311
  73.1 4.3 %collective-permute-start.11 = (f32[1,32,256]{2,1,0:T(8,128)S(1)}, f32[1,32,256]{2,1,0:T(8,128)S(1)}, u32[]{:S(2)}, u32[]{:S(2)}) collective-permute-start(f32[1,32,256]{2,1,0:T(8,128)S(1)} %fusion.6), channel_id=1, source_target_pairs={{0,1},{1,0},{2,3},{3,2},{4,5},{5,4},{6,7},{7,6},{8,9},{9,8},{10,11... | collective-permute-start | bytes 98312 | tf_op jit(solution)/shard_map/ppermute | solution.py:315
  74.2 38.0 %collective-permute-start.17 = (f32[12,128,256]{2,1,0:T(8,128)S(1)}, f32[12,128,256]{2,1,0:T(8,128)S(1)}, u32[]{:S(2)}, u32[]{:S(2)}) collective-permute-start(f32[12,128,256]{2,1,0:T(8,128)S(1)} %slice.83), channel_id=1, source_target_pairs={{0,1},{1,0},{2,3},{3,2},{4,5},{5,4},{6,7},{7,6},{8,9},{9,8},{10,11... | collective-permute-start | bytes 4718600 | tf_op jit(solution)/shard_map/ppermute | solution.py:315
  77.4 6.7 %collective-permute-start.12 = (f32[1,2,32,256]{3,2,1,0:T(8,128)S(1)}, f32[1,2,32,256]{3,2,1,0:T(8,128)S(1)}, u32[]{:S(2)}, u32[]{:S(2)}) collective-permute-start(f32[1,2,32,256]{3,2,1,0:T(8,128)S(1)} %maximum_bitcast_fusion), channel_id=1, source_target_pairs={{0,24},{2,26},{4,28},{6,30},{8,16},{10,18},{12,20},{14,22},{16,8},... | collective-permute-start | bytes 196616 | tf_op jit(solution)/shard_map/ppermute | solution.py:311
  81.0 5.2 %collective-permute-start.13 = (f32[1,2,32,256]{3,2,1,0:T(8,128)S(1)}, f32[1,2,32,256]{3,2,1,0:T(8,128)S(1)}, u32[]{:S(2)}, u32[]{:S(2)}) collective-permute-start(f32[1,2,32,256]{3,2,1,0:T(8,128)S(1)} %maximum_bitcast_fusion), channel_id=1, source_target_pairs={{0,16},{2,18},{4,20},{6,22},{8,24},{10,26},{12,28},{14,30},{16,0},... | collective-permute-start | bytes 196616 | tf_op jit(solution)/shard_map/ppermute | solution.py:311
  81.0 5.2 %collective-permute-start.14 = (f32[1,2,32,256]{3,2,1,0:T(8,128)S(1)}, f32[1,2,32,256]{3,2,1,0:T(8,128)S(1)}, u32[]{:S(2)}, u32[]{:S(2)}) collective-permute-start(f32[1,2,32,256]{3,2,1,0:T(8,128)S(1)} %maximum_bitcast_fusion), channel_id=1, source_target_pairs={{0,8},{2,10},{4,12},{6,14},{8,0},{10,2},{12,4},{14,6},{16,24},{18,... | collective-permute-start | bytes 196616 | tf_op jit(solution)/shard_map/ppermute | solution.py:311
  86.1 6.4 %collective-permute-start.15 = (f32[4,2,32,256]{3,2,1,0:T(8,128)S(1)}, f32[4,2,32,256]{3,2,1,0:T(8,128)S(1)}, u32[]{:S(2)}, u32[]{:S(2)}) collective-permute-start(f32[4,2,32,256]{3,2,1,0:T(8,128)S(1)} %pad_maximum_fusion.2), channel_id=1, source_target_pairs={{0,4},{2,6},{4,0},{6,2},{8,12},{10,14},{12,8},{14,10},{16,20},{18,... | collective-permute-start | bytes 786440 | tf_op jit(solution)/shard_map/ppermute | solution.py:311
  92.6 2.0 %collective-permute-start.16 = (f32[8,2,32,256]{3,2,1,0:T(8,128)S(1)}, f32[8,2,32,256]{3,2,1,0:T(8,128)S(1)}, u32[]{:S(2)}, u32[]{:S(2)}) collective-permute-start(f32[8,2,32,256]{3,2,1,0:T(8,128)S(1)} %constant_dynamic-update-slice_fusion.refs_0_), channel_id=1, source_target_pairs={{0,2},{2,0},{4,6},{6,4},{8,10},{10,8},{12,14},{14,12},{16,18},{18,... | collective-permute-start | bytes 1572872 | tf_op jit(solution)/shard_map/ppermute | solution.py:311
  116.7 1.6 %collective-permute-start.18 = (f32[8,32,256]{2,1,0:T(8,128)S(1)}, f32[8,32,256]{2,1,0:T(8,128)S(1)}, u32[]{:S(2)}, u32[]{:S(2)}) collective-permute-start(f32[8,32,256]{2,1,0:T(8,128)S(1)} %slice.85), channel_id=1, source_target_pairs={{0,2},{2,0},{4,6},{6,4},{8,10},{10,8},{12,14},{14,12},{16,18},{18,... | collective-permute-start | bytes 786440 | tf_op jit(solution)/shard_map/ppermute | solution.py:311
  118.4 5.6 %collective-permute-start.19 = (f32[4,32,256]{2,1,0:T(8,128)S(1)}, f32[4,32,256]{2,1,0:T(8,128)S(1)}, u32[]{:S(2)}, u32[]{:S(2)}) collective-permute-start(f32[4,32,256]{2,1,0:T(8,128)S(1)} %slice.87), channel_id=1, source_target_pairs={{0,4},{2,6},{4,0},{6,2},{8,12},{10,14},{12,8},{14,10},{16,20},{18,... | collective-permute-start | bytes 393224 | tf_op jit(solution)/shard_map/ppermute | solution.py:311
  124.0 6.1 %collective-permute-start.20 = (f32[1,32,256]{2,1,0:T(8,128)S(1)}, f32[1,32,256]{2,1,0:T(8,128)S(1)}, u32[]{:S(2)}, u32[]{:S(2)}) collective-permute-start(f32[1,32,256]{2,1,0:T(8,128)S(1)} %get-tuple-element.29), channel_id=1, source_target_pairs={{0,24},{2,26},{4,28},{6,30},{8,16},{10,18},{12,20},{14,22},{16,8},... | collective-permute-start | bytes 98312 | tf_op jit(solution)/shard_map/ppermute | solution.py:311
  125.7 4.9 %collective-permute-start.21 = (f32[1,32,256]{2,1,0:T(8,128)S(1)}, f32[1,32,256]{2,1,0:T(8,128)S(1)}, u32[]{:S(2)}, u32[]{:S(2)}) collective-permute-start(f32[1,32,256]{2,1,0:T(8,128)S(1)} %get-tuple-element.31), channel_id=1, source_target_pairs={{0,16},{2,18},{4,20},{6,22},{8,24},{10,26},{12,28},{14,30},{16,0},... | collective-permute-start | bytes 98312 | tf_op jit(solution)/shard_map/ppermute | solution.py:311
  126.2 4.6 %collective-permute-start.22 = (f32[1,32,256]{2,1,0:T(8,128)S(1)}, f32[1,32,256]{2,1,0:T(8,128)S(1)}, u32[]{:S(2)}, u32[]{:S(2)}) collective-permute-start(f32[1,32,256]{2,1,0:T(8,128)S(1)} %get-tuple-element.30), channel_id=1, source_target_pairs={{0,8},{2,10},{4,12},{6,14},{8,0},{10,2},{12,4},{14,6},{16,24},{18,... | collective-permute-start | bytes 98312 | tf_op jit(solution)/shard_map/ppermute | solution.py:311
  130.8 5.8 %collective-permute-start.23 = (f32[1,32,256]{2,1,0:T(8,128)S(1)}, f32[1,32,256]{2,1,0:T(8,128)S(1)}, u32[]{:S(2)}, u32[]{:S(2)}) collective-permute-start(f32[1,32,256]{2,1,0:T(8,128)S(1)} %get-tuple-element.28), channel_id=1, source_target_pairs={{0,24},{2,26},{4,28},{6,30},{8,16},{10,18},{12,20},{14,22},{16,8},... | collective-permute-start | bytes 98312 | tf_op jit(solution)/shard_map/ppermute | solution.py:311
  133.2 4.9 %collective-permute-start.24 = (f32[1,32,256]{2,1,0:T(8,128)S(1)}, f32[1,32,256]{2,1,0:T(8,128)S(1)}, u32[]{:S(2)}, u32[]{:S(2)}) collective-permute-start(f32[1,32,256]{2,1,0:T(8,128)S(1)} %get-tuple-element.28), channel_id=1, source_target_pairs={{0,16},{2,18},{4,20},{6,22},{8,24},{10,26},{12,28},{14,30},{16,0},... | collective-permute-start | bytes 98312 | tf_op jit(solution)/shard_map/ppermute | solution.py:311
  133.9 4.3 %collective-permute-start.25 = (f32[1,32,256]{2,1,0:T(8,128)S(1)}, f32[1,32,256]{2,1,0:T(8,128)S(1)}, u32[]{:S(2)}, u32[]{:S(2)}) collective-permute-start(f32[1,32,256]{2,1,0:T(8,128)S(1)} %get-tuple-element.28), channel_id=1, source_target_pairs={{0,8},{2,10},{4,12},{6,14},{8,0},{10,2},{12,4},{14,6},{16,24},{18,... | collective-permute-start | bytes 98312 | tf_op jit(solution)/shard_map/ppermute | solution.py:311
  138.2 5.0 %collective-permute-start.26 = (f32[4,32,256]{2,1,0:T(8,128)S(1)}, f32[4,32,256]{2,1,0:T(8,128)S(1)}, u32[]{:S(2)}, u32[]{:S(2)}) collective-permute-start(f32[4,32,256]{2,1,0:T(8,128)S(1)} %pad_maximum_fusion.4), channel_id=1, source_target_pairs={{0,4},{2,6},{4,0},{6,2},{8,12},{10,14},{12,8},{14,10},{16,20},{18,... | collective-permute-start | bytes 393224 | tf_op jit(solution)/shard_map/ppermute | solution.py:311
  143.3 1.6 %collective-permute-start.27 = (f32[8,32,256]{2,1,0:T(8,128)S(1)}, f32[8,32,256]{2,1,0:T(8,128)S(1)}, u32[]{:S(2)}, u32[]{:S(2)}) collective-permute-start(f32[8,32,256]{2,1,0:T(8,128)S(1)} %constant_dynamic-update-slice_fusion.5.refs_0_), channel_id=1, source_target_pairs={{0,2},{2,0},{4,6},{6,4},{8,10},{10,8},{12,14},{14,12},{16,18},{18,... | collective-permute-start | bytes 786440 | tf_op jit(solution)/shard_map/ppermute | solution.py:311

commit v5 on v4

--- a/solution.py
+++ b/solution.py
@@ -57,7 +57,9 @@
         for copy in copies(k):
             copy.wait()
         h, l = halves(buf[lax.rem(k, slots)])
-        h, l = halves(dot(jnp.concatenate([h, h, l], axis=1), weights[...]))
+        both = dot(h, weights[...])
+        columns = both.shape[1] // 2
+        h, l = halves(both[:, :columns] + both[:, columns:] + dot(l, weights[:, :columns]))
         for u in range(width):
             high[k * width + u] = h[u * rows : (u + 1) * rows]
             low[k * width + u] = l[u * rows : (u + 1) * rows]
@@ -67,11 +69,8 @@
 
 
 def spread_whole(carried_ref, weights):
-    depth = carried_ref.shape[0]
-    h, l = halves(carried_ref[...])
-    weights[0:depth] = h
-    weights[depth : 2 * depth] = l
-    weights[2 * depth :] = h
+    columns = carried_ref.shape[1]
+    weights[:, :columns], weights[:, columns:] = halves(carried_ref[...])
 
 
 def first_kernel(core_hbm, carried_ref, sketch_ref, high, low, out, prepared, *scratch):
@@ -88,7 +87,7 @@
 def spread_pieces(ranks, place_ref, parts, weights):
     own, rank = place_ref[0], place_ref[1]
     _, _, rows, columns = parts[0].shape
-    depth, width = weights.shape[0] // 3, columns // ranks
+    depth, width = weights.shape[0], columns // ranks
     position = 0
     for part in parts:
         for p in range(part.shape[0]):
@@ -96,11 +95,10 @@
                 source = lax.rem(rank - d + ranks, ranks)
                 at = pl.multiple_of(source * (depth // ranks) + (own ^ position) * rows, rows)
                 for e in range(ranks):
-                    to = pl.ds(pl.multiple_of(lax.rem(source - e + ranks, ranks) * width, width), width)
+                    to = pl.multiple_of(lax.rem(source - e + ranks, ranks) * width, width)
                     h, l = halves(part[p, d, :, e * width : (e + 1) * width])
-                    weights[pl.ds(at, rows), to] = h
-                    weights[pl.ds(at + depth, rows), to] = l
-                    weights[pl.ds(at + 2 * depth, rows), to] = h
+                    weights[pl.ds(at, rows), pl.ds(to, width)] = h
+                    weights[pl.ds(at, rows), pl.ds(to + columns, width)] = l
             position += 1
 
 
@@ -177,7 +175,7 @@
     return [
         pltpu.VMEM((SLOTS, width * rows, depth), F32),
         pltpu.SemaphoreType.DMA((SLOTS, width)),
-        pltpu.VMEM((3 * depth, columns), BF16),
+        pltpu.VMEM((depth, 2 * columns), BF16),
     ]
 
 
@@ -227,7 +225,7 @@
         out_specs=(VMEM,) * 3,
         scratch_shapes=[pltpu.VMEM((slices, depth, 2 * size), BF16)] + loop_scratch(core, columns),
         compiler_params=limit(36),
-        cost_estimate=cost(4 * core.size * columns, 1),
+        cost_estimate=cost(28 * core.size * columns // 8, 1),
     )(core, carried, sketch)
 
 
@@ -345,7 +343,7 @@
 
 
 def part_groups(modes):
-    return [(low, 1) for low in range(min(3, modes.bit_length() - 1))]
+    return [(low, 1) for low in range(min(4, modes.bit_length() - 1))]
 
 
 def own_part(x, modes, mode):

time: 146 us -> 146 us (level)
  waiting for transfers between devices: 55.5 us -> 50.2 us
  local copies, waits for them, and re-layouts: 6.81 us -> 11.2 us
  starting transfers between devices: 32.4 us -> 33.9 us
    ppermute x5, waiting for transfers between devices: 13.6 us -> 6.97 us  [shift(): return lax.ppermute(x, 'rank', [(i, (i + d) % ranks) for i in range(ranks)])]
    unnamed x17 -> x23, local copies, waits for them, and re-layouts: 4.19 us -> 6.75 us
    ppermute x23 -> x24, starting transfers between devices: 26.3 us -> 28 us  [partner(): return lax.ppermute(x, 'mode', [(i, i ^ distance) for i in range(count)])]
    ppermute x23 -> x24, waiting for transfers between devices: 41.9 us -> 43.2 us  [partner(): return lax.ppermute(x, 'mode', [(i, i ^ distance) for i in range(count)])]
  transfers between devices with their start and end apart: 28 -> 29, of which waited for: 24 -> 24; matrix products, arithmetic and copies ran while one was open for 5% -> 7% of each run, Pallas kernels for 26% -> 26%
where the time goes in v5:
time: 146 us
  waiting for transfers between devices  50.2 us (34%)
  Pallas kernels  48.8 us (33%)
  starting transfers between devices  33.9 us (23%)
  local copies, waits for them, and re-layouts  11.2 us (8%)
    ppermute x24, waiting for transfers between devices, partner(): return lax.ppermute(x, 'mode', [(i, i ^ distance) for i in range(count)])  43.2 us
    ppermute x24, starting transfers between devices, partner(): return lax.ppermute(x, 'mode', [(i, i ^ distance) for i in range(count)])  28 us
    pallas_call x1, Pallas kernels, first_step(): pl.pallas_call(first_kernel, out_shape=(out, out, jax.ShapeDtypeStruct((c...  19.6 us
    pallas_call x1, Pallas kernels, hidden(): pl.pallas_call(kernel, out_shape=(out, out), in_specs=[HBM] + ([VMEM] if...  17.6 us
    ppermute x5, waiting for transfers between devices, shift(): return lax.ppermute(x, 'rank', [(i, (i + d) % ranks) for i in range(ranks)])  6.97 us
    unnamed x23, local copies, waits for them, and re-layouts  6.75 us
    ppermute x5, starting transfers between devices, shift(): return lax.ppermute(x, 'rank', [(i, (i + d) % ranks) for i in range(ranks)])  5.85 us
    pallas_call x1, Pallas kernels, second_product(): pl.pallas_call(second_kernel, out_shape=out_shape(rows, columns, count),...  4.51 us
  transfers between devices with their start and end apart: 29, of which 24 were waited for; matrix products, arithmetic and copies ran while one was open for 7% of the time, Pallas kernels for 26%

profile of v5, /device:TPU:0, one launch (start us, length us, event | category | flops | bytes accessed | tf_op | source)
XLA Modules:
  0.0 145.8 jit_solution(11164268955273690212)
XLA Ops:
  0.8 3.0 %collective-permute-start = (f32[32,256]{1,0:T(8,128)S(1)}, f32[32,256]{1,0:T(8,128)S(1)}, u32[]{:S(2)}, u32[]{:S(2)}) collective-permute-start(f32[32,256]{1,0:T(8,128)S(1)} %constant_dynamic-slice_fusion), channel_id=1, source_target_pairs={{0,1},{1,0},{2,3},{3,2},{4,5},{5,4},{6,7},{7,6},{8,9},{9,8},{10,11... | collective-permute-start | bytes 98312 | tf_op jit(solution)/shard_map/ppermute | solution.py:313
  3.8 1.8 %collective-permute-done = f32[32,256]{1,0:T(8,128)S(1)} collective-permute-done((f32[32,256]{1,0:T(8,128)S(1)}, f32[32,256]{1,0:T(8,128)S(1)}, u32[]{:S(2)}, u32[]{:S(2)}) %collective-permute-start) | collective-permute-done | bytes 32800 | tf_op jit(solution)/shard_map/ppermute | solution.py:313
  5.6 3.1 %collective-permute-start.1 = (f32[1,32,256]{2,1,0:T(8,128)S(1)}, f32[1,32,256]{2,1,0:T(8,128)S(1)}, u32[]{:S(2)}, u32[]{:S(2)}) collective-permute-start(f32[1,32,256]{2,1,0:T(8,128)S(1)} %bitcast.17), channel_id=1, source_target_pairs={{0,16},{2,18},{4,20},{6,22},{8,24},{10,26},{12,28},{14,30},{16,0},... | collective-permute-start | bytes 98312 | tf_op jit(solution)/shard_map/ppermute | solution.py:309
  8.9 2.8 %copy.8 = f32[128,16,256]{2,0,1:T(8,128)S(1)} copy(f32[128,16,256]{2,1,0:T(8,128)} %sketch_ref.3) | data formatting | bytes 4194304 | tf_op args[3]
  11.7 1.4 copy-done.2
  13.1 0.8 slice.74
  13.9 1.6 %collective-permute-start.2 = (f32[2,32,256]{2,1,0:T(8,128)S(1)}, f32[2,32,256]{2,1,0:T(8,128)S(1)}, u32[]{:S(2)}, u32[]{:S(2)}) collective-permute-start(f32[2,32,256]{2,1,0:T(8,128)S(1)} %pad_maximum_fusion.4), channel_id=1, source_target_pairs={{0,8},{2,10},{4,12},{6,14},{8,0},{10,2},{12,4},{14,6},{16,24},{18,... | collective-permute-start | bytes 196616 | tf_op jit(solution)/shard_map/ppermute | solution.py:309
  15.7 2.6 %collective-permute-done.2 = f32[2,32,256]{2,1,0:T(8,128)S(1)} collective-permute-done((f32[2,32,256]{2,1,0:T(8,128)S(1)}, f32[2,32,256]{2,1,0:T(8,128)S(1)}, u32[]{:S(2)}, u32[]{:S(2)}) %collective-permute-start.2) | collective-permute-done | bytes 65568 | tf_op jit(solution)/shard_map/ppermute | solution.py:309
  18.3 1.6 %collective-permute-start.3 = (f32[4,32,256]{2,1,0:T(8,128)S(1)}, f32[4,32,256]{2,1,0:T(8,128)S(1)}, u32[]{:S(2)}, u32[]{:S(2)}) collective-permute-start(f32[4,32,256]{2,1,0:T(8,128)S(1)} %pad_maximum_fusion.2), channel_id=1, source_target_pairs={{0,4},{2,6},{4,0},{6,2},{8,12},{10,14},{12,8},{14,10},{16,20},{18,... | collective-permute-start | bytes 393224 | tf_op jit(solution)/shard_map/ppermute | solution.py:309
  20.5 2.9 %collective-permute-done.3 = f32[4,32,256]{2,1,0:T(8,128)S(1)} collective-permute-done((f32[4,32,256]{2,1,0:T(8,128)S(1)}, f32[4,32,256]{2,1,0:T(8,128)S(1)}, u32[]{:S(2)}, u32[]{:S(2)}) %collective-permute-start.3) | collective-permute-done | bytes 131104 | tf_op jit(solution)/shard_map/ppermute | solution.py:309
  26.1 1.8 %gather_fusion = f32[16,32,256]{2,1,0:T(8,128)S(1)} fusion(f32[16,32,256]{2,1,0:T(8,128)} %constant_dynamic-update-slice_fusion, s32[1024]{0:T(1024)S(1)} %pad_clamp_fusion), kind=kCustom, calls=%fused_computation | custom fusion | bytes 1048640 | tf_op jit(solution)/shard_map/jit(_take)/gather | solution.py:337
  28.0 1.0 fusion.2.carried_ref
  29.0 19.6 %shard_map.55 = (bf16[16,512,256]{2,1,0:T(8,128)(2,1)S(1)}, bf16[16,512,256]{2,1,0:T(8,128)(2,1)S(1)}, f32[512,128]{1,0:T(8,128)S(1)}) custom-call(f32[512,16,1024]{2,1,0:T(8,128)} %core_hbm.2, f32[1024,256]{1,0:T(8,128)S(1)} %fusion.2.carried_ref, f32[128,16,256]{2,1,0:T(8,128)S(1)} %copy-done.1), custom_call_target="tpu_custom_call" | custom-call | flops 7516192768 | bytes 1 | tf_op jit(solution)/shard_map/pallas_call | solution.py:221
  48.6 2.5 %collective-permute-done.5.refs_0_ = f32[128,16,256]{2,1,0:T(8,128)} collective-permute-done((f32[128,16,256]{2,1,0:T(8,128)}, f32[128,16,256]{2,1,0:T(8,128)}, u32[]{:S(2)}, u32[]{:S(2)}) %collective-permute-start.5) | collective-permute-done | bytes 2097184 | tf_op jit(solution)/shard_map/ppermute | solution.py:313
  51.1 4.5 %shard_map.56 = f32[16,32,256]{2,1,0:T(8,128)S(1)} custom-call(s32[2]{0:T(128)S(1)} %pad_add_fusion.place_ref, bf16[16,512,256]{2,1,0:T(8,128)(2,1)S(1)} %get-tuple-element.16.high, bf16[16,512,256]{2,1,0:T(8,128)(2,1)S(1)} %get-tuple-element.17.low, f32[512,128]{1,0:T(8,128)S(1)} %get-tuple-element.18.own_ref, f32[128,16,256]{2,1,0:T(8,128)} %collective-permute-done.5.refs_0_), custom_call_target="tpu_custom_call" | custom-call | flops 1610612736 | bytes 8388608 | tf_op jit(solution)/shard_map/pallas_call | solution.py:239
  55.8 1.5 %collective-permute-done.6 = f32[8,32,256]{2,1,0:T(8,128)S(1)} collective-permute-done((f32[8,32,256]{2,1,0:T(8,128)S(1)}, f32[8,32,256]{2,1,0:T(8,128)S(1)}, u32[]{:S(2)}, u32[]{:S(2)}) %collective-permute-start.6) | collective-permute-done | bytes 262176 | tf_op jit(solution)/shard_map/ppermute | solution.py:309
  57.3 1.6 %collective-permute-start.7 = (f32[4,32,256]{2,1,0:T(8,128)S(1)}, f32[4,32,256]{2,1,0:T(8,128)S(1)}, u32[]{:S(2)}, u32[]{:S(2)}) collective-permute-start(f32[4,32,256]{2,1,0:T(8,128)S(1)} %slice.78), channel_id=1, source_target_pairs={{0,4},{2,6},{4,0},{6,2},{8,12},{10,14},{12,8},{14,10},{16,20},{18,... | collective-permute-start | bytes 393224 | tf_op jit(solution)/shard_map/ppermute | solution.py:309
  58.9 0.8 collective-permute-start.11
  59.8 3.2 %collective-permute-done.7 = f32[4,32,256]{2,1,0:T(8,128)S(1)} collective-permute-done((f32[4,32,256]{2,1,0:T(8,128)S(1)}, f32[4,32,256]{2,1,0:T(8,128)S(1)}, u32[]{:S(2)}, u32[]{:S(2)}) %collective-permute-start.7) | collective-permute-done | bytes 131104 | tf_op jit(solution)/shard_map/ppermute | solution.py:309
  63.0 1.7 %collective-permute-start.10 = (f32[1,32,256]{2,1,0:T(8,128)S(1)}, f32[1,32,256]{2,1,0:T(8,128)S(1)}, u32[]{:S(2)}, u32[]{:S(2)}) collective-permute-start(f32[1,32,256]{2,1,0:T(8,128)S(1)} %get-tuple-element.33), channel_id=1, source_target_pairs={{0,8},{2,10},{4,12},{6,14},{8,0},{10,2},{12,4},{14,6},{16,24},{18,... | collective-permute-start | bytes 98312 | tf_op jit(solution)/shard_map/ppermute | solution.py:309
  64.7 2.5 %collective-permute-start.8 = (f32[1,32,256]{2,1,0:T(8,128)S(1)}, f32[1,32,256]{2,1,0:T(8,128)S(1)}, u32[]{:S(2)}, u32[]{:S(2)}) collective-permute-start(f32[1,32,256]{2,1,0:T(8,128)S(1)} %get-tuple-element.32), channel_id=1, source_target_pairs={{0,24},{2,26},{4,28},{6,30},{8,16},{10,18},{12,20},{14,22},{16,8},... | collective-permute-start | bytes 98312 | tf_op jit(solution)/shard_map/ppermute | solution.py:309
  67.4 3.0 %collective-permute-done.8 = f32[1,32,256]{2,1,0:T(8,128)S(1)} collective-permute-done((f32[1,32,256]{2,1,0:T(8,128)S(1)}, f32[1,32,256]{2,1,0:T(8,128)S(1)}, u32[]{:S(2)}, u32[]{:S(2)}) %collective-permute-start.8) | collective-permute-done | bytes 32800 | tf_op jit(solution)/shard_map/ppermute | solution.py:309
  70.4 1.9 %collective-permute-done.9 = f32[1,32,256]{2,1,0:T(8,128)S(1)} collective-permute-done((f32[1,32,256]{2,1,0:T(8,128)S(1)}, f32[1,32,256]{2,1,0:T(8,128)S(1)}, u32[]{:S(2)}, u32[]{:S(2)}) %collective-permute-start.9) | collective-permute-done | bytes 32800 | tf_op jit(solution)/shard_map/ppermute | solution.py:309
  72.6 0.8 collective-permute-start.12
  73.5 1.2 collective-permute-start.18
  74.7 2.3 %collective-permute-done.12 = f32[1,32,256]{2,1,0:T(8,128)S(1)} collective-permute-done((f32[1,32,256]{2,1,0:T(8,128)S(1)}, f32[1,32,256]{2,1,0:T(8,128)S(1)}, u32[]{:S(2)}, u32[]{:S(2)}) %collective-permute-start.12) | collective-permute-done | bytes 32800 | tf_op jit(solution)/shard_map/ppermute | solution.py:313
  77.0 3.6 %collective-permute-start.13 = (f32[1,2,32,256]{3,2,1,0:T(8,128)S(1)}, f32[1,2,32,256]{3,2,1,0:T(8,128)S(1)}, u32[]{:S(2)}, u32[]{:S(2)}) collective-permute-start(f32[1,2,32,256]{3,2,1,0:T(8,128)S(1)} %maximum_bitcast_fusion), channel_id=1, source_target_pairs={{0,24},{2,26},{4,28},{6,30},{8,16},{10,18},{12,20},{14,22},{16,8},... | collective-permute-start | bytes 196616 | tf_op jit(solution)/shard_map/ppermute | solution.py:309
  80.6 0.8 collective-permute-start.15
  81.4 2.3 %collective-permute-done.13 = f32[1,2,32,256]{3,2,1,0:T(8,128)S(1)} collective-permute-done((f32[1,2,32,256]{3,2,1,0:T(8,128)S(1)}, f32[1,2,32,256]{3,2,1,0:T(8,128)S(1)}, u32[]{:S(2)}, u32[]{:S(2)}) %collective-permute-start.13) | collective-permute-done | bytes 65568 | tf_op jit(solution)/shard_map/ppermute | solution.py:309
  83.7 2.1 %collective-permute-done.14 = f32[1,2,32,256]{3,2,1,0:T(8,128)S(1)} collective-permute-done((f32[1,2,32,256]{3,2,1,0:T(8,128)S(1)}, f32[1,2,32,256]{3,2,1,0:T(8,128)S(1)}, u32[]{:S(2)}, u32[]{:S(2)}) %collective-permute-start.14) | collective-permute-done | bytes 65568 | tf_op jit(solution)/shard_map/ppermute | solution.py:309
  86.4 5.8 %collective-permute-done.16 = f32[4,2,32,256]{3,2,1,0:T(8,128)S(1)} collective-permute-done((f32[4,2,32,256]{3,2,1,0:T(8,128)S(1)}, f32[4,2,32,256]{3,2,1,0:T(8,128)S(1)}, u32[]{:S(2)}, u32[]{:S(2)}) %collective-permute-start.16) | collective-permute-done | bytes 262176 | tf_op jit(solution)/shard_map/ppermute | solution.py:309
  92.3 1.1 shard_map.58.refs_0_
  94.2 17.6 %shard_map.57 = (bf16[16,512,256]{2,1,0:T(8,128)(2,1)S(1)}, bf16[16,512,256]{2,1,0:T(8,128)(2,1)S(1)}) custom-call(f32[512,16,1024]{2,1,0:T(8,128)} %core_hbm.3, s32[2]{0:T(128)S(1)} %pad_add_fusion.place_ref, f32[8,2,32,256]{3,2,1,0:T(8,128)S(1)} %constant_dynamic-update-slice_fusion.5.refs_0_, f32[8,2,32,256]{3,2,1,0:T(8,128)S(1)} %collective-permute-done.17.refs_1_), custom_call_target="tpu_custom_call" | custom-call | flops 4294967296 | bytes 1 | tf_op jit(solution)/shard_map/pallas_call | solution.py:202
  112.3 4.0 %shard_map.61 = f32[16,32,256]{2,1,0:T(8,128)S(1)} custom-call(s32[2]{0:T(128)S(1)} %pad_add_fusion.place_ref, bf16[16,512,256]{2,1,0:T(8,128)(2,1)S(1)} %get-tuple-element.23.high, bf16[16,512,256]{2,1,0:T(8,128)(2,1)S(1)} %get-tuple-element.24.low, bf16[16,256,256]{2,1,0:T(8,128)(2,1)S(1)} %shard_map.58.refs_0_, ...), custom_call_target="tpu_custom_call" | custom-call | flops 3221225472 | bytes 8388608 | tf_op jit(solution)/shard_map/pallas_call | solution.py:252
  116.5 1.4 collective-permute-done.19
  118.5 5.0 %collective-permute-done.20 = f32[4,32,256]{2,1,0:T(8,128)S(1)} collective-permute-done((f32[4,32,256]{2,1,0:T(8,128)S(1)}, f32[4,32,256]{2,1,0:T(8,128)S(1)}, u32[]{:S(2)}, u32[]{:S(2)}) %collective-permute-start.20) | collective-permute-done | bytes 131104 | tf_op jit(solution)/shard_map/ppermute | solution.py:309
  123.6 1.7 %collective-permute-start.21 = (f32[1,32,256]{2,1,0:T(8,128)S(1)}, f32[1,32,256]{2,1,0:T(8,128)S(1)}, u32[]{:S(2)}, u32[]{:S(2)}) collective-permute-start(f32[1,32,256]{2,1,0:T(8,128)S(1)} %get-tuple-element.29), channel_id=1, source_target_pairs={{0,24},{2,26},{4,28},{6,30},{8,16},{10,18},{12,20},{14,22},{16,8},... | collective-permute-start | bytes 98312 | tf_op jit(solution)/shard_map/ppermute | solution.py:309
  125.8 2.3 %collective-permute-start.23 = (f32[1,32,256]{2,1,0:T(8,128)S(1)}, f32[1,32,256]{2,1,0:T(8,128)S(1)}, u32[]{:S(2)}, u32[]{:S(2)}) collective-permute-start(f32[1,32,256]{2,1,0:T(8,128)S(1)} %get-tuple-element.30), channel_id=1, source_target_pairs={{0,8},{2,10},{4,12},{6,14},{8,0},{10,2},{12,4},{14,6},{16,24},{18,... | collective-permute-start | bytes 98312 | tf_op jit(solution)/shard_map/ppermute | solution.py:309
  128.0 1.6 %collective-permute-done.21 = f32[1,32,256]{2,1,0:T(8,128)S(1)} collective-permute-done((f32[1,32,256]{2,1,0:T(8,128)S(1)}, f32[1,32,256]{2,1,0:T(8,128)S(1)}, u32[]{:S(2)}, u32[]{:S(2)}) %collective-permute-start.21) | collective-permute-done | bytes 32800 | tf_op jit(solution)/shard_map/ppermute | solution.py:309
  130.4 2.4 %collective-permute-start.24 = (f32[1,32,256]{2,1,0:T(8,128)S(1)}, f32[1,32,256]{2,1,0:T(8,128)S(1)}, u32[]{:S(2)}, u32[]{:S(2)}) collective-permute-start(f32[1,32,256]{2,1,0:T(8,128)S(1)} %get-tuple-element.28), channel_id=1, source_target_pairs={{0,24},{2,26},{4,28},{6,30},{8,16},{10,18},{12,20},{14,22},{16,8},... | collective-permute-start | bytes 98312 | tf_op jit(solution)/shard_map/ppermute | solution.py:309
  132.7 0.8 collective-permute-start.25
  133.5 1.3 collective-permute-start.26
  134.8 1.3 collective-permute-done.24
  136.1 1.5 %collective-permute-done.25 = f32[1,32,256]{2,1,0:T(8,128)S(1)} collective-permute-done((f32[1,32,256]{2,1,0:T(8,128)S(1)}, f32[1,32,256]{2,1,0:T(8,128)S(1)}, u32[]{:S(2)}, u32[]{:S(2)}) %collective-permute-start.25) | collective-permute-done | bytes 32800 | tf_op jit(solution)/shard_map/ppermute | solution.py:309
  137.8 0.9 collective-permute-start.27
  138.7 4.1 %collective-permute-done.27 = f32[4,32,256]{2,1,0:T(8,128)S(1)} collective-permute-done((f32[4,32,256]{2,1,0:T(8,128)S(1)}, f32[4,32,256]{2,1,0:T(8,128)S(1)}, u32[]{:S(2)}, u32[]{:S(2)}) %collective-permute-start.27) | collective-permute-done | bytes 131104 | tf_op jit(solution)/shard_map/ppermute | solution.py:309
  142.9 1.5 %collective-permute-done.28.refs_1_ = f32[8,32,256]{2,1,0:T(8,128)S(1)} collective-permute-done((f32[8,32,256]{2,1,0:T(8,128)S(1)}, f32[8,32,256]{2,1,0:T(8,128)S(1)}, u32[]{:S(2)}, u32[]{:S(2)}) %collective-permute-start.28) | collective-permute-done | bytes 262176 | tf_op jit(solution)/shard_map/ppermute | solution.py:309
  144.4 1.4 shard_map.62
  (75 shorter events, 9.5 us)
Async XLA Ops:
  0.8 4.9 %collective-permute-start = (f32[32,256]{1,0:T(8,128)S(1)}, f32[32,256]{1,0:T(8,128)S(1)}, u32[]{:S(2)}, u32[]{:S(2)}) collective-permute-start(f32[32,256]{1,0:T(8,128)S(1)} %constant_dynamic-slice_fusion), channel_id=1, source_target_pairs={{0,1},{1,0},{2,3},{3,2},{4,5},{5,4},{6,7},{7,6},{8,9},{9,8},{10,11... | collective-permute-start | bytes 98312 | tf_op jit(solution)/shard_map/ppermute | solution.py:313
  3.7 47.4 %collective-permute-start.5 = (f32[128,16,256]{2,1,0:T(8,128)}, f32[128,16,256]{2,1,0:T(8,128)}, u32[]{:S(2)}, u32[]{:S(2)}) collective-permute-start(f32[128,16,256]{2,1,0:T(8,128)} %sketch_ref.2), channel_id=1, source_target_pairs={{0,1},{1,0},{2,3},{3,2},{4,5},{5,4},{6,7},{7,6},{8,9},{9,8},{10,11... | collective-permute-start | bytes 6291464 | tf_op jit(solution)/shard_map/ppermute | solution.py:313
  5.6 8.3 %collective-permute-start.1 = (f32[1,32,256]{2,1,0:T(8,128)S(1)}, f32[1,32,256]{2,1,0:T(8,128)S(1)}, u32[]{:S(2)}, u32[]{:S(2)}) collective-permute-start(f32[1,32,256]{2,1,0:T(8,128)S(1)} %bitcast.17), channel_id=1, source_target_pairs={{0,16},{2,18},{4,20},{6,22},{8,24},{10,26},{12,28},{14,30},{16,0},... | collective-permute-start | bytes 98312 | tf_op jit(solution)/shard_map/ppermute | solution.py:309
  11.7 1.4 copy-start.2
  13.9 14.1 %copy-start.4 = (f32[512,256]{1,0:T(8,128)S(1)}, f32[512,256]{1,0:T(8,128)}, u32[]{:S(2)}) copy-start(f32[512,256]{1,0:T(8,128)} %param.9) | copy-start | bytes 1572868
  13.9 4.3 %collective-permute-start.2 = (f32[2,32,256]{2,1,0:T(8,128)S(1)}, f32[2,32,256]{2,1,0:T(8,128)S(1)}, u32[]{:S(2)}, u32[]{:S(2)}) collective-permute-start(f32[2,32,256]{2,1,0:T(8,128)S(1)} %pad_maximum_fusion.4), channel_id=1, source_target_pairs={{0,8},{2,10},{4,12},{6,14},{8,0},{10,2},{12,4},{14,6},{16,24},{18,... | collective-permute-start | bytes 196616 | tf_op jit(solution)/shard_map/ppermute | solution.py:309
  18.3 5.0 %collective-permute-start.3 = (f32[4,32,256]{2,1,0:T(8,128)S(1)}, f32[4,32,256]{2,1,0:T(8,128)S(1)}, u32[]{:S(2)}, u32[]{:S(2)}) collective-permute-start(f32[4,32,256]{2,1,0:T(8,128)S(1)} %pad_maximum_fusion.2), channel_id=1, source_target_pairs={{0,4},{2,6},{4,0},{6,2},{8,12},{10,14},{12,8},{14,10},{16,20},{18,... | collective-permute-start | bytes 393224 | tf_op jit(solution)/shard_map/ppermute | solution.py:309
  23.3 2.0 %collective-permute-start.4 = (f32[8,32,256]{2,1,0:T(8,128)S(1)}, f32[8,32,256]{2,1,0:T(8,128)S(1)}, u32[]{:S(2)}, u32[]{:S(2)}) collective-permute-start(f32[8,32,256]{2,1,0:T(8,128)S(1)} %pad_maximum_fusion), channel_id=1, source_target_pairs={{0,2},{2,0},{4,6},{6,4},{8,10},{10,8},{12,14},{14,12},{16,18},{18,... | collective-permute-start | bytes 786440 | tf_op jit(solution)/shard_map/ppermute | solution.py:309
  26.1 2.9 %copy-start.1 = (f32[128,16,256]{2,1,0:T(8,128)S(1)}, f32[128,16,256]{2,1,0:T(8,128)}, u32[]{:S(2)}) copy-start(f32[128,16,256]{2,1,0:T(8,128)} %sketch_ref.2) | copy-start | bytes 6291460
  51.1 7.8 %copy-start.5 = (f32[4,128,256]{2,1,0:T(8,128)S(1)}, f32[4,128,256]{2,1,0:T(8,128)}, u32[]{:S(2)}) copy-start(f32[4,128,256]{2,1,0:T(8,128)} %slice.74) | copy-start | bytes 1572868
  55.7 11.6 %copy-start.3 = (f32[128,16,256]{2,0,1:T(8,128)S(1)}, f32[128,16,256]{2,0,1:T(8,128)}, u32[]{:S(2)}) copy-start(f32[128,16,256]{2,0,1:T(8,128)} %copy-done.2) | copy-start | bytes 6291460
  55.7 1.6 %collective-permute-start.6 = (f32[8,32,256]{2,1,0:T(8,128)S(1)}, f32[8,32,256]{2,1,0:T(8,128)S(1)}, u32[]{:S(2)}, u32[]{:S(2)}) collective-permute-start(f32[8,32,256]{2,1,0:T(8,128)S(1)} %slice.76), channel_id=1, source_target_pairs={{0,2},{2,0},{4,6},{6,4},{8,10},{10,8},{12,14},{14,12},{16,18},{18,... | collective-permute-start | bytes 786440 | tf_op jit(solution)/shard_map/ppermute | solution.py:309
  57.3 5.6 %collective-permute-start.7 = (f32[4,32,256]{2,1,0:T(8,128)S(1)}, f32[4,32,256]{2,1,0:T(8,128)S(1)}, u32[]{:S(2)}, u32[]{:S(2)}) collective-permute-start(f32[4,32,256]{2,1,0:T(8,128)S(1)} %slice.78), channel_id=1, source_target_pairs={{0,4},{2,6},{4,0},{6,2},{8,12},{10,14},{12,8},{14,10},{16,20},{18,... | collective-permute-start | bytes 393224 | tf_op jit(solution)/shard_map/ppermute | solution.py:309
  58.9 13.7 %collective-permute-start.11 = (f32[4,128,256]{2,1,0:T(8,128)S(1)}, f32[4,128,256]{2,1,0:T(8,128)S(1)}, u32[]{:S(2)}, u32[]{:S(2)}) collective-permute-start(f32[4,128,256]{2,1,0:T(8,128)S(1)} %copy-done.5), channel_id=1, source_target_pairs={{0,1},{1,0},{2,3},{3,2},{4,5},{5,4},{6,7},{7,6},{8,9},{9,8},{10,11... | collective-permute-start | bytes 1572872 | tf_op jit(solution)/shard_map/ppermute | solution.py:313
  63.0 4.4 %collective-permute-start.10 = (f32[1,32,256]{2,1,0:T(8,128)S(1)}, f32[1,32,256]{2,1,0:T(8,128)S(1)}, u32[]{:S(2)}, u32[]{:S(2)}) collective-permute-start(f32[1,32,256]{2,1,0:T(8,128)S(1)} %get-tuple-element.33), channel_id=1, source_target_pairs={{0,8},{2,10},{4,12},{6,14},{8,0},{10,2},{12,4},{14,6},{16,24},{18,... | collective-permute-start | bytes 98312 | tf_op jit(solution)/shard_map/ppermute | solution.py:309
  64.7 5.7 %collective-permute-start.8 = (f32[1,32,256]{2,1,0:T(8,128)S(1)}, f32[1,32,256]{2,1,0:T(8,128)S(1)}, u32[]{:S(2)}, u32[]{:S(2)}) collective-permute-start(f32[1,32,256]{2,1,0:T(8,128)S(1)} %get-tuple-element.32), channel_id=1, source_target_pairs={{0,24},{2,26},{4,28},{6,30},{8,16},{10,18},{12,20},{14,22},{16,8},... | collective-permute-start | bytes 98312 | tf_op jit(solution)/shard_map/ppermute | solution.py:309
  67.1 25.1 %copy-start = (f32[128,16,256]{2,1,0:T(8,128)S(1)}, f32[128,16,256]{2,1,0:T(8,128)}, u32[]{:S(2)}) copy-start(f32[128,16,256]{2,1,0:T(8,128)} %sketch_ref.3) | copy-start | bytes 6291460
  67.1 5.2 %collective-permute-start.9 = (f32[1,32,256]{2,1,0:T(8,128)S(1)}, f32[1,32,256]{2,1,0:T(8,128)S(1)}, u32[]{:S(2)}, u32[]{:S(2)}) collective-permute-start(f32[1,32,256]{2,1,0:T(8,128)S(1)} %get-tuple-element.34), channel_id=1, source_target_pairs={{0,16},{2,18},{4,20},{6,22},{8,24},{10,26},{12,28},{14,30},{16,0},... | collective-permute-start | bytes 98312 | tf_op jit(solution)/shard_map/ppermute | solution.py:309
  72.6 4.3 %collective-permute-start.12 = (f32[1,32,256]{2,1,0:T(8,128)S(1)}, f32[1,32,256]{2,1,0:T(8,128)S(1)}, u32[]{:S(2)}, u32[]{:S(2)}) collective-permute-start(f32[1,32,256]{2,1,0:T(8,128)S(1)} %fusion.6), channel_id=1, source_target_pairs={{0,1},{1,0},{2,3},{3,2},{4,5},{5,4},{6,7},{7,6},{8,9},{9,8},{10,11... | collective-permute-start | bytes 98312 | tf_op jit(solution)/shard_map/ppermute | solution.py:313
  73.5 38.3 %collective-permute-start.18 = (f32[12,128,256]{2,1,0:T(8,128)S(1)}, f32[12,128,256]{2,1,0:T(8,128)S(1)}, u32[]{:S(2)}, u32[]{:S(2)}) collective-permute-start(f32[12,128,256]{2,1,0:T(8,128)S(1)} %slice.83), channel_id=1, source_target_pairs={{0,1},{1,0},{2,3},{3,2},{4,5},{5,4},{6,7},{7,6},{8,9},{9,8},{10,11... | collective-permute-start | bytes 4718600 | tf_op jit(solution)/shard_map/ppermute | solution.py:313
  77.0 6.7 %collective-permute-start.13 = (f32[1,2,32,256]{3,2,1,0:T(8,128)S(1)}, f32[1,2,32,256]{3,2,1,0:T(8,128)S(1)}, u32[]{:S(2)}, u32[]{:S(2)}) collective-permute-start(f32[1,2,32,256]{3,2,1,0:T(8,128)S(1)} %maximum_bitcast_fusion), channel_id=1, source_target_pairs={{0,24},{2,26},{4,28},{6,30},{8,16},{10,18},{12,20},{14,22},{16,8},... | collective-permute-start | bytes 196616 | tf_op jit(solution)/shard_map/ppermute | solution.py:309
  80.6 5.2 %collective-permute-start.14 = (f32[1,2,32,256]{3,2,1,0:T(8,128)S(1)}, f32[1,2,32,256]{3,2,1,0:T(8,128)S(1)}, u32[]{:S(2)}, u32[]{:S(2)}) collective-permute-start(f32[1,2,32,256]{3,2,1,0:T(8,128)S(1)} %maximum_bitcast_fusion), channel_id=1, source_target_pairs={{0,16},{2,18},{4,20},{6,22},{8,24},{10,26},{12,28},{14,30},{16,0},... | collective-permute-start | bytes 196616 | tf_op jit(solution)/shard_map/ppermute | solution.py:309
  80.6 5.2 %collective-permute-start.15 = (f32[1,2,32,256]{3,2,1,0:T(8,128)S(1)}, f32[1,2,32,256]{3,2,1,0:T(8,128)S(1)}, u32[]{:S(2)}, u32[]{:S(2)}) collective-permute-start(f32[1,2,32,256]{3,2,1,0:T(8,128)S(1)} %maximum_bitcast_fusion), channel_id=1, source_target_pairs={{0,8},{2,10},{4,12},{6,14},{8,0},{10,2},{12,4},{14,6},{16,24},{18,... | collective-permute-start | bytes 196616 | tf_op jit(solution)/shard_map/ppermute | solution.py:309
  85.8 6.4 %collective-permute-start.16 = (f32[4,2,32,256]{3,2,1,0:T(8,128)S(1)}, f32[4,2,32,256]{3,2,1,0:T(8,128)S(1)}, u32[]{:S(2)}, u32[]{:S(2)}) collective-permute-start(f32[4,2,32,256]{3,2,1,0:T(8,128)S(1)} %pad_maximum_fusion.1), channel_id=1, source_target_pairs={{0,4},{2,6},{4,0},{6,2},{8,12},{10,14},{12,8},{14,10},{16,20},{18,... | collective-permute-start | bytes 786440 | tf_op jit(solution)/shard_map/ppermute | solution.py:309
  92.2 2.0 %collective-permute-start.17 = (f32[8,2,32,256]{3,2,1,0:T(8,128)S(1)}, f32[8,2,32,256]{3,2,1,0:T(8,128)S(1)}, u32[]{:S(2)}, u32[]{:S(2)}) collective-permute-start(f32[8,2,32,256]{3,2,1,0:T(8,128)S(1)} %constant_dynamic-update-slice_fusion.5.refs_0_), channel_id=1, source_target_pairs={{0,2},{2,0},{4,6},{6,4},{8,10},{10,8},{12,14},{14,12},{16,18},{18,... | collective-permute-start | bytes 1572872 | tf_op jit(solution)/shard_map/ppermute | solution.py:309
  116.3 1.6 %collective-permute-start.19 = (f32[8,32,256]{2,1,0:T(8,128)S(1)}, f32[8,32,256]{2,1,0:T(8,128)S(1)}, u32[]{:S(2)}, u32[]{:S(2)}) collective-permute-start(f32[8,32,256]{2,1,0:T(8,128)S(1)} %slice.85), channel_id=1, source_target_pairs={{0,2},{2,0},{4,6},{6,4},{8,10},{10,8},{12,14},{14,12},{16,18},{18,... | collective-permute-start | bytes 786440 | tf_op jit(solution)/shard_map/ppermute | solution.py:309
  117.9 5.6 %collective-permute-start.20 = (f32[4,32,256]{2,1,0:T(8,128)S(1)}, f32[4,32,256]{2,1,0:T(8,128)S(1)}, u32[]{:S(2)}, u32[]{:S(2)}) collective-permute-start(f32[4,32,256]{2,1,0:T(8,128)S(1)} %slice.87), channel_id=1, source_target_pairs={{0,4},{2,6},{4,0},{6,2},{8,12},{10,14},{12,8},{14,10},{16,20},{18,... | collective-permute-start | bytes 393224 | tf_op jit(solution)/shard_map/ppermute | solution.py:309
  123.6 6.1 %collective-permute-start.21 = (f32[1,32,256]{2,1,0:T(8,128)S(1)}, f32[1,32,256]{2,1,0:T(8,128)S(1)}, u32[]{:S(2)}, u32[]{:S(2)}) collective-permute-start(f32[1,32,256]{2,1,0:T(8,128)S(1)} %get-tuple-element.29), channel_id=1, source_target_pairs={{0,24},{2,26},{4,28},{6,30},{8,16},{10,18},{12,20},{14,22},{16,8},... | collective-permute-start | bytes 98312 | tf_op jit(solution)/shard_map/ppermute | solution.py:309
  125.3 4.9 %collective-permute-start.22 = (f32[1,32,256]{2,1,0:T(8,128)S(1)}, f32[1,32,256]{2,1,0:T(8,128)S(1)}, u32[]{:S(2)}, u32[]{:S(2)}) collective-permute-start(f32[1,32,256]{2,1,0:T(8,128)S(1)} %get-tuple-element.31), channel_id=1, source_target_pairs={{0,16},{2,18},{4,20},{6,22},{8,24},{10,26},{12,28},{14,30},{16,0},... | collective-permute-start | bytes 98312 | tf_op jit(solution)/shard_map/ppermute | solution.py:309
  125.8 4.6 %collective-permute-start.23 = (f32[1,32,256]{2,1,0:T(8,128)S(1)}, f32[1,32,256]{2,1,0:T(8,128)S(1)}, u32[]{:S(2)}, u32[]{:S(2)}) collective-permute-start(f32[1,32,256]{2,1,0:T(8,128)S(1)} %get-tuple-element.30), channel_id=1, source_target_pairs={{0,8},{2,10},{4,12},{6,14},{8,0},{10,2},{12,4},{14,6},{16,24},{18,... | collective-permute-start | bytes 98312 | tf_op jit(solution)/shard_map/ppermute | solution.py:309
  130.4 5.8 %collective-permute-start.24 = (f32[1,32,256]{2,1,0:T(8,128)S(1)}, f32[1,32,256]{2,1,0:T(8,128)S(1)}, u32[]{:S(2)}, u32[]{:S(2)}) collective-permute-start(f32[1,32,256]{2,1,0:T(8,128)S(1)} %get-tuple-element.28), channel_id=1, source_target_pairs={{0,24},{2,26},{4,28},{6,30},{8,16},{10,18},{12,20},{14,22},{16,8},... | collective-permute-start | bytes 98312 | tf_op jit(solution)/shard_map/ppermute | solution.py:309
  132.7 4.9 %collective-permute-start.25 = (f32[1,32,256]{2,1,0:T(8,128)S(1)}, f32[1,32,256]{2,1,0:T(8,128)S(1)}, u32[]{:S(2)}, u32[]{:S(2)}) collective-permute-start(f32[1,32,256]{2,1,0:T(8,128)S(1)} %get-tuple-element.28), channel_id=1, source_target_pairs={{0,16},{2,18},{4,20},{6,22},{8,24},{10,26},{12,28},{14,30},{16,0},... | collective-permute-start | bytes 98312 | tf_op jit(solution)/shard_map/ppermute | solution.py:309
  133.5 4.3 %collective-permute-start.26 = (f32[1,32,256]{2,1,0:T(8,128)S(1)}, f32[1,32,256]{2,1,0:T(8,128)S(1)}, u32[]{:S(2)}, u32[]{:S(2)}) collective-permute-start(f32[1,32,256]{2,1,0:T(8,128)S(1)} %get-tuple-element.28), channel_id=1, source_target_pairs={{0,8},{2,10},{4,12},{6,14},{8,0},{10,2},{12,4},{14,6},{16,24},{18,... | collective-permute-start | bytes 98312 | tf_op jit(solution)/shard_map/ppermute | solution.py:309
  137.8 5.0 %collective-permute-start.27 = (f32[4,32,256]{2,1,0:T(8,128)S(1)}, f32[4,32,256]{2,1,0:T(8,128)S(1)}, u32[]{:S(2)}, u32[]{:S(2)}) collective-permute-start(f32[4,32,256]{2,1,0:T(8,128)S(1)} %pad_maximum_fusion.3), channel_id=1, source_target_pairs={{0,4},{2,6},{4,0},{6,2},{8,12},{10,14},{12,8},{14,10},{16,20},{18,... | collective-permute-start | bytes 393224 | tf_op jit(solution)/shard_map/ppermute | solution.py:309
  142.8 1.6 %collective-permute-start.28 = (f32[8,32,256]{2,1,0:T(8,128)S(1)}, f32[8,32,256]{2,1,0:T(8,128)S(1)}, u32[]{:S(2)}, u32[]{:S(2)}) collective-permute-start(f32[8,32,256]{2,1,0:T(8,128)S(1)} %constant_dynamic-update-slice_fusion.10.refs_0_), channel_id=1, source_target_pairs={{0,2},{2,0},{4,6},{6,4},{8,10},{10,8},{12,14},{14,12},{16,18},{18,... | collective-permute-start | bytes 786440 | tf_op jit(solution)/shard_map/ppermute | solution.py:309

commit v6 on v5

--- a/solution.py
+++ b/solution.py
@@ -183,7 +183,7 @@
     return pltpu.CompilerParams(vmem_limit_bytes=mib << 20)
 
 
-SLOTS, GROUP = 3, 8
+SLOTS, GROUP = 4, 8
 
 
 def cost(flops, size):
@@ -205,7 +205,7 @@
         in_specs=[HBM] + ([VMEM] if place is None else [SMEM] + [VMEM] * len(carried)),
         out_specs=(VMEM, VMEM),
         scratch_shapes=loop_scratch(core, columns),
-        compiler_params=limit(32),
+        compiler_params=limit(40),
         cost_estimate=cost(6 * count * slices * depth * columns, 4 * core.size) if place is None else cost(2 * core.size * columns, 1),
     )(core, *operands)
 
@@ -224,7 +224,7 @@
         in_specs=[HBM, VMEM, VMEM],
         out_specs=(VMEM,) * 3,
         scratch_shapes=[pltpu.VMEM((slices, depth, 2 * size), BF16)] + loop_scratch(core, columns),
-        compiler_params=limit(36),
+        compiler_params=limit(40),
         cost_estimate=cost(28 * core.size * columns // 8, 1),
     )(core, carried, sketch)
 

time: 146 us -> 146 us (level)
  no operation moved by 1% of the time
where the time goes in v6:
time: 146 us
  waiting for transfers between devices  50.2 us (34%)
  Pallas kernels  48.8 us (33%)
  starting transfers between devices  33.9 us (23%)
  local copies, waits for them, and re-layouts  11.2 us (8%)
    ppermute x24, waiting for transfers between devices, partner(): return lax.ppermute(x, 'mode', [(i, i ^ distance) for i in range(count)])  43.2 us
    ppermute x24, starting transfers between devices, partner(): return lax.ppermute(x, 'mode', [(i, i ^ distance) for i in range(count)])  28.1 us
    pallas_call x1, Pallas kernels, first_step(): pl.pallas_call(first_kernel, out_shape=(out, out, jax.ShapeDtypeStruct((c...  19.6 us
    pallas_call x1, Pallas kernels, hidden(): pl.pallas_call(kernel, out_shape=(out, out), in_specs=[HBM] + ([VMEM] if...  17.6 us
    ppermute x5, waiting for transfers between devices, shift(): return lax.ppermute(x, 'rank', [(i, (i + d) % ranks) for i in range(ranks)])  6.97 us
    unnamed x23, local copies, waits for them, and re-layouts  6.75 us
    ppermute x5, starting transfers between devices, shift(): return lax.ppermute(x, 'rank', [(i, (i + d) % ranks) for i in range(ranks)])  5.85 us
    pallas_call x1, Pallas kernels, second_product(): pl.pallas_call(second_kernel, out_shape=out_shape(rows, columns, count),...  4.51 us
  transfers between devices with their start and end apart: 29, of which 24 were waited for; matrix products, arithmetic and copies ran while one was open for 7% of the time, Pallas kernels for 26%

profile of v6, /device:TPU:0, one launch (start us, length us, event | category | flops | bytes accessed | tf_op | source)
XLA Modules:
  0.0 145.8 jit_solution(16889853358024536126)
XLA Ops:
  0.8 3.0 %collective-permute-start = (f32[32,256]{1,0:T(8,128)S(1)}, f32[32,256]{1,0:T(8,128)S(1)}, u32[]{:S(2)}, u32[]{:S(2)}) collective-permute-start(f32[32,256]{1,0:T(8,128)S(1)} %constant_dynamic-slice_fusion), channel_id=1, source_target_pairs={{0,1},{1,0},{2,3},{3,2},{4,5},{5,4},{6,7},{7,6},{8,9},{9,8},{10,11... | collective-permute-start | bytes 98312 | tf_op jit(solution)/shard_map/ppermute | solution.py:313
  3.8 1.8 %collective-permute-done = f32[32,256]{1,0:T(8,128)S(1)} collective-permute-done((f32[32,256]{1,0:T(8,128)S(1)}, f32[32,256]{1,0:T(8,128)S(1)}, u32[]{:S(2)}, u32[]{:S(2)}) %collective-permute-start) | collective-permute-done | bytes 32800 | tf_op jit(solution)/shard_map/ppermute | solution.py:313
  5.6 3.1 %collective-permute-start.1 = (f32[1,32,256]{2,1,0:T(8,128)S(1)}, f32[1,32,256]{2,1,0:T(8,128)S(1)}, u32[]{:S(2)}, u32[]{:S(2)}) collective-permute-start(f32[1,32,256]{2,1,0:T(8,128)S(1)} %bitcast.17), channel_id=1, source_target_pairs={{0,16},{2,18},{4,20},{6,22},{8,24},{10,26},{12,28},{14,30},{16,0},... | collective-permute-start | bytes 98312 | tf_op jit(solution)/shard_map/ppermute | solution.py:309
  8.9 2.8 %copy.8 = f32[128,16,256]{2,0,1:T(8,128)S(1)} copy(f32[128,16,256]{2,1,0:T(8,128)} %sketch_ref.3) | data formatting | bytes 4194304 | tf_op args[3]
  11.7 1.4 copy-done.2
  13.1 0.8 slice.74
  13.9 1.6 %collective-permute-start.2 = (f32[2,32,256]{2,1,0:T(8,128)S(1)}, f32[2,32,256]{2,1,0:T(8,128)S(1)}, u32[]{:S(2)}, u32[]{:S(2)}) collective-permute-start(f32[2,32,256]{2,1,0:T(8,128)S(1)} %pad_maximum_fusion.4), channel_id=1, source_target_pairs={{0,8},{2,10},{4,12},{6,14},{8,0},{10,2},{12,4},{14,6},{16,24},{18,... | collective-permute-start | bytes 196616 | tf_op jit(solution)/shard_map/ppermute | solution.py:309
  15.7 2.6 %collective-permute-done.2 = f32[2,32,256]{2,1,0:T(8,128)S(1)} collective-permute-done((f32[2,32,256]{2,1,0:T(8,128)S(1)}, f32[2,32,256]{2,1,0:T(8,128)S(1)}, u32[]{:S(2)}, u32[]{:S(2)}) %collective-permute-start.2) | collective-permute-done | bytes 65568 | tf_op jit(solution)/shard_map/ppermute | solution.py:309
  18.3 1.6 %collective-permute-start.3 = (f32[4,32,256]{2,1,0:T(8,128)S(1)}, f32[4,32,256]{2,1,0:T(8,128)S(1)}, u32[]{:S(2)}, u32[]{:S(2)}) collective-permute-start(f32[4,32,256]{2,1,0:T(8,128)S(1)} %pad_maximum_fusion.2), channel_id=1, source_target_pairs={{0,4},{2,6},{4,0},{6,2},{8,12},{10,14},{12,8},{14,10},{16,20},{18,... | collective-permute-start | bytes 393224 | tf_op jit(solution)/shard_map/ppermute | solution.py:309
  20.5 2.9 %collective-permute-done.3 = f32[4,32,256]{2,1,0:T(8,128)S(1)} collective-permute-done((f32[4,32,256]{2,1,0:T(8,128)S(1)}, f32[4,32,256]{2,1,0:T(8,128)S(1)}, u32[]{:S(2)}, u32[]{:S(2)}) %collective-permute-start.3) | collective-permute-done | bytes 131104 | tf_op jit(solution)/shard_map/ppermute | solution.py:309
  26.1 1.8 %gather_fusion = f32[16,32,256]{2,1,0:T(8,128)S(1)} fusion(f32[16,32,256]{2,1,0:T(8,128)} %constant_dynamic-update-slice_fusion, s32[1024]{0:T(1024)S(1)} %pad_clamp_fusion), kind=kCustom, calls=%fused_computation | custom fusion | bytes 1048640 | tf_op jit(solution)/shard_map/jit(_take)/gather | solution.py:337
  28.0 1.0 fusion.2.carried_ref
  29.0 19.6 %shard_map.55 = (bf16[16,512,256]{2,1,0:T(8,128)(2,1)S(1)}, bf16[16,512,256]{2,1,0:T(8,128)(2,1)S(1)}, f32[512,128]{1,0:T(8,128)S(1)}) custom-call(f32[512,16,1024]{2,1,0:T(8,128)} %core_hbm.2, f32[1024,256]{1,0:T(8,128)S(1)} %fusion.2.carried_ref, f32[128,16,256]{2,1,0:T(8,128)S(1)} %copy-done.1), custom_call_target="tpu_custom_call" | custom-call | flops 7516192768 | bytes 1 | tf_op jit(solution)/shard_map/pallas_call | solution.py:221
  48.6 2.5 %collective-permute-done.5.refs_0_ = f32[128,16,256]{2,1,0:T(8,128)} collective-permute-done((f32[128,16,256]{2,1,0:T(8,128)}, f32[128,16,256]{2,1,0:T(8,128)}, u32[]{:S(2)}, u32[]{:S(2)}) %collective-permute-start.5) | collective-permute-done | bytes 2097184 | tf_op jit(solution)/shard_map/ppermute | solution.py:313
  51.1 4.5 %shard_map.56 = f32[16,32,256]{2,1,0:T(8,128)S(1)} custom-call(s32[2]{0:T(128)S(1)} %pad_add_fusion.place_ref, bf16[16,512,256]{2,1,0:T(8,128)(2,1)S(1)} %get-tuple-element.16.high, bf16[16,512,256]{2,1,0:T(8,128)(2,1)S(1)} %get-tuple-element.17.low, f32[512,128]{1,0:T(8,128)S(1)} %get-tuple-element.18.own_ref, f32[128,16,256]{2,1,0:T(8,128)} %collective-permute-done.5.refs_0_), custom_call_target="tpu_custom_call" | custom-call | flops 1610612736 | bytes 8388608 | tf_op jit(solution)/shard_map/pallas_call | solution.py:239
  55.8 1.5 %collective-permute-done.6 = f32[8,32,256]{2,1,0:T(8,128)S(1)} collective-permute-done((f32[8,32,256]{2,1,0:T(8,128)S(1)}, f32[8,32,256]{2,1,0:T(8,128)S(1)}, u32[]{:S(2)}, u32[]{:S(2)}) %collective-permute-start.6) | collective-permute-done | bytes 262176 | tf_op jit(solution)/shard_map/ppermute | solution.py:309
  57.3 1.6 %collective-permute-start.7 = (f32[4,32,256]{2,1,0:T(8,128)S(1)}, f32[4,32,256]{2,1,0:T(8,128)S(1)}, u32[]{:S(2)}, u32[]{:S(2)}) collective-permute-start(f32[4,32,256]{2,1,0:T(8,128)S(1)} %slice.78), channel_id=1, source_target_pairs={{0,4},{2,6},{4,0},{6,2},{8,12},{10,14},{12,8},{14,10},{16,20},{18,... | collective-permute-start | bytes 393224 | tf_op jit(solution)/shard_map/ppermute | solution.py:309
  58.9 0.8 collective-permute-start.11
  59.8 3.2 %collective-permute-done.7 = f32[4,32,256]{2,1,0:T(8,128)S(1)} collective-permute-done((f32[4,32,256]{2,1,0:T(8,128)S(1)}, f32[4,32,256]{2,1,0:T(8,128)S(1)}, u32[]{:S(2)}, u32[]{:S(2)}) %collective-permute-start.7) | collective-permute-done | bytes 131104 | tf_op jit(solution)/shard_map/ppermute | solution.py:309
  63.0 1.7 %collective-permute-start.10 = (f32[1,32,256]{2,1,0:T(8,128)S(1)}, f32[1,32,256]{2,1,0:T(8,128)S(1)}, u32[]{:S(2)}, u32[]{:S(2)}) collective-permute-start(f32[1,32,256]{2,1,0:T(8,128)S(1)} %get-tuple-element.33), channel_id=1, source_target_pairs={{0,8},{2,10},{4,12},{6,14},{8,0},{10,2},{12,4},{14,6},{16,24},{18,... | collective-permute-start | bytes 98312 | tf_op jit(solution)/shard_map/ppermute | solution.py:309
  64.7 2.5 %collective-permute-start.8 = (f32[1,32,256]{2,1,0:T(8,128)S(1)}, f32[1,32,256]{2,1,0:T(8,128)S(1)}, u32[]{:S(2)}, u32[]{:S(2)}) collective-permute-start(f32[1,32,256]{2,1,0:T(8,128)S(1)} %get-tuple-element.32), channel_id=1, source_target_pairs={{0,24},{2,26},{4,28},{6,30},{8,16},{10,18},{12,20},{14,22},{16,8},... | collective-permute-start | bytes 98312 | tf_op jit(solution)/shard_map/ppermute | solution.py:309
  67.4 3.0 %collective-permute-done.8 = f32[1,32,256]{2,1,0:T(8,128)S(1)} collective-permute-done((f32[1,32,256]{2,1,0:T(8,128)S(1)}, f32[1,32,256]{2,1,0:T(8,128)S(1)}, u32[]{:S(2)}, u32[]{:S(2)}) %collective-permute-start.8) | collective-permute-done | bytes 32800 | tf_op jit(solution)/shard_map/ppermute | solution.py:309
  70.4 1.9 %collective-permute-done.9 = f32[1,32,256]{2,1,0:T(8,128)S(1)} collective-permute-done((f32[1,32,256]{2,1,0:T(8,128)S(1)}, f32[1,32,256]{2,1,0:T(8,128)S(1)}, u32[]{:S(2)}, u32[]{:S(2)}) %collective-permute-start.9) | collective-permute-done | bytes 32800 | tf_op jit(solution)/shard_map/ppermute | solution.py:309
  72.6 0.8 collective-permute-start.12
  73.5 1.2 collective-permute-start.18
  74.7 2.3 %collective-permute-done.12 = f32[1,32,256]{2,1,0:T(8,128)S(1)} collective-permute-done((f32[1,32,256]{2,1,0:T(8,128)S(1)}, f32[1,32,256]{2,1,0:T(8,128)S(1)}, u32[]{:S(2)}, u32[]{:S(2)}) %collective-permute-start.12) | collective-permute-done | bytes 32800 | tf_op jit(solution)/shard_map/ppermute | solution.py:313
  77.0 3.6 %collective-permute-start.13 = (f32[1,2,32,256]{3,2,1,0:T(8,128)S(1)}, f32[1,2,32,256]{3,2,1,0:T(8,128)S(1)}, u32[]{:S(2)}, u32[]{:S(2)}) collective-permute-start(f32[1,2,32,256]{3,2,1,0:T(8,128)S(1)} %maximum_bitcast_fusion), channel_id=1, source_target_pairs={{0,24},{2,26},{4,28},{6,30},{8,16},{10,18},{12,20},{14,22},{16,8},... | collective-permute-start | bytes 196616 | tf_op jit(solution)/shard_map/ppermute | solution.py:309
  80.6 0.8 collective-permute-start.15
  81.4 2.3 %collective-permute-done.13 = f32[1,2,32,256]{3,2,1,0:T(8,128)S(1)} collective-permute-done((f32[1,2,32,256]{3,2,1,0:T(8,128)S(1)}, f32[1,2,32,256]{3,2,1,0:T(8,128)S(1)}, u32[]{:S(2)}, u32[]{:S(2)}) %collective-permute-start.13) | collective-permute-done | bytes 65568 | tf_op jit(solution)/shard_map/ppermute | solution.py:309
  83.7 2.1 %collective-permute-done.14 = f32[1,2,32,256]{3,2,1,0:T(8,128)S(1)} collective-permute-done((f32[1,2,32,256]{3,2,1,0:T(8,128)S(1)}, f32[1,2,32,256]{3,2,1,0:T(8,128)S(1)}, u32[]{:S(2)}, u32[]{:S(2)}) %collective-permute-start.14) | collective-permute-done | bytes 65568 | tf_op jit(solution)/shard_map/ppermute | solution.py:309
  86.4 5.8 %collective-permute-done.16 = f32[4,2,32,256]{3,2,1,0:T(8,128)S(1)} collective-permute-done((f32[4,2,32,256]{3,2,1,0:T(8,128)S(1)}, f32[4,2,32,256]{3,2,1,0:T(8,128)S(1)}, u32[]{:S(2)}, u32[]{:S(2)}) %collective-permute-start.16) | collective-permute-done | bytes 262176 | tf_op jit(solution)/shard_map/ppermute | solution.py:309
  92.3 1.1 shard_map.58.refs_0_
  94.2 17.6 %shard_map.57 = (bf16[16,512,256]{2,1,0:T(8,128)(2,1)S(1)}, bf16[16,512,256]{2,1,0:T(8,128)(2,1)S(1)}) custom-call(f32[512,16,1024]{2,1,0:T(8,128)} %core_hbm.3, s32[2]{0:T(128)S(1)} %pad_add_fusion.place_ref, f32[8,2,32,256]{3,2,1,0:T(8,128)S(1)} %constant_dynamic-update-slice_fusion.5.refs_0_, f32[8,2,32,256]{3,2,1,0:T(8,128)S(1)} %collective-permute-done.17.refs_1_), custom_call_target="tpu_custom_call" | custom-call | flops 4294967296 | bytes 1 | tf_op jit(solution)/shard_map/pallas_call | solution.py:202
  112.3 4.0 %shard_map.61 = f32[16,32,256]{2,1,0:T(8,128)S(1)} custom-call(s32[2]{0:T(128)S(1)} %pad_add_fusion.place_ref, bf16[16,512,256]{2,1,0:T(8,128)(2,1)S(1)} %get-tuple-element.23.high, bf16[16,512,256]{2,1,0:T(8,128)(2,1)S(1)} %get-tuple-element.24.low, bf16[16,256,256]{2,1,0:T(8,128)(2,1)S(1)} %shard_map.58.refs_0_, ...), custom_call_target="tpu_custom_call" | custom-call | flops 3221225472 | bytes 8388608 | tf_op jit(solution)/shard_map/pallas_call | solution.py:252
  116.5 1.4 collective-permute-done.19
  118.5 5.0 %collective-permute-done.20 = f32[4,32,256]{2,1,0:T(8,128)S(1)} collective-permute-done((f32[4,32,256]{2,1,0:T(8,128)S(1)}, f32[4,32,256]{2,1,0:T(8,128)S(1)}, u32[]{:S(2)}, u32[]{:S(2)}) %collective-permute-start.20) | collective-permute-done | bytes 131104 | tf_op jit(solution)/shard_map/ppermute | solution.py:309
  123.6 1.7 %collective-permute-start.21 = (f32[1,32,256]{2,1,0:T(8,128)S(1)}, f32[1,32,256]{2,1,0:T(8,128)S(1)}, u32[]{:S(2)}, u32[]{:S(2)}) collective-permute-start(f32[1,32,256]{2,1,0:T(8,128)S(1)} %get-tuple-element.29), channel_id=1, source_target_pairs={{0,24},{2,26},{4,28},{6,30},{8,16},{10,18},{12,20},{14,22},{16,8},... | collective-permute-start | bytes 98312 | tf_op jit(solution)/shard_map/ppermute | solution.py:309
  125.8 2.3 %collective-permute-start.23 = (f32[1,32,256]{2,1,0:T(8,128)S(1)}, f32[1,32,256]{2,1,0:T(8,128)S(1)}, u32[]{:S(2)}, u32[]{:S(2)}) collective-permute-start(f32[1,32,256]{2,1,0:T(8,128)S(1)} %get-tuple-element.30), channel_id=1, source_target_pairs={{0,8},{2,10},{4,12},{6,14},{8,0},{10,2},{12,4},{14,6},{16,24},{18,... | collective-permute-start | bytes 98312 | tf_op jit(solution)/shard_map/ppermute | solution.py:309
  128.1 1.7 %collective-permute-done.21 = f32[1,32,256]{2,1,0:T(8,128)S(1)} collective-permute-done((f32[1,32,256]{2,1,0:T(8,128)S(1)}, f32[1,32,256]{2,1,0:T(8,128)S(1)}, u32[]{:S(2)}, u32[]{:S(2)}) %collective-permute-start.21) | collective-permute-done | bytes 32800 | tf_op jit(solution)/shard_map/ppermute | solution.py:309
  130.4 2.4 %collective-permute-start.24 = (f32[1,32,256]{2,1,0:T(8,128)S(1)}, f32[1,32,256]{2,1,0:T(8,128)S(1)}, u32[]{:S(2)}, u32[]{:S(2)}) collective-permute-start(f32[1,32,256]{2,1,0:T(8,128)S(1)} %get-tuple-element.28), channel_id=1, source_target_pairs={{0,24},{2,26},{4,28},{6,30},{8,16},{10,18},{12,20},{14,22},{16,8},... | collective-permute-start | bytes 98312 | tf_op jit(solution)/shard_map/ppermute | solution.py:309
  132.7 0.8 collective-permute-start.25
  133.5 1.3 collective-permute-start.26
  134.8 1.3 collective-permute-done.24
  136.2 1.5 %collective-permute-done.25 = f32[1,32,256]{2,1,0:T(8,128)S(1)} collective-permute-done((f32[1,32,256]{2,1,0:T(8,128)S(1)}, f32[1,32,256]{2,1,0:T(8,128)S(1)}, u32[]{:S(2)}, u32[]{:S(2)}) %collective-permute-start.25) | collective-permute-done | bytes 32800 | tf_op jit(solution)/shard_map/ppermute | solution.py:309
  137.8 0.9 collective-permute-start.27
  138.7 4.1 %collective-permute-done.27 = f32[4,32,256]{2,1,0:T(8,128)S(1)} collective-permute-done((f32[4,32,256]{2,1,0:T(8,128)S(1)}, f32[4,32,256]{2,1,0:T(8,128)S(1)}, u32[]{:S(2)}, u32[]{:S(2)}) %collective-permute-start.27) | collective-permute-done | bytes 131104 | tf_op jit(solution)/shard_map/ppermute | solution.py:309
  142.9 1.5 %collective-permute-done.28.refs_1_ = f32[8,32,256]{2,1,0:T(8,128)S(1)} collective-permute-done((f32[8,32,256]{2,1,0:T(8,128)S(1)}, f32[8,32,256]{2,1,0:T(8,128)S(1)}, u32[]{:S(2)}, u32[]{:S(2)}) %collective-permute-start.28) | collective-permute-done | bytes 262176 | tf_op jit(solution)/shard_map/ppermute | solution.py:309
  144.5 1.4 shard_map.62
  (75 shorter events, 9.5 us)
Async XLA Ops:
  0.8 4.9 %collective-permute-start = (f32[32,256]{1,0:T(8,128)S(1)}, f32[32,256]{1,0:T(8,128)S(1)}, u32[]{:S(2)}, u32[]{:S(2)}) collective-permute-start(f32[32,256]{1,0:T(8,128)S(1)} %constant_dynamic-slice_fusion), channel_id=1, source_target_pairs={{0,1},{1,0},{2,3},{3,2},{4,5},{5,4},{6,7},{7,6},{8,9},{9,8},{10,11... | collective-permute-start | bytes 98312 | tf_op jit(solution)/shard_map/ppermute | solution.py:313
  3.7 47.4 %collective-permute-start.5 = (f32[128,16,256]{2,1,0:T(8,128)}, f32[128,16,256]{2,1,0:T(8,128)}, u32[]{:S(2)}, u32[]{:S(2)}) collective-permute-start(f32[128,16,256]{2,1,0:T(8,128)} %sketch_ref.2), channel_id=1, source_target_pairs={{0,1},{1,0},{2,3},{3,2},{4,5},{5,4},{6,7},{7,6},{8,9},{9,8},{10,11... | collective-permute-start | bytes 6291464 | tf_op jit(solution)/shard_map/ppermute | solution.py:313
  5.6 8.3 %collective-permute-start.1 = (f32[1,32,256]{2,1,0:T(8,128)S(1)}, f32[1,32,256]{2,1,0:T(8,128)S(1)}, u32[]{:S(2)}, u32[]{:S(2)}) collective-permute-start(f32[1,32,256]{2,1,0:T(8,128)S(1)} %bitcast.17), channel_id=1, source_target_pairs={{0,16},{2,18},{4,20},{6,22},{8,24},{10,26},{12,28},{14,30},{16,0},... | collective-permute-start | bytes 98312 | tf_op jit(solution)/shard_map/ppermute | solution.py:309
  11.7 1.4 copy-start.2
  13.9 14.1 %copy-start.4 = (f32[512,256]{1,0:T(8,128)S(1)}, f32[512,256]{1,0:T(8,128)}, u32[]{:S(2)}) copy-start(f32[512,256]{1,0:T(8,128)} %param.9) | copy-start | bytes 1572868
  13.9 4.3 %collective-permute-start.2 = (f32[2,32,256]{2,1,0:T(8,128)S(1)}, f32[2,32,256]{2,1,0:T(8,128)S(1)}, u32[]{:S(2)}, u32[]{:S(2)}) collective-permute-start(f32[2,32,256]{2,1,0:T(8,128)S(1)} %pad_maximum_fusion.4), channel_id=1, source_target_pairs={{0,8},{2,10},{4,12},{6,14},{8,0},{10,2},{12,4},{14,6},{16,24},{18,... | collective-permute-start | bytes 196616 | tf_op jit(solution)/shard_map/ppermute | solution.py:309
  18.3 5.0 %collective-permute-start.3 = (f32[4,32,256]{2,1,0:T(8,128)S(1)}, f32[4,32,256]{2,1,0:T(8,128)S(1)}, u32[]{:S(2)}, u32[]{:S(2)}) collective-permute-start(f32[4,32,256]{2,1,0:T(8,128)S(1)} %pad_maximum_fusion.2), channel_id=1, source_target_pairs={{0,4},{2,6},{4,0},{6,2},{8,12},{10,14},{12,8},{14,10},{16,20},{18,... | collective-permute-start | bytes 393224 | tf_op jit(solution)/shard_map/ppermute | solution.py:309
  23.3 2.0 %collective-permute-start.4 = (f32[8,32,256]{2,1,0:T(8,128)S(1)}, f32[8,32,256]{2,1,0:T(8,128)S(1)}, u32[]{:S(2)}, u32[]{:S(2)}) collective-permute-start(f32[8,32,256]{2,1,0:T(8,128)S(1)} %pad_maximum_fusion), channel_id=1, source_target_pairs={{0,2},{2,0},{4,6},{6,4},{8,10},{10,8},{12,14},{14,12},{16,18},{18,... | collective-permute-start | bytes 786440 | tf_op jit(solution)/shard_map/ppermute | solution.py:309
  26.1 2.9 %copy-start.1 = (f32[128,16,256]{2,1,0:T(8,128)S(1)}, f32[128,16,256]{2,1,0:T(8,128)}, u32[]{:S(2)}) copy-start(f32[128,16,256]{2,1,0:T(8,128)} %sketch_ref.2) | copy-start | bytes 6291460
  51.1 7.8 %copy-start.5 = (f32[4,128,256]{2,1,0:T(8,128)S(1)}, f32[4,128,256]{2,1,0:T(8,128)}, u32[]{:S(2)}) copy-start(f32[4,128,256]{2,1,0:T(8,128)} %slice.74) | copy-start | bytes 1572868
  55.7 11.6 %copy-start.3 = (f32[128,16,256]{2,0,1:T(8,128)S(1)}, f32[128,16,256]{2,0,1:T(8,128)}, u32[]{:S(2)}) copy-start(f32[128,16,256]{2,0,1:T(8,128)} %copy-done.2) | copy-start | bytes 6291460
  55.7 1.6 %collective-permute-start.6 = (f32[8,32,256]{2,1,0:T(8,128)S(1)}, f32[8,32,256]{2,1,0:T(8,128)S(1)}, u32[]{:S(2)}, u32[]{:S(2)}) collective-permute-start(f32[8,32,256]{2,1,0:T(8,128)S(1)} %slice.76), channel_id=1, source_target_pairs={{0,2},{2,0},{4,6},{6,4},{8,10},{10,8},{12,14},{14,12},{16,18},{18,... | collective-permute-start | bytes 786440 | tf_op jit(solution)/shard_map/ppermute | solution.py:309
  57.3 5.6 %collective-permute-start.7 = (f32[4,32,256]{2,1,0:T(8,128)S(1)}, f32[4,32,256]{2,1,0:T(8,128)S(1)}, u32[]{:S(2)}, u32[]{:S(2)}) collective-permute-start(f32[4,32,256]{2,1,0:T(8,128)S(1)} %slice.78), channel_id=1, source_target_pairs={{0,4},{2,6},{4,0},{6,2},{8,12},{10,14},{12,8},{14,10},{16,20},{18,... | collective-permute-start | bytes 393224 | tf_op jit(solution)/shard_map/ppermute | solution.py:309
  58.9 13.7 %collective-permute-start.11 = (f32[4,128,256]{2,1,0:T(8,128)S(1)}, f32[4,128,256]{2,1,0:T(8,128)S(1)}, u32[]{:S(2)}, u32[]{:S(2)}) collective-permute-start(f32[4,128,256]{2,1,0:T(8,128)S(1)} %copy-done.5), channel_id=1, source_target_pairs={{0,1},{1,0},{2,3},{3,2},{4,5},{5,4},{6,7},{7,6},{8,9},{9,8},{10,11... | collective-permute-start | bytes 1572872 | tf_op jit(solution)/shard_map/ppermute | solution.py:313
  63.0 4.4 %collective-permute-start.10 = (f32[1,32,256]{2,1,0:T(8,128)S(1)}, f32[1,32,256]{2,1,0:T(8,128)S(1)}, u32[]{:S(2)}, u32[]{:S(2)}) collective-permute-start(f32[1,32,256]{2,1,0:T(8,128)S(1)} %get-tuple-element.33), channel_id=1, source_target_pairs={{0,8},{2,10},{4,12},{6,14},{8,0},{10,2},{12,4},{14,6},{16,24},{18,... | collective-permute-start | bytes 98312 | tf_op jit(solution)/shard_map/ppermute | solution.py:309
  64.7 5.7 %collective-permute-start.8 = (f32[1,32,256]{2,1,0:T(8,128)S(1)}, f32[1,32,256]{2,1,0:T(8,128)S(1)}, u32[]{:S(2)}, u32[]{:S(2)}) collective-permute-start(f32[1,32,256]{2,1,0:T(8,128)S(1)} %get-tuple-element.32), channel_id=1, source_target_pairs={{0,24},{2,26},{4,28},{6,30},{8,16},{10,18},{12,20},{14,22},{16,8},... | collective-permute-start | bytes 98312 | tf_op jit(solution)/shard_map/ppermute | solution.py:309
  67.1 25.1 %copy-start = (f32[128,16,256]{2,1,0:T(8,128)S(1)}, f32[128,16,256]{2,1,0:T(8,128)}, u32[]{:S(2)}) copy-start(f32[128,16,256]{2,1,0:T(8,128)} %sketch_ref.3) | copy-start | bytes 6291460
  67.1 5.2 %collective-permute-start.9 = (f32[1,32,256]{2,1,0:T(8,128)S(1)}, f32[1,32,256]{2,1,0:T(8,128)S(1)}, u32[]{:S(2)}, u32[]{:S(2)}) collective-permute-start(f32[1,32,256]{2,1,0:T(8,128)S(1)} %get-tuple-element.34), channel_id=1, source_target_pairs={{0,16},{2,18},{4,20},{6,22},{8,24},{10,26},{12,28},{14,30},{16,0},... | collective-permute-start | bytes 98312 | tf_op jit(solution)/shard_map/ppermute | solution.py:309
  72.6 4.3 %collective-permute-start.12 = (f32[1,32,256]{2,1,0:T(8,128)S(1)}, f32[1,32,256]{2,1,0:T(8,128)S(1)}, u32[]{:S(2)}, u32[]{:S(2)}) collective-permute-start(f32[1,32,256]{2,1,0:T(8,128)S(1)} %fusion.6), channel_id=1, source_target_pairs={{0,1},{1,0},{2,3},{3,2},{4,5},{5,4},{6,7},{7,6},{8,9},{9,8},{10,11... | collective-permute-start | bytes 98312 | tf_op jit(solution)/shard_map/ppermute | solution.py:313
  73.5 38.3 %collective-permute-start.18 = (f32[12,128,256]{2,1,0:T(8,128)S(1)}, f32[12,128,256]{2,1,0:T(8,128)S(1)}, u32[]{:S(2)}, u32[]{:S(2)}) collective-permute-start(f32[12,128,256]{2,1,0:T(8,128)S(1)} %slice.83), channel_id=1, source_target_pairs={{0,1},{1,0},{2,3},{3,2},{4,5},{5,4},{6,7},{7,6},{8,9},{9,8},{10,11... | collective-permute-start | bytes 4718600 | tf_op jit(solution)/shard_map/ppermute | solution.py:313
  77.0 6.7 %collective-permute-start.13 = (f32[1,2,32,256]{3,2,1,0:T(8,128)S(1)}, f32[1,2,32,256]{3,2,1,0:T(8,128)S(1)}, u32[]{:S(2)}, u32[]{:S(2)}) collective-permute-start(f32[1,2,32,256]{3,2,1,0:T(8,128)S(1)} %maximum_bitcast_fusion), channel_id=1, source_target_pairs={{0,24},{2,26},{4,28},{6,30},{8,16},{10,18},{12,20},{14,22},{16,8},... | collective-permute-start | bytes 196616 | tf_op jit(solution)/shard_map/ppermute | solution.py:309
  80.6 5.2 %collective-permute-start.14 = (f32[1,2,32,256]{3,2,1,0:T(8,128)S(1)}, f32[1,2,32,256]{3,2,1,0:T(8,128)S(1)}, u32[]{:S(2)}, u32[]{:S(2)}) collective-permute-start(f32[1,2,32,256]{3,2,1,0:T(8,128)S(1)} %maximum_bitcast_fusion), channel_id=1, source_target_pairs={{0,16},{2,18},{4,20},{6,22},{8,24},{10,26},{12,28},{14,30},{16,0},... | collective-permute-start | bytes 196616 | tf_op jit(solution)/shard_map/ppermute | solution.py:309
  80.6 5.2 %collective-permute-start.15 = (f32[1,2,32,256]{3,2,1,0:T(8,128)S(1)}, f32[1,2,32,256]{3,2,1,0:T(8,128)S(1)}, u32[]{:S(2)}, u32[]{:S(2)}) collective-permute-start(f32[1,2,32,256]{3,2,1,0:T(8,128)S(1)} %maximum_bitcast_fusion), channel_id=1, source_target_pairs={{0,8},{2,10},{4,12},{6,14},{8,0},{10,2},{12,4},{14,6},{16,24},{18,... | collective-permute-start | bytes 196616 | tf_op jit(solution)/shard_map/ppermute | solution.py:309
  85.8 6.4 %collective-permute-start.16 = (f32[4,2,32,256]{3,2,1,0:T(8,128)S(1)}, f32[4,2,32,256]{3,2,1,0:T(8,128)S(1)}, u32[]{:S(2)}, u32[]{:S(2)}) collective-permute-start(f32[4,2,32,256]{3,2,1,0:T(8,128)S(1)} %pad_maximum_fusion.1), channel_id=1, source_target_pairs={{0,4},{2,6},{4,0},{6,2},{8,12},{10,14},{12,8},{14,10},{16,20},{18,... | collective-permute-start | bytes 786440 | tf_op jit(solution)/shard_map/ppermute | solution.py:309
  92.2 2.0 %collective-permute-start.17 = (f32[8,2,32,256]{3,2,1,0:T(8,128)S(1)}, f32[8,2,32,256]{3,2,1,0:T(8,128)S(1)}, u32[]{:S(2)}, u32[]{:S(2)}) collective-permute-start(f32[8,2,32,256]{3,2,1,0:T(8,128)S(1)} %constant_dynamic-update-slice_fusion.5.refs_0_), channel_id=1, source_target_pairs={{0,2},{2,0},{4,6},{6,4},{8,10},{10,8},{12,14},{14,12},{16,18},{18,... | collective-permute-start | bytes 1572872 | tf_op jit(solution)/shard_map/ppermute | solution.py:309
  116.3 1.6 %collective-permute-start.19 = (f32[8,32,256]{2,1,0:T(8,128)S(1)}, f32[8,32,256]{2,1,0:T(8,128)S(1)}, u32[]{:S(2)}, u32[]{:S(2)}) collective-permute-start(f32[8,32,256]{2,1,0:T(8,128)S(1)} %slice.85), channel_id=1, source_target_pairs={{0,2},{2,0},{4,6},{6,4},{8,10},{10,8},{12,14},{14,12},{16,18},{18,... | collective-permute-start | bytes 786440 | tf_op jit(solution)/shard_map/ppermute | solution.py:309
  117.9 5.6 %collective-permute-start.20 = (f32[4,32,256]{2,1,0:T(8,128)S(1)}, f32[4,32,256]{2,1,0:T(8,128)S(1)}, u32[]{:S(2)}, u32[]{:S(2)}) collective-permute-start(f32[4,32,256]{2,1,0:T(8,128)S(1)} %slice.87), channel_id=1, source_target_pairs={{0,4},{2,6},{4,0},{6,2},{8,12},{10,14},{12,8},{14,10},{16,20},{18,... | collective-permute-start | bytes 393224 | tf_op jit(solution)/shard_map/ppermute | solution.py:309
  123.6 6.1 %collective-permute-start.21 = (f32[1,32,256]{2,1,0:T(8,128)S(1)}, f32[1,32,256]{2,1,0:T(8,128)S(1)}, u32[]{:S(2)}, u32[]{:S(2)}) collective-permute-start(f32[1,32,256]{2,1,0:T(8,128)S(1)} %get-tuple-element.29), channel_id=1, source_target_pairs={{0,24},{2,26},{4,28},{6,30},{8,16},{10,18},{12,20},{14,22},{16,8},... | collective-permute-start | bytes 98312 | tf_op jit(solution)/shard_map/ppermute | solution.py:309
  125.3 4.9 %collective-permute-start.22 = (f32[1,32,256]{2,1,0:T(8,128)S(1)}, f32[1,32,256]{2,1,0:T(8,128)S(1)}, u32[]{:S(2)}, u32[]{:S(2)}) collective-permute-start(f32[1,32,256]{2,1,0:T(8,128)S(1)} %get-tuple-element.31), channel_id=1, source_target_pairs={{0,16},{2,18},{4,20},{6,22},{8,24},{10,26},{12,28},{14,30},{16,0},... | collective-permute-start | bytes 98312 | tf_op jit(solution)/shard_map/ppermute | solution.py:309
  125.8 4.6 %collective-permute-start.23 = (f32[1,32,256]{2,1,0:T(8,128)S(1)}, f32[1,32,256]{2,1,0:T(8,128)S(1)}, u32[]{:S(2)}, u32[]{:S(2)}) collective-permute-start(f32[1,32,256]{2,1,0:T(8,128)S(1)} %get-tuple-element.30), channel_id=1, source_target_pairs={{0,8},{2,10},{4,12},{6,14},{8,0},{10,2},{12,4},{14,6},{16,24},{18,... | collective-permute-start | bytes 98312 | tf_op jit(solution)/shard_map/ppermute | solution.py:309
  130.4 5.8 %collective-permute-start.24 = (f32[1,32,256]{2,1,0:T(8,128)S(1)}, f32[1,32,256]{2,1,0:T(8,128)S(1)}, u32[]{:S(2)}, u32[]{:S(2)}) collective-permute-start(f32[1,32,256]{2,1,0:T(8,128)S(1)} %get-tuple-element.28), channel_id=1, source_target_pairs={{0,24},{2,26},{4,28},{6,30},{8,16},{10,18},{12,20},{14,22},{16,8},... | collective-permute-start | bytes 98312 | tf_op jit(solution)/shard_map/ppermute | solution.py:309
  132.7 4.9 %collective-permute-start.25 = (f32[1,32,256]{2,1,0:T(8,128)S(1)}, f32[1,32,256]{2,1,0:T(8,128)S(1)}, u32[]{:S(2)}, u32[]{:S(2)}) collective-permute-start(f32[1,32,256]{2,1,0:T(8,128)S(1)} %get-tuple-element.28), channel_id=1, source_target_pairs={{0,16},{2,18},{4,20},{6,22},{8,24},{10,26},{12,28},{14,30},{16,0},... | collective-permute-start | bytes 98312 | tf_op jit(solution)/shard_map/ppermute | solution.py:309
  133.5 4.3 %collective-permute-start.26 = (f32[1,32,256]{2,1,0:T(8,128)S(1)}, f32[1,32,256]{2,1,0:T(8,128)S(1)}, u32[]{:S(2)}, u32[]{:S(2)}) collective-permute-start(f32[1,32,256]{2,1,0:T(8,128)S(1)} %get-tuple-element.28), channel_id=1, source_target_pairs={{0,8},{2,10},{4,12},{6,14},{8,0},{10,2},{12,4},{14,6},{16,24},{18,... | collective-permute-start | bytes 98312 | tf_op jit(solution)/shard_map/ppermute | solution.py:309
  137.8 5.0 %collective-permute-start.27 = (f32[4,32,256]{2,1,0:T(8,128)S(1)}, f32[4,32,256]{2,1,0:T(8,128)S(1)}, u32[]{:S(2)}, u32[]{:S(2)}) collective-permute-start(f32[4,32,256]{2,1,0:T(8,128)S(1)} %pad_maximum_fusion.3), channel_id=1, source_target_pairs={{0,4},{2,6},{4,0},{6,2},{8,12},{10,14},{12,8},{14,10},{16,20},{18,... | collective-permute-start | bytes 393224 | tf_op jit(solution)/shard_map/ppermute | solution.py:309
  142.9 1.6 %collective-permute-start.28 = (f32[8,32,256]{2,1,0:T(8,128)S(1)}, f32[8,32,256]{2,1,0:T(8,128)S(1)}, u32[]{:S(2)}, u32[]{:S(2)}) collective-permute-start(f32[8,32,256]{2,1,0:T(8,128)S(1)} %constant_dynamic-update-slice_fusion.10.refs_0_), channel_id=1, source_target_pairs={{0,2},{2,0},{4,6},{6,4},{8,10},{10,8},{12,14},{14,12},{16,18},{18,... | collective-permute-start | bytes 786440 | tf_op jit(solution)/shard_map/ppermute | solution.py:309
